TPU v7x, 128 devices: a whole 4x4x4 slice. The times are simulated.
128 devices in a mesh: gx: 16 (over y, x), yz: 8 (over z, core).
Axes of the slice: x: 4, y: 4, z: 4, core: 2. Of those that a mesh axis runs over, the one named last changes fastest.
Arguments:
- fields: bfloat16 [4, 512, 262144], P(None, 'gx', 'yz'), may hold values from -8 to 8
- test_matrix: float32 [512, 64], replicated, may hold values from -6 to 6
Outputs:
- factor: float32 [512, 64], replicated
- core: bfloat16 [64, 4, 262144], P('gx', None, 'yz')
All inputs are finite; a program needn't handle non-finite values.
Results may differ from a plain program's by a relative error of at most 0.0036.
Values may be sent and summed in bfloat16 or wider, within the bound.
No kernel may reach another device: no remote copies, remote signals or barrier semaphores. Data moves between devices by JAX's collectives and lax.ppermute only.
A program may use at most 192 MiB of HBM per device.

v0:
```python
import jax
import jax.numpy as jnp
from jax import lax
from jax.sharding import PartitionSpec as P


def orthonormal(matrix_y):
    moment = jnp.dot(matrix_y.T, matrix_y, precision=lax.Precision.HIGHEST)
    lower = jnp.linalg.cholesky(moment)
    return lax.linalg.triangular_solve(
        lower, matrix_y, left_side=False, lower=True, transpose_a=True
    )


def body(fields, test_matrix):
    species_count, slab_len, cell_count = fields.shape
    norm_scale = 1.0 / (species_count * cell_count * lax.axis_size("yz"))
    pieces = lax.all_to_all(fields, "gx", split_axis=2, concat_axis=1, tiled=True)
    gram_parts = jnp.einsum("sxc,syc->sxy", pieces, pieces, preferred_element_type=jnp.float32)
    gram_parts, fibres = (gram_parts, pieces)
    local_gram = jnp.sum(gram_parts, axis=0)
    summed_gram = lax.psum(local_gram, ("gx", "yz"))
    sketch = jnp.dot(summed_gram, test_matrix, precision=lax.Precision.HIGHEST) * norm_scale
    factor = orthonormal(orthonormal(sketch))
    factor_low = factor.astype(jnp.bfloat16)
    core_block = jnp.einsum(
        "xr,sxc->rsc", factor_low, fibres, preferred_element_type=jnp.float32
    ).astype(jnp.bfloat16)
    core_block = lax.all_to_all(core_block, "gx", split_axis=0, concat_axis=2, tiled=True)
    return (factor, core_block)


def solution(mesh):
    in_specs = (P(None, "gx", "yz"), P())
    out_specs = (P(), P("gx", None, "yz"))
    return jax.shard_map(body, mesh=mesh, in_specs=in_specs, out_specs=out_specs, check_vma=False)
```

profile of v0, /device:TPU:0, one launch (start us, length us, event | category | flops | bytes accessed | tf_op | source)
XLA Modules:
  0.0 475.0 jit_solution(1052672916725822940)
XLA Ops:
  7.2 0.0 copy-start
  7.2 0.0 all-reduce.2.cloned.1.call-start
  7.2 39.0 %copy.8 = bf16[4,32,32768]{1,0,2:T(4,128)(2,1)} copy(bf16[4,32,32768]{2,1,0:T(8,128)(2,1)} %param.5) | data formatting | bytes 16777216 | tf_op args[0]
  46.2 35.0 %reshape.23 = bf16[16,2,131072]{2,1,0:T(2,128)(2,1)} reshape(bf16[32768,4,32]{2,1,0:T(4,128)(2,1)} %bitcast.50) | data formatting | bytes 16777216
  81.3 103.0 %all_to_all.36 = bf16[16,2,131072]{2,1,0:T(2,128)(2,1)} all-to-all(bf16[16,2,131072]{2,1,0:T(2,128)(2,1)} %reshape.23), channel_id=1, replica_groups=mesh['gx'=16,'yz'=8] {'gx'}, dimensions={0} | all-to-all | bytes 16777216 | tf_op jit(solution)/shard_map/all_to_all | solution.py:18
  184.3 22.9 %reshape.24 = bf16[32768,4,32]{2,1,0:T(4,128)(2,1)} reshape(bf16[16,2,131072]{2,1,0:T(2,128)(2,1)} %all_to_all.36) | data formatting | bytes 16777216
  207.2 45.2 %copy.9 = bf16[4,32,16,2048]{3,1,2,0:T(8,128)(2,1)} copy(bf16[4,32,16,2048]{1,0,3,2:T(4,128)(2,1)} %bitcast.49) | data formatting | bytes 16777216 | tf_op jit(solution)/shard_map/all_to_all | solution.py:18
  252.4 11.3 %convolution_bitcast_fusion = f32[512,512]{1,0:T(8,128)} fusion(bf16[4,512,2048]{2,1,0:T(8,128)(2,1)} %bitcast.51), kind=kOutput, calls=%fused_computation.1 | convolution fusion | flops 4294967296 | bytes 9437184 | tf_op jit(solution)/shard_map/sxc,syc->sxy/dot_general | solution.py:19
  263.7 0.0 all-reduce.2.cloned.1.call-update
  263.7 146.2 %all-reduce.2.cloned.1.call-done = f32[512,512]{1,0:T(8,128)} async-done(((f32[512,512]{1,0:T(8,128)}), f32[512,512]{1,0:T(8,128)}) %all-reduce.2.cloned.1.call-update) | async-done | bytes 1048592 | tf_op jit(solution)/shard_map/psum | solution.py:22
  409.9 0.0 copy-done
  409.9 2.4 convolution_multiply_fusion
  412.3 0.3 fusion.10
  412.5 0.1 copy.10
  412.6 5.8 %cholesky.44 = f32[64,64]{1,0:T(8,128)S(1)} custom-call(f32[64,64]{1,0:T(8,128)S(1)} %fusion.7), custom_call_target="Cholesky" | custom-call | tf_op jit(solution)/shard_map/jit(cholesky)/cholesky | solution.py:9
  418.5 0.6 compare_reduce_fusion.1
  419.1 0.7 fusion.2
  419.8 4.9 %custom-call.6 = f32[1,64,64]{1,2,0:T(8,128)S(1)} custom-call(f32[1,64,64]{2,1,0:T(8,128)S(1)} %fusion.2), custom_call_target="InvertDiagBlocksLowerTriangular" | custom-call | tf_op jit(solution)/shard_map/triangular_solve/custom-call.0 | solution.py:10
  424.7 0.3 convolution_bitcast_fusion.2
  425.0 0.3 fusion.11
  425.3 0.1 copy.11
  425.4 5.8 %cholesky.55 = f32[64,64]{1,0:T(8,128)S(1)} custom-call(f32[64,64]{1,0:T(8,128)S(1)} %fusion.5), custom_call_target="Cholesky" | custom-call | tf_op jit(solution)/shard_map/jit(cholesky)/cholesky | solution.py:9
  431.3 0.6 compare_reduce_fusion
  431.9 0.7 fusion.3
  432.6 4.9 %custom-call.7 = f32[1,64,64]{1,2,0:T(8,128)S(1)} custom-call(f32[1,64,64]{2,1,0:T(8,128)S(1)} %fusion.3), custom_call_target="InvertDiagBlocksLowerTriangular" | custom-call | tf_op jit(solution)/shard_map/triangular_solve/custom-call.0 | solution.py:10
  437.5 0.3 convolution_bitcast_fusion.1
  437.8 0.0 copy-start.1
  437.8 5.0 %convolution_convert_fusion = bf16[64,4,2048]{2,0,1:T(8,128)(2,1)S(1)} fusion(bf16[4,512,2048]{2,1,0:T(8,128)(2,1)} %bitcast.52, f32[512,64]{0,1:T(8,128)S(1)} %convolution_bitcast_fusion.1), kind=kOutput, calls=%fused_computation | convolution fusion | flops 537427968 | bytes 9568256 | tf_op jit(solution)/shard_map/xr,sxc->rsc/dot_general | solution.py:26
  442.9 0.8 copy.12
  443.7 23.0 %all_to_all.37 = bf16[64,4,2048]{2,1,0:T(4,128)(2,1)S(1)} all-to-all(bf16[64,4,2048]{2,1,0:T(4,128)(2,1)S(1)} %copy.12), channel_id=1, replica_groups=mesh['gx'=16,'yz'=8] {'gx'}, dimensions={0} | all-to-all | bytes 2097152 | tf_op jit(solution)/shard_map/all_to_all | solution.py:29
  466.7 1.4 copy.14
  468.1 0.0 copy-done.1
  (4 shorter events, 0.1 us)
Async XLA Ops:
  7.2 402.7 %copy-start = (f32[512,64]{0,1:T(8,128)S(1)}, f32[512,64]{0,1:T(8,128)}, u32[]{:S(2)}) copy-start(f32[512,64]{0,1:T(8,128)} %param.6) | copy-start | bytes 393220
  7.2 402.7 %all-reduce.2.cloned.1.call-start = ((), (), s32[]{:S(2)}) async-start(), calls=%async_computation.2 | async-start | bytes 2097152 | tf_op jit(solution)/shard_map/psum | solution.py:22
  437.8 30.3 %copy-start.1 = (f32[512,64]{0,1:T(8,128)}, f32[512,64]{0,1:T(8,128)S(1)}, u32[]{:S(2)}) copy-start(f32[512,64]{0,1:T(8,128)S(1)} %convolution_bitcast_fusion.1) | copy-start | bytes 393220
Sparse Core Ops, SparseCore 0:
  263.8 145.9 all-reduce.1
where the time goes:
time: 478 us; the launch traced here: 475 us
  waiting for transfers between devices  146 us (31%)
  local copies, waits for them, and re-layouts  145 us (30%)
  blocking collectives  126 us (26%)
  other arithmetic  24.2 us (5%)
  matrix products  19.8 us (4%)
  between operations  14.1 us (3%)
    psum x1, waiting for transfers between devices, body(): summed_gram = lax.psum(local_gram, ('gx', 'yz'))  146 us
    all_to_all x1, blocking collectives, body(): lax.all_to_all(fields, 'gx', split_axis=2, concat_axis=1, tiled=True)  103 us
    unnamed x7, local copies, waits for them, and re-layouts  97 us
    all_to_all x1, local copies, waits for them, and re-layouts, body(): lax.all_to_all(fields, 'gx', split_axis=2, concat_axis=1, tiled=True)  45.2 us
    all_to_all x1, blocking collectives, body(): lax.all_to_all(core_block, 'gx', split_axis=0, concat_axis=2, tiled=True)  23 us
    another operation x6, other arithmetic, orthonormal(): lower = jnp.linalg.cholesky(moment)  13 us
    dot_general x1, matrix products, body(): jnp.einsum('sxc,syc->sxy', pieces, pieces, preferred_element_type=jnp.flo...  11.3 us
    another operation x4, other arithmetic, orthonormal(): lax.linalg.triangular_solve(lower, matrix_y, left_side=False, lower=True,...  11.1 us
  transfers between devices with their start and end apart: 1, of which 1 were waited for; matrix products, arithmetic and copies ran while one was open for 0% of the time, Pallas kernels for 0%

commit v1 on v0

v1 whole, which is shorter than its diff:
```python
import jax
import jax.numpy as jnp
from jax import lax
from jax.sharding import PartitionSpec as P
from jax.experimental import pallas as pl
from jax.experimental.pallas import tpu as pltpu

HIGH = lax.Precision.HIGHEST
F32 = jnp.float32
BF16 = jnp.bfloat16
VM = pl.BlockSpec(memory_space=pltpu.VMEM)
ANY = pl.BlockSpec(memory_space=pl.ANY)


def nt(a, b, precision=None):
    return lax.dot_general(a, b, (((1,), (1,)), ((), ())), precision=precision,
                           preferred_element_type=F32)


def split_kernel(x_ref, o_ref, buf, sem_in, sem_out):
    parts, _, _, w = o_ref.shape

    def load(j):
        return pltpu.make_async_copy(x_ref.at[:, :, pl.ds(j * w, w)], buf.at[j], sem_in.at[j])

    def store(j):
        return pltpu.make_async_copy(buf.at[j], o_ref.at[j], sem_out.at[j])

    for j in range(parts):
        load(j).start()
    for j in range(parts):
        load(j).wait()
        store(j).start()
    for j in range(parts):
        store(j).wait()


def split_cells(fields, parts):
    s, m, n = fields.shape
    shape = (parts, s, m, n // parts)
    return pl.pallas_call(
        split_kernel,
        in_specs=[ANY],
        out_specs=ANY,
        out_shape=jax.ShapeDtypeStruct(shape, fields.dtype),
        scratch_shapes=[pltpu.VMEM(shape, fields.dtype),
                        pltpu.SemaphoreType.DMA((parts,)), pltpu.SemaphoreType.DMA((parts,))],
        compiler_params=pltpu.CompilerParams(vmem_limit_bytes=12 << 20),
        name="split",
    )(fields)


def sketch_kernel(scale, x_ref, t_ref, o_ref, acc):
    k = pl.program_id(0)
    x = x_ref[...].reshape(-1, x_ref.shape[-1])
    g = nt(x, x)

    @pl.when(k == 0)
    def _():
        acc[...] = g

    @pl.when(k > 0)
    def _():
        acc[...] += g

    @pl.when(k == pl.num_programs(0) - 1)
    def _():
        sk = lax.dot_general(t_ref[...], acc[...], (((0,), (0,)), ((), ())), precision=HIGH,
                             preferred_element_type=F32) * scale
        for c in range(4):
            o_ref[c * 64:(c + 1) * 64, :] = sk[:, c * 128:(c + 1) * 128]


def local_sketch(pieces, test_matrix, scale):
    parts, s, m, w = pieces.shape
    return pl.pallas_call(
        lambda *r: sketch_kernel(scale, *r),
        grid=(s,),
        in_specs=[pl.BlockSpec((parts, 1, m, w), lambda k: (0, k, 0, 0)),
                  pl.BlockSpec((512, 64), lambda k: (0, 0))],
        out_specs=pl.BlockSpec((256, 128), lambda k: (0, 0)),
        out_shape=jax.ShapeDtypeStruct((256, 128), F32),
        scratch_shapes=[pltpu.VMEM((512, 512), F32)],
        compiler_params=pltpu.CompilerParams(vmem_limit_bytes=16 << 20),
        name="sketch",
    )(pieces, test_matrix)


def inverse_lower(aug, step):
    blocks = [aug[8 * b:8 * b + 8, :] for b in range(8)]
    sub = lax.broadcasted_iota(jnp.int32, (8, 128), 0)
    for k in range(0, 64, step):
        b0 = k // 8
        cols = [[jnp.broadcast_to(blocks[b][:, 64 + k + j:65 + k + j], (8, 128)) for b in range(b0, 8)]
                for j in range(step)]
        rows = [blocks[b0][k % 8 + j:k % 8 + j + 1, :] for j in range(step)]
        mult = []
        for j in range(step):
            r = k % 8 + j
            inv = 1.0 / cols[j][0][r:r + 1, :]
            l = [c * inv for c in cols[j]]
            l[0] = jnp.where(sub > r, l[0], 0.0)
            for j2 in range(j + 1, step):
                e = cols[j2][0][r:r + 1, :]
                cols[j2] = [c - x * e for c, x in zip(cols[j2], l)]
                rows[j2] = rows[j2] - l[0][r + j2 - j:r + j2 - j + 1, :] * rows[j]
            mult.append(l)
        for b in range(b0, 8):
            t = blocks[b]
            for j in range(step):
                t = t - mult[j][b - b0] * rows[j]
            blocks[b] = t
    lane = lax.broadcasted_iota(jnp.int32, (8, 128), 1)
    out = []
    for b in range(8):
        diag = jnp.sum(jnp.where(lane == sub + 64 + 8 * b, blocks[b], 0.0), axis=1, keepdims=True)
        out.append(blocks[b] * lax.rsqrt(diag))
    return jnp.concatenate(out, axis=0)[:, :64]


def orthonormal_t(yt, step):
    zero = jnp.zeros_like(yt)
    aug = nt(yt, jnp.concatenate([zero, yt], axis=0), HIGH)
    i = lax.broadcasted_iota(jnp.int32, aug.shape, 0)
    j = lax.broadcasted_iota(jnp.int32, aug.shape, 1)
    aug = jnp.where(i == j, 1.0, aug)
    return jnp.dot(inverse_lower(aug, step), yt, precision=HIGH, preferred_element_type=F32)


def core_kernel(y_ref, x_ref, f_ref, o_ref, buf, sem):
    s = x_ref.shape[1]
    w = x_ref.shape[-1]
    loads = [pltpu.make_async_copy(x_ref.at[:, k], buf.at[k], sem.at[k]) for k in range(s)]
    for c in loads:
        c.start()
    yt = jnp.concatenate([y_ref[c * 64:(c + 1) * 64, :] for c in range(4)], axis=1)
    ft = orthonormal_t(orthonormal_t(yt, 4), 4)
    f_ref[...] = ft
    low = ft.astype(BF16)
    i = lax.broadcasted_iota(jnp.int32, (64 * s, 64), 0)
    j = lax.broadcasted_iota(jnp.int32, (64 * s, 64), 1)
    wide = [jnp.dot((i == j * s + k).astype(BF16), low, preferred_element_type=F32).astype(BF16)
            for k in range(s)]
    for c in loads:
        c.wait()
    step = 512
    for c in range(w // step):
        acc = None
        for k in range(s):
            x = buf[k, :, :, c * step:(c + 1) * step].reshape(512, step)
            t = jnp.dot(wide[k], x, preferred_element_type=F32)
            acc = t if acc is None else acc + t
        o_ref[:, :, c * step:(c + 1) * step] = acc.astype(BF16).reshape(16, 4 * s, step)


def core_blocks(full, pieces):
    parts, s, m, w = pieces.shape
    return pl.pallas_call(
        core_kernel,
        in_specs=[VM, ANY],
        out_specs=[VM, VM],
        out_shape=[jax.ShapeDtypeStruct((64, 512), F32),
                   jax.ShapeDtypeStruct((parts, 4 * s, w), BF16)],
        scratch_shapes=[pltpu.VMEM((s, parts, m, w), BF16), pltpu.SemaphoreType.DMA((s,))],
        compiler_params=pltpu.CompilerParams(vmem_limit_bytes=24 << 20),
        name="core",
    )(full, pieces)


def merge_kernel(x_ref, o_ref):
    o_ref[...] = x_ref[0].reshape(o_ref.shape)


def merge_cells(core, s):
    parts, q, w = core.shape
    return pl.pallas_call(
        merge_kernel,
        grid=(parts,),
        in_specs=[pl.BlockSpec((1, q, w), lambda j: (j, 0, 0))],
        out_specs=pl.BlockSpec((q // s, s, w), lambda j: (0, 0, j)),
        out_shape=jax.ShapeDtypeStruct((q // s, s, parts * w), BF16),
        name="merge",
    )(core)


def body(fields, test_matrix):
    s, m, n = fields.shape
    parts = lax.axis_size("gx")
    w = n // parts
    axes = ("gx", "yz")
    scale = 1.0 / (s * n * lax.axis_size("yz"))
    f = split_cells(fields, parts).reshape(parts, s * m, w)
    pieces = lax.all_to_all(f, "gx", split_axis=0, concat_axis=0, tiled=True)
    pieces = pieces.reshape(parts, s, m, w)
    part = local_sketch(pieces, test_matrix, scale)
    part = lax.all_to_all(part.reshape(128, 2, 128), axes, split_axis=0, concat_axis=0, tiled=True)
    part = jnp.sum(part, axis=0, keepdims=True)
    full = lax.all_to_all(jnp.broadcast_to(part, (128, 2, 128)), axes, split_axis=0, concat_axis=0, tiled=True)
    ft, core = core_blocks(full.reshape(256, 128), pieces)
    core = lax.all_to_all(core, "gx", split_axis=0, concat_axis=0, tiled=True)
    return (ft.T, merge_cells(core, s))


def solution(mesh):
    in_specs = (P(None, "gx", "yz"), P())
    out_specs = (P(), P("gx", None, "yz"))
    return jax.shard_map(body, mesh=mesh, in_specs=in_specs, out_specs=out_specs, check_vma=False)
```

time: 478 us -> 224 us (0.47)
  local copies, waits for them, and re-layouts: 145 us -> 6.75 us
  blocking collectives: 126 us -> 53.9 us
  Pallas kernels: 0 us -> 30.3 us
  other arithmetic: 24.2 us -> 0.14 us
  waiting for transfers between devices: 146 us -> 124 us
  matrix products: 19.8 us -> 0 us
  between operations: 14.1 us -> 0.7 us
  starting transfers between devices: 0.04 us -> 7.33 us
    psum x1 -> x0, waiting for transfers between devices: 146 us -> none  [body(): summed_gram = lax.psum(local_gram, ('gx', 'yz'))]
    all_to_all x0 -> x1, waiting for transfers between devices: none -> 124 us  [body(): pieces = lax.all_to_all(f, 'gx', split_axis=0, concat_axis=0, tiled=True)]
    unnamed x7, local copies, waits for them, and re-layouts: 97 us -> 6.72 us
    all_to_all x2 -> x3, blocking collectives: 126 us -> 53.9 us  [the longest x1 20.4 us: body(): core = lax.all_to_all(core, 'gx', split_axis=0, concat_axis=0, tiled=True)]
    all_to_all x2 -> x0, local copies, waits for them, and re-layouts: 46.7 us -> none  [the longest x1 45.2 us: body(): lax.all_to_all(fields, 'gx', split_axis=2, concat_axis=1, tiled=True)]
    pallas_call x0 -> x4, Pallas kernels: none -> 30.3 us  [the longest x1 11.9 us: core_blocks(): pl.pallas_call(core_kernel, in_specs=[VM, ANY], out_specs=[VM, VM], out_s...]
    another operation x10 -> x0, other arithmetic: 24.1 us -> none  [the longest x6 13 us: orthonormal(): lower = jnp.linalg.cholesky(moment)]
    dot_general x5 -> x0, matrix products: 19.1 us -> none  [the longest x1 11.3 us: body(): jnp.einsum('sxc,syc->sxy', pieces, pieces, preferred_element_type=jnp.flo...]
where the time goes in v1:
time: 224 us; the launch traced here: 223 us
  waiting for transfers between devices  124 us (55%)
  blocking collectives  53.9 us (24%)
  Pallas kernels  30.3 us (14%)
  starting transfers between devices  7.33 us (3%)
  local copies, waits for them, and re-layouts  6.75 us (3%)
    all_to_all x1, waiting for transfers between devices, body(): pieces = lax.all_to_all(f, 'gx', split_axis=0, concat_axis=0, tiled=True)  124 us
    all_to_all x1, blocking collectives, body(): core = lax.all_to_all(core, 'gx', split_axis=0, concat_axis=0, tiled=True)  20.4 us
    all_to_all x1, blocking collectives, body(): lax.all_to_all(part.reshape(128, 2, 128), axes, split_axis=0, concat_axis...  19.3 us
    all_to_all x1, blocking collectives, body(): lax.all_to_all(jnp.broadcast_to(part, (128, 2, 128)), axes, split_axis=0,...  14.2 us
    pallas_call x1, Pallas kernels, core_blocks(): pl.pallas_call(core_kernel, in_specs=[VM, ANY], out_specs=[VM, VM], out_s...  11.9 us
    pallas_call x1, Pallas kernels, merge_cells(): pl.pallas_call(merge_kernel, grid=(parts,), in_specs=[pl.BlockSpec((1, q,...  8.88 us
    pallas_call x1, Pallas kernels, local_sketch(): pl.pallas_call(lambda *r: sketch_kernel(scale, *r), grid=(s,), in_specs=[...  8.1 us
    all_to_all x1, starting transfers between devices, body(): pieces = lax.all_to_all(f, 'gx', split_axis=0, concat_axis=0, tiled=True)  7.33 us
  transfers between devices with their start and end apart: 1, of which 1 were waited for; matrix products, arithmetic and copies ran while one was open for 0% of the time, Pallas kernels for 0%

profile of v1, /device:TPU:0, one launch (start us, length us, event | category | flops | bytes accessed | tf_op | source)
XLA Modules:
  0.0 223.1 jit_solution(1896190571547824025)
XLA Ops:
  0.6 0.0 copy-start.1
  0.6 3.4 %copy-done.1 = bf16[4,32,32768]{2,1,0:T(8,128)(2,1)S(1)} copy-done((bf16[4,32,32768]{2,1,0:T(8,128)(2,1)S(1)}, bf16[4,32,32768]{2,1,0:T(8,128)(2,1)}, u32[]{:S(2)}) %copy-start.1) | copy-done | bytes 8388632
  4.0 1.5 split.1
  5.5 0.0 copy-start
  5.5 3.2 %copy-done = bf16[16,4,32,2048]{3,2,1,0:T(8,128)(2,1)} copy-done((bf16[16,4,32,2048]{3,2,1,0:T(8,128)(2,1)}, bf16[16,4,32,2048]{3,2,1,0:T(8,128)(2,1)S(1)}, u32[]{:S(2)}) %copy-start) | copy-done | bytes 8388632
  8.7 0.0 copy-start.2
  8.7 7.3 %all-to-all-start = ((bf16[16,128,2048]{2,1,0:T(8,128)(2,1)}), bf16[16,128,2048]{2,1,0:T(8,128)(2,1)}, u32[]{:S(2)}, u32[]{:S(2)}) async-start(bf16[16,128,2048]{2,1,0:T(8,128)(2,1)} %bitcast.5), calls=%async_computation | async-start | bytes 16777216 | tf_op jit(solution)/shard_map/all_to_all | solution.py:193
  16.1 0.0 copy-done.2
  16.1 0.1 copy.4.r_1_
  16.2 124.0 %all-to-all-done = bf16[16,128,2048]{2,1,0:T(8,128)(2,1)} async-done(((bf16[16,128,2048]{2,1,0:T(8,128)(2,1)}), bf16[16,128,2048]{2,1,0:T(8,128)(2,1)}, u32[]{:S(2)}, u32[]{:S(2)}) %all-to-all-start) | async-done | bytes 8388640 | tf_op jit(solution)/shard_map/all_to_all | solution.py:193
  140.2 8.1 %sketch.1 = f32[256,128]{1,0:T(8,128)S(1)} custom-call(bf16[16,4,32,2048]{3,2,1,0:T(8,128)(2,1)} %bitcast.1.r_0_.x_ref, f32[512,64]{1,0:T(8,128)S(1)} %copy.4.r_1_), custom_call_target="tpu_custom_call" | custom-call | tf_op jit(solution)/shard_map/sketch/pallas_call | solution.py:76
  148.3 19.3 %all_to_all.20 = f32[128,2,128]{2,1,0:T(2,128)S(1)} all-to-all(f32[128,2,128]{2,1,0:T(2,128)S(1)} %bitcast.7), channel_id=1, replica_groups=mesh['gx'=16,'yz'=8] {'gx','yz'}, dimensions={0} | all-to-all | bytes 262144 | tf_op jit(solution)/shard_map/all_to_all | solution.py:196
  167.6 0.1 reduce_sum.9
  167.8 14.2 %all_to_all.21 = f32[128,2,128]{2,1,0:T(2,128)S(1)} all-to-all(f32[128,2,128]{2,1,0:T(2,128)S(1)} %broadcast_in_dim.2), channel_id=1, replica_groups=mesh['gx'=16,'yz'=8] {'gx','yz'}, dimensions={0} | all-to-all | bytes 262144 | tf_op jit(solution)/shard_map/all_to_all | solution.py:198
  182.0 11.9 %core.1 = (f32[64,512]{1,0:T(8,128)}, bf16[16,16,2048]{2,1,0:T(8,128)(2,1)S(1)}) custom-call(f32[256,128]{1,0:T(8,128)S(1)} %bitcast.6, bf16[16,4,32,2048]{3,2,1,0:T(8,128)(2,1)} %bitcast.1.r_0_.x_ref), custom_call_target="tpu_custom_call" | custom-call | tf_op jit(solution)/shard_map/core/pallas_call | solution.py:158
  193.9 20.4 %all_to_all.22.x_ref = bf16[16,16,2048]{2,1,0:T(8,128)(2,1)} all-to-all(bf16[16,16,2048]{2,1,0:T(8,128)(2,1)S(1)} %get-tuple-element.5), channel_id=1, replica_groups=mesh['gx'=16,'yz'=8] {'gx'}, dimensions={0} | all-to-all | bytes 2097152 | tf_op jit(solution)/shard_map/all_to_all | solution.py:200
  214.3 8.9 %merge.1 = bf16[4,4,32768]{2,1,0:T(4,128)(2,1)} custom-call(bf16[16,16,2048]{2,1,0:T(8,128)(2,1)} %all_to_all.22.x_ref), custom_call_target="tpu_custom_call" | custom-call | tf_op jit(solution)/shard_map/merge/pallas_call | solution.py:176
  (1 shorter events, 0.0 us)
Async XLA Ops:
  0.6 3.4 %copy-start.1 = (bf16[4,32,32768]{2,1,0:T(8,128)(2,1)S(1)}, bf16[4,32,32768]{2,1,0:T(8,128)(2,1)}, u32[]{:S(2)}) copy-start(bf16[4,32,32768]{2,1,0:T(8,128)(2,1)} %x_ref.1) | copy-start | bytes 25165828
  5.5 3.2 %copy-start = (bf16[16,4,32,2048]{3,2,1,0:T(8,128)(2,1)}, bf16[16,4,32,2048]{3,2,1,0:T(8,128)(2,1)S(1)}, u32[]{:S(2)}) copy-start(bf16[16,4,32,2048]{3,2,1,0:T(8,128)(2,1)S(1)} %split.1) | copy-start | bytes 25165828
  8.7 7.3 %copy-start.2 = (f32[512,64]{0,1:T(8,128)S(1)}, f32[512,64]{0,1:T(8,128)}, u32[]{:S(2)}) copy-start(f32[512,64]{0,1:T(8,128)} %param.3) | copy-start | bytes 393220
  8.7 131.5 %all-to-all-start = ((bf16[16,128,2048]{2,1,0:T(8,128)(2,1)}), bf16[16,128,2048]{2,1,0:T(8,128)(2,1)}, u32[]{:S(2)}, u32[]{:S(2)}) async-start(bf16[16,128,2048]{2,1,0:T(8,128)(2,1)} %bitcast.5), calls=%async_computation | async-start | bytes 16777216 | tf_op jit(solution)/shard_map/all_to_all | solution.py:193

commit v2 on v1

--- a/solution.py
+++ b/solution.py
@@ -50,40 +50,50 @@
     )(fields)
 
 
-def sketch_kernel(scale, x_ref, t_ref, o_ref, acc):
-    k = pl.program_id(0)
-    x = x_ref[...].reshape(-1, x_ref.shape[-1])
-    g = nt(x, x)
-
-    @pl.when(k == 0)
-    def _():
-        acc[...] = g
-
-    @pl.when(k > 0)
-    def _():
-        acc[...] += g
-
-    @pl.when(k == pl.num_programs(0) - 1)
-    def _():
-        sk = lax.dot_general(t_ref[...], acc[...], (((0,), (0,)), ((), ())), precision=HIGH,
-                             preferred_element_type=F32) * scale
-        for c in range(4):
-            o_ref[c * 64:(c + 1) * 64, :] = sk[:, c * 128:(c + 1) * 128]
-
-
-def local_sketch(pieces, test_matrix, scale):
-    parts, s, m, w = pieces.shape
+def sketch_kernel(scale, x_ref, t_ref, o_ref):
+    parts, s, m, w = x_ref.shape
+    h = parts * m // 2
+    gram = [None] * 3
+    for k in range(s):
+        x = x_ref[:, k].reshape(2 * h, w)
+        top, low = x[:h], x[h:]
+        for i, (p, q) in enumerate(((top, top), (top, low), (low, low))):
+            g = nt(p, q)
+            gram[i] = g if k == 0 else gram[i] + g
+    gram = jnp.concatenate([jnp.concatenate(gram[:2], axis=1),
+                            jnp.concatenate([gram[1].T, gram[2]], axis=1)], axis=0)
+    sk = jnp.dot(t_ref[...], gram, precision=HIGH, preferred_element_type=F32) * scale
+    for c in range(4):
+        o_ref[c * 64:(c + 1) * 64, :] = sk[:, c * 128:(c + 1) * 128]
+
+
+def local_sketch(pieces, test_t, scale):
     return pl.pallas_call(
         lambda *r: sketch_kernel(scale, *r),
-        grid=(s,),
-        in_specs=[pl.BlockSpec((parts, 1, m, w), lambda k: (0, k, 0, 0)),
-                  pl.BlockSpec((512, 64), lambda k: (0, 0))],
-        out_specs=pl.BlockSpec((256, 128), lambda k: (0, 0)),
+        in_specs=[VM, VM],
+        out_specs=VM,
         out_shape=jax.ShapeDtypeStruct((256, 128), F32),
-        scratch_shapes=[pltpu.VMEM((512, 512), F32)],
-        compiler_params=pltpu.CompilerParams(vmem_limit_bytes=16 << 20),
+        compiler_params=pltpu.CompilerParams(vmem_limit_bytes=24 << 20),
         name="sketch",
-    )(pieces, test_matrix)
+    )(pieces, test_t)
+
+
+def total_kernel(x_ref, o_ref):
+    y = jnp.sum(x_ref[...].reshape(-1, 8, 128), axis=0)
+    y = y + pltpu.roll(y, 4, 0)
+    y = y + pltpu.roll(y, 2, 0)
+    o_ref[...] = jnp.broadcast_to(y[None], (32, 8, 128)).reshape(256, 128)
+
+
+def total(part):
+    return pl.pallas_call(
+        total_kernel,
+        in_specs=[VM],
+        out_specs=VM,
+        out_shape=jax.ShapeDtypeStruct((256, 128), F32),
+        compiler_params=pltpu.CompilerParams(vmem_limit_bytes=2 << 20),
+        name="total",
+    )(part)
 
 
 def inverse_lower(aug, step):
@@ -127,12 +137,8 @@
     return jnp.dot(inverse_lower(aug, step), yt, precision=HIGH, preferred_element_type=F32)
 
 
-def core_kernel(y_ref, x_ref, f_ref, o_ref, buf, sem):
-    s = x_ref.shape[1]
-    w = x_ref.shape[-1]
-    loads = [pltpu.make_async_copy(x_ref.at[:, k], buf.at[k], sem.at[k]) for k in range(s)]
-    for c in loads:
-        c.start()
+def core_kernel(y_ref, x_ref, f_ref, o_ref):
+    parts, s, m, w = x_ref.shape
     yt = jnp.concatenate([y_ref[c * 64:(c + 1) * 64, :] for c in range(4)], axis=1)
     ft = orthonormal_t(orthonormal_t(yt, 4), 4)
     f_ref[...] = ft
@@ -141,44 +147,48 @@
     j = lax.broadcasted_iota(jnp.int32, (64 * s, 64), 1)
     wide = [jnp.dot((i == j * s + k).astype(BF16), low, preferred_element_type=F32).astype(BF16)
             for k in range(s)]
-    for c in loads:
-        c.wait()
     step = 512
     for c in range(w // step):
         acc = None
         for k in range(s):
-            x = buf[k, :, :, c * step:(c + 1) * step].reshape(512, step)
+            x = x_ref[:, k, :, c * step:(c + 1) * step].reshape(parts * m, step)
             t = jnp.dot(wide[k], x, preferred_element_type=F32)
             acc = t if acc is None else acc + t
-        o_ref[:, :, c * step:(c + 1) * step] = acc.astype(BF16).reshape(16, 4 * s, step)
+        o_ref[:, :, :, c * step:(c + 1) * step] = acc.astype(BF16).reshape(o_ref.shape[:3] + (step,))
 
 
 def core_blocks(full, pieces):
     parts, s, m, w = pieces.shape
     return pl.pallas_call(
         core_kernel,
-        in_specs=[VM, ANY],
+        in_specs=[VM, VM],
         out_specs=[VM, VM],
         out_shape=[jax.ShapeDtypeStruct((64, 512), F32),
-                   jax.ShapeDtypeStruct((parts, 4 * s, w), BF16)],
-        scratch_shapes=[pltpu.VMEM((s, parts, m, w), BF16), pltpu.SemaphoreType.DMA((s,))],
+                   jax.ShapeDtypeStruct((parts, 64 // parts, s, w), BF16)],
         compiler_params=pltpu.CompilerParams(vmem_limit_bytes=24 << 20),
         name="core",
     )(full, pieces)
 
 
-def merge_kernel(x_ref, o_ref):
-    o_ref[...] = x_ref[0].reshape(o_ref.shape)
-
-
-def merge_cells(core, s):
-    parts, q, w = core.shape
+def merge_kernel(x_ref, o_ref, sem):
+    parts, _, _, w = x_ref.shape
+    copies = [pltpu.make_async_copy(x_ref.at[j], o_ref.at[:, :, pl.ds(j * w, w)], sem.at[j])
+              for j in range(parts)]
+    for c in copies:
+        c.start()
+    for c in copies:
+        c.wait()
+
+
+def merge_cells(core):
+    parts, q, s, w = core.shape
     return pl.pallas_call(
         merge_kernel,
-        grid=(parts,),
-        in_specs=[pl.BlockSpec((1, q, w), lambda j: (j, 0, 0))],
-        out_specs=pl.BlockSpec((q // s, s, w), lambda j: (0, 0, j)),
-        out_shape=jax.ShapeDtypeStruct((q // s, s, parts * w), BF16),
+        in_specs=[VM],
+        out_specs=ANY,
+        out_shape=jax.ShapeDtypeStruct((q, s, parts * w), BF16),
+        scratch_shapes=[pltpu.SemaphoreType.DMA((parts,))],
+        compiler_params=pltpu.CompilerParams(vmem_limit_bytes=4 << 20),
         name="merge",
     )(core)
 
@@ -192,13 +202,13 @@
     f = split_cells(fields, parts).reshape(parts, s * m, w)
     pieces = lax.all_to_all(f, "gx", split_axis=0, concat_axis=0, tiled=True)
     pieces = pieces.reshape(parts, s, m, w)
-    part = local_sketch(pieces, test_matrix, scale)
+    part = local_sketch(pieces, test_matrix.T, scale)
     part = lax.all_to_all(part.reshape(128, 2, 128), axes, split_axis=0, concat_axis=0, tiled=True)
-    part = jnp.sum(part, axis=0, keepdims=True)
-    full = lax.all_to_all(jnp.broadcast_to(part, (128, 2, 128)), axes, split_axis=0, concat_axis=0, tiled=True)
+    part = total(part.reshape(256, 128))
+    full = lax.all_to_all(part.reshape(128, 2, 128), axes, split_axis=0, concat_axis=0, tiled=True)
     ft, core = core_blocks(full.reshape(256, 128), pieces)
     core = lax.all_to_all(core, "gx", split_axis=0, concat_axis=0, tiled=True)
-    return (ft.T, merge_cells(core, s))
+    return (ft.T, merge_cells(core))
 
 
 def solution(mesh):

time: 224 us -> 175 us (0.78)
  waiting for transfers between devices: 124 us -> 0 us
  blocking collectives: 53.9 us -> 154 us
  Pallas kernels: 30.3 us -> 16.9 us
  starting transfers between devices: 7.33 us -> 0 us
  local copies, waits for them, and re-layouts: 6.75 us -> 3.38 us
    all_to_all x1 -> x0, waiting for transfers between devices: 124 us -> none  [body(): pieces = lax.all_to_all(f, 'gx', split_axis=0, concat_axis=0, tiled=True)]
    all_to_all x1, blocking collectives: 14.2 us -> 103 us  [body(): pieces = lax.all_to_all(f, 'gx', split_axis=0, concat_axis=0, tiled=True)]
    pallas_call x3 -> x4, Pallas kernels: 28.8 us -> 15.4 us  [the longest x1 10 us: core_blocks(): pl.pallas_call(core_kernel, in_specs=[VM, VM], out_specs=[VM, VM], out_sh...]
    all_to_all x1 -> x2, blocking collectives: 19.3 us -> 31 us  [body(): lax.all_to_all(part.reshape(128, 2, 128), axes, split_axis=0, concat_axis...]
    all_to_all x1 -> x0, starting transfers between devices: 7.33 us -> none  [body(): pieces = lax.all_to_all(f, 'gx', split_axis=0, concat_axis=0, tiled=True)]
    unnamed x7 -> x4, local copies, waits for them, and re-layouts: 6.72 us -> 3.38 us
  transfers between devices with their start and end apart: 1 -> 0, of which waited for: 1 -> 0; matrix products, arithmetic and copies ran while one was open for 0% -> 0% of each run, Pallas kernels for 0% -> 0%
where the time goes in v2:
time: 175 us
  blocking collectives  154 us (88%)
  Pallas kernels  16.9 us (10%)
  local copies, waits for them, and re-layouts  3.38 us (2%)
    all_to_all x1, blocking collectives, body(): pieces = lax.all_to_all(f, 'gx', split_axis=0, concat_axis=0, tiled=True)  103 us
    all_to_all x2, blocking collectives, body(): lax.all_to_all(part.reshape(128, 2, 128), axes, split_axis=0, concat_axis...  31 us
    all_to_all x1, blocking collectives, body(): core = lax.all_to_all(core, 'gx', split_axis=0, concat_axis=0, tiled=True)  20 us
    pallas_call x1, Pallas kernels, core_blocks(): pl.pallas_call(core_kernel, in_specs=[VM, VM], out_specs=[VM, VM], out_sh...  10 us
    pallas_call x1, Pallas kernels, local_sketch(): pl.pallas_call(lambda *r: sketch_kernel(scale, *r), in_specs=[VM, VM], ou...  4.28 us

profile of v2, /device:TPU:0, one launch (start us, length us, event | category | flops | bytes accessed | tf_op | source)
XLA Modules:
  0.0 174.9 jit_solution(8190155069243520887)
XLA Ops:
  0.6 0.0 copy-start
  0.6 3.4 %copy-done = bf16[4,32,32768]{2,1,0:T(8,128)(2,1)S(1)} copy-done((bf16[4,32,32768]{2,1,0:T(8,128)(2,1)S(1)}, bf16[4,32,32768]{2,1,0:T(8,128)(2,1)}, u32[]{:S(2)}) %copy-start) | copy-done | bytes 8388632
  4.0 1.5 split.1
  5.5 0.0 copy-start.1
  5.5 102.9 %all_to_all.20 = bf16[16,128,2048]{2,1,0:T(8,128)(2,1)S(1)} all-to-all(bf16[16,128,2048]{2,1,0:T(8,128)(2,1)S(1)} %bitcast.10), channel_id=1, replica_groups=mesh['gx'=16,'yz'=8] {'gx'}, dimensions={0} | all-to-all | bytes 16777216 | tf_op jit(solution)/shard_map/all_to_all | solution.py:203
  108.4 0.0 copy-done.1
  108.4 4.3 %sketch.1 = f32[256,128]{1,0:T(8,128)S(1)} custom-call(bf16[16,4,32,2048]{3,2,1,0:T(8,128)(2,1)S(1)} %bitcast.8, f32[64,512]{1,0:T(8,128)S(1)} %bitcast.15), custom_call_target="tpu_custom_call" | custom-call | tf_op jit(solution)/shard_map/sketch/pallas_call | solution.py:71
  112.7 16.9 %all_to_all.21 = f32[128,2,128]{2,1,0:T(2,128)S(1)} all-to-all(f32[128,2,128]{2,1,0:T(2,128)S(1)} %bitcast.12), channel_id=1, replica_groups=mesh['gx'=16,'yz'=8] {'gx','yz'}, dimensions={0} | all-to-all | bytes 262144 | tf_op jit(solution)/shard_map/all_to_all | solution.py:206
  129.6 14.2 %all_to_all.22 = f32[128,2,128]{2,1,0:T(2,128)S(1)} all-to-all(f32[128,2,128]{2,1,0:T(2,128)S(1)} %bitcast.14), channel_id=1, replica_groups=mesh['gx'=16,'yz'=8] {'gx','yz'}, dimensions={0} | all-to-all | bytes 262144 | tf_op jit(solution)/shard_map/all_to_all | solution.py:208
  143.8 10.0 %core.1 = (f32[64,512]{1,0:T(8,128)}, bf16[16,4,4,2048]{3,2,1,0:T(4,128)(2,1)S(1)}) custom-call(f32[256,128]{1,0:T(8,128)S(1)} %bitcast.11, bf16[16,4,32,2048]{3,2,1,0:T(8,128)(2,1)S(1)} %bitcast.9), custom_call_target="tpu_custom_call" | custom-call | tf_op jit(solution)/shard_map/core/pallas_call | solution.py:162
  153.8 20.0 %all_to_all.23.x_ref = bf16[16,4,4,2048]{3,2,1,0:T(4,128)(2,1)S(1)} all-to-all(bf16[16,4,4,2048]{3,2,1,0:T(4,128)(2,1)S(1)} %get-tuple-element.5), channel_id=1, replica_groups=mesh['gx'=16,'yz'=8] {'gx'}, dimensions={0} | all-to-all | bytes 2097152 | tf_op jit(solution)/shard_map/all_to_all | solution.py:210
  173.8 1.1 merge.1
  (1 shorter events, 0.0 us)
Async XLA Ops:
  0.6 3.4 %copy-start = (bf16[4,32,32768]{2,1,0:T(8,128)(2,1)S(1)}, bf16[4,32,32768]{2,1,0:T(8,128)(2,1)}, u32[]{:S(2)}) copy-start(bf16[4,32,32768]{2,1,0:T(8,128)(2,1)} %x_ref.1) | copy-start | bytes 25165828
  5.5 102.9 %copy-start.1 = (f32[512,64]{0,1:T(8,128)S(1)}, f32[512,64]{0,1:T(8,128)}, u32[]{:S(2)}) copy-start(f32[512,64]{0,1:T(8,128)} %param.3) | copy-start | bytes 393220

commit v3 on v2

--- a/solution.py
+++ b/solution.py
@@ -17,49 +17,92 @@
                            preferred_element_type=F32)
 
 
-def split_kernel(x_ref, o_ref, buf, sem_in, sem_out):
-    parts, _, _, w = o_ref.shape
-
-    def load(j):
-        return pltpu.make_async_copy(x_ref.at[:, :, pl.ds(j * w, w)], buf.at[j], sem_in.at[j])
-
-    def store(j):
-        return pltpu.make_async_copy(buf.at[j], o_ref.at[j], sem_out.at[j])
-
-    for j in range(parts):
-        load(j).start()
-    for j in range(parts):
-        load(j).wait()
-        store(j).start()
-    for j in range(parts):
-        store(j).wait()
-
-
-def split_cells(fields, parts):
-    s, m, n = fields.shape
-    shape = (parts, s, m, n // parts)
-    return pl.pallas_call(
+def place():
+    g = lax.axis_index("gx")
+    return lax.rem(g, 4), lax.div(g, 4)
+
+
+def member(x, y):
+    return lax.rem(y + 4, 4) * 4 + lax.rem(x + 4, 4)
+
+
+def split_kernel(x_ref, *outs):
+    w = outs[0].shape[-1]
+    x, y = place()
+    for k in range(2):
+        for d in range(4):
+            for q in range(4):
+                j = member(x + q, y + d) if k else member(x + d, y + q)
+                outs[4 * k + d][q] = x_ref[k, :, pl.ds(pl.multiple_of(j * w, w), w)]
+
+
+def split_pair(pair, parts):
+    _, m, n = pair.shape
+    out = jax.ShapeDtypeStruct((4, m, n // parts), pair.dtype)
+    outs = pl.pallas_call(
         split_kernel,
-        in_specs=[ANY],
-        out_specs=ANY,
-        out_shape=jax.ShapeDtypeStruct(shape, fields.dtype),
-        scratch_shapes=[pltpu.VMEM(shape, fields.dtype),
-                        pltpu.SemaphoreType.DMA((parts,)), pltpu.SemaphoreType.DMA((parts,))],
-        compiler_params=pltpu.CompilerParams(vmem_limit_bytes=12 << 20),
+        in_specs=[VM],
+        out_specs=[VM] * 8,
+        out_shape=[out] * 8,
+        compiler_params=pltpu.CompilerParams(vmem_limit_bytes=10 << 20),
+        cost_estimate=pl.CostEstimate(flops=0, transcendentals=0, bytes_accessed=8 * m * n),
         name="split",
-    )(fields)
-
-
-def sketch_kernel(scale, x_ref, t_ref, o_ref):
-    parts, s, m, w = x_ref.shape
+    )(pair)
+    return list(outs[:4]), list(outs[4:])
+
+
+def shift(v, along, d):
+    step = 1 if along == "x" else 4
+    pairs = []
+    for g in range(16):
+        c = (g // step) % 4
+        pairs.append((g, g + ((c + d) % 4 - c) * step))
+    return lax.ppermute(v, "gx", pairs)
+
+
+def regroup_kernel(*refs):
+    for k in range(2):
+        got, out = refs[4 * k:4 * k + 4], refs[8 + 3 * k:11 + 3 * k]
+        for q in range(1, 4):
+            for d in range(4):
+                out[q - 1][d] = got[d][q]
+
+
+def regroup(one, two):
+    out = jax.ShapeDtypeStruct(one[0].shape, one[0].dtype)
+    outs = pl.pallas_call(
+        regroup_kernel,
+        in_specs=[VM] * 8,
+        out_specs=[VM] * 6,
+        out_shape=[out] * 6,
+        compiler_params=pltpu.CompilerParams(vmem_limit_bytes=6 << 20),
+        cost_estimate=pl.CostEstimate(flops=0, transcendentals=0, bytes_accessed=4 * out.size),
+        name="regroup",
+    )(*one, *two)
+    return outs[:3], outs[3:]
+
+
+def gram_kernel(first, scale, *refs):
+    blocks, rest = refs[:7], list(refs[7:])
+    acc = rest.pop(0) if len(rest) > 2 else None
+    t_ref = rest.pop(0) if len(rest) > 2 else None
+    p_ref, o_ref = rest
+    parts, m, w = p_ref.shape
+    x, y = place()
+    for d1 in range(4):
+        for d2 in range(4):
+            g = member(x - d1, y - d2) if first == "x" else member(x - d2, y - d1)
+            p_ref[g] = blocks[d1][0] if d2 == 0 else blocks[3 + d2][d1]
     h = parts * m // 2
-    gram = [None] * 3
-    for k in range(s):
-        x = x_ref[:, k].reshape(2 * h, w)
-        top, low = x[:h], x[h:]
-        for i, (p, q) in enumerate(((top, top), (top, low), (low, low))):
-            g = nt(p, q)
-            gram[i] = g if k == 0 else gram[i] + g
+    top = p_ref[:parts // 2].reshape(h, w)
+    low = p_ref[parts // 2:].reshape(h, w)
+    gram = [nt(p, q) for p, q in ((top, top), (top, low), (low, low))]
+    if acc is not None:
+        gram = [g + acc[k] for k, g in enumerate(gram)]
+    if t_ref is None:
+        for k in range(3):
+            o_ref[k] = gram[k]
+        return
     gram = jnp.concatenate([jnp.concatenate(gram[:2], axis=1),
                             jnp.concatenate([gram[1].T, gram[2]], axis=1)], axis=0)
     sk = jnp.dot(t_ref[...], gram, precision=HIGH, preferred_element_type=F32) * scale
@@ -67,15 +110,20 @@
         o_ref[c * 64:(c + 1) * 64, :] = sk[:, c * 128:(c + 1) * 128]
 
 
-def local_sketch(pieces, test_t, scale):
-    return pl.pallas_call(
-        lambda *r: sketch_kernel(scale, *r),
-        in_specs=[VM, VM],
-        out_specs=VM,
-        out_shape=jax.ShapeDtypeStruct((256, 128), F32),
-        compiler_params=pltpu.CompilerParams(vmem_limit_bytes=24 << 20),
-        name="sketch",
-    )(pieces, test_t)
+def add_gram(first, blocks, acc=None, test_t=None, scale=1.0):
+    _, m, w = blocks[0].shape
+    args = list(blocks) + [v for v in (acc, test_t) if v is not None]
+    shape = (3, 256, 256) if test_t is None else (256, 128)
+    return pl.pallas_call(
+        lambda *r: gram_kernel(first, scale, *r),
+        in_specs=[VM] * len(args),
+        out_specs=[VM, VM],
+        out_shape=[jax.ShapeDtypeStruct((16, m, w), BF16), jax.ShapeDtypeStruct(shape, F32)],
+        compiler_params=pltpu.CompilerParams(vmem_limit_bytes=16 << 20),
+        cost_estimate=pl.CostEstimate(flops=3 * 2 * 256 * 256 * w, transcendentals=0,
+                                      bytes_accessed=16 * m * w * 4),
+        name="gram",
+    )(*args)
 
 
 def total_kernel(x_ref, o_ref):
@@ -137,10 +185,12 @@
     return jnp.dot(inverse_lower(aug, step), yt, precision=HIGH, preferred_element_type=F32)
 
 
-def core_kernel(y_ref, x_ref, f_ref, o_ref):
-    parts, s, m, w = x_ref.shape
+def core_kernel(y_ref, *refs):
+    x_refs, (f_ref, o_ref) = refs[:-2], refs[-2:]
+    s = len(x_refs)
+    parts, m, w = x_refs[0].shape
     yt = jnp.concatenate([y_ref[c * 64:(c + 1) * 64, :] for c in range(4)], axis=1)
-    ft = orthonormal_t(orthonormal_t(yt, 4), 4)
+    ft = orthonormal_t(orthonormal_t(yt, 8), 8)
     f_ref[...] = ft
     low = ft.astype(BF16)
     i = lax.broadcasted_iota(jnp.int32, (64 * s, 64), 0)
@@ -151,23 +201,24 @@
     for c in range(w // step):
         acc = None
         for k in range(s):
-            x = x_ref[:, k, :, c * step:(c + 1) * step].reshape(parts * m, step)
+            x = x_refs[k][:, :, c * step:(c + 1) * step].reshape(parts * m, step)
             t = jnp.dot(wide[k], x, preferred_element_type=F32)
             acc = t if acc is None else acc + t
         o_ref[:, :, :, c * step:(c + 1) * step] = acc.astype(BF16).reshape(o_ref.shape[:3] + (step,))
 
 
 def core_blocks(full, pieces):
-    parts, s, m, w = pieces.shape
+    s = len(pieces)
+    parts, _, w = pieces[0].shape
     return pl.pallas_call(
         core_kernel,
-        in_specs=[VM, VM],
+        in_specs=[VM] * (1 + s),
         out_specs=[VM, VM],
         out_shape=[jax.ShapeDtypeStruct((64, 512), F32),
                    jax.ShapeDtypeStruct((parts, 64 // parts, s, w), BF16)],
         compiler_params=pltpu.CompilerParams(vmem_limit_bytes=24 << 20),
         name="core",
-    )(full, pieces)
+    )(full, *pieces)
 
 
 def merge_kernel(x_ref, o_ref, sem):
@@ -194,15 +245,35 @@
 
 
 def body(fields, test_matrix):
-    s, m, n = fields.shape
+    s, _, n = fields.shape
     parts = lax.axis_size("gx")
-    w = n // parts
     axes = ("gx", "yz")
     scale = 1.0 / (s * n * lax.axis_size("yz"))
-    f = split_cells(fields, parts).reshape(parts, s * m, w)
-    pieces = lax.all_to_all(f, "gx", split_axis=0, concat_axis=0, tiled=True)
-    pieces = pieces.reshape(parts, s, m, w)
-    part = local_sketch(pieces, test_matrix.T, scale)
+    order = ("x", "y", "x", "y")
+    near = [None] * s
+    for k in (0, 2):
+        if k:
+            fields, near[0][0] = lax.optimization_barrier((fields, near[0][0]))
+        near[k], near[k + 1] = split_pair(fields[k:k + 2], parts)
+    for k in (0, 2):
+        far = [[near[k + i][0]] + [None] * 3 for i in range(2)]
+        for d in (1, 3, 2):
+            for i in range(2):
+                far[i][d] = shift(near[k + i][d], order[k + i], d)
+        near[k], near[k + 1] = far
+    blocks = [None] * s
+    for k in (0, 2):
+        sent = regroup(near[k], near[k + 1])
+        rest = [[None] * 3, [None] * 3]
+        for d in (1, 3, 2):
+            for i in range(2):
+                rest[i][d - 1] = shift(sent[i][d - 1], order[1 - i], d)
+        for i in range(2):
+            blocks[k + i] = list(near[k + i]) + rest[i]
+    pieces = [None] * s
+    part = None
+    for k in range(s):
+        pieces[k], part = add_gram(order[k], blocks[k], part, test_matrix.T if k == s - 1 else None, scale)
     part = lax.all_to_all(part.reshape(128, 2, 128), axes, split_axis=0, concat_axis=0, tiled=True)
     part = total(part.reshape(256, 128))
     full = lax.all_to_all(part.reshape(128, 2, 128), axes, split_axis=0, concat_axis=0, tiled=True)

time: 175 us -> 189 us (1.080)
  blocking collectives: 154 us -> 52.7 us
  waiting for transfers between devices: 0 us -> 84.8 us
  starting transfers between devices: 0 us -> 31.5 us
    all_to_all x1 -> x0, blocking collectives: 103 us -> none  [body(): pieces = lax.all_to_all(f, 'gx', split_axis=0, concat_axis=0, tiled=True)]
    ppermute x0 -> x24, waiting for transfers between devices: none -> 84.8 us  [shift(): return lax.ppermute(v, 'gx', pairs)]
    ppermute x0 -> x24, starting transfers between devices: none -> 31.5 us  [shift(): return lax.ppermute(v, 'gx', pairs)]
    unnamed x4, local copies, waits for them, and re-layouts: 3.38 us -> 0.01 us
    slice x0 -> x2, local copies, waits for them, and re-layouts: none -> 2.88 us  [body(): near[k], near[k + 1] = split_pair(fields[k:k + 2], parts)]
    pallas_call x3 -> x9, Pallas kernels: 15.8 us -> 14.5 us  [the longest x1 8.05 us: core_blocks(): pl.pallas_call(core_kernel, in_specs=[VM] * (1 + s), out_specs=[VM, VM],...]
  transfers between devices with their start and end apart: 0 -> 24, of which waited for: 0 -> 11; matrix products, arithmetic and copies ran while one was open for 0% -> 0% of each run, Pallas kernels for 0% -> 2%
where the time goes in v3:
time: 189 us; the launch traced here: 188 us
  waiting for transfers between devices  84.8 us (45%)
  blocking collectives  52.7 us (28%)
  starting transfers between devices  31.5 us (17%)
  Pallas kernels  15.6 us (8%)
  local copies, waits for them, and re-layouts  2.89 us (2%)
    ppermute x24, waiting for transfers between devices, shift(): return lax.ppermute(v, 'gx', pairs)  84.8 us
    all_to_all x2, blocking collectives, body(): lax.all_to_all(part.reshape(128, 2, 128), axes, split_axis=0, concat_axis...  32.7 us
    ppermute x24, starting transfers between devices, shift(): return lax.ppermute(v, 'gx', pairs)  31.5 us
    all_to_all x1, blocking collectives, body(): core = lax.all_to_all(core, 'gx', split_axis=0, concat_axis=0, tiled=True)  20.1 us
    pallas_call x1, Pallas kernels, core_blocks(): pl.pallas_call(core_kernel, in_specs=[VM] * (1 + s), out_specs=[VM, VM],...  8.05 us
    pallas_call x4, Pallas kernels, add_gram(): pl.pallas_call(lambda *r: gram_kernel(first, scale, *r), in_specs=[VM] *...  5.42 us
  transfers between devices with their start and end apart: 24, of which 11 were waited for; matrix products, arithmetic and copies ran while one was open for 0% of the time, Pallas kernels for 2%

profile of v3, /device:TPU:0, one launch (start us, length us, event | category | flops | bytes accessed | tf_op | source)
XLA Modules:
  0.0 188.5 jit_solution(6266012696715320476)
XLA Ops:
  0.6 2.6 %slice.6.x_ref = bf16[2,32,32768]{2,1,0:T(8,128)(2,1)S(1)} slice(bf16[4,32,32768]{2,1,0:T(8,128)(2,1)} %param.2), slice={[0:2], [0:32], [0:32768]} | slice | bytes 8388608 | tf_op jit(solution)/shard_map/slice | solution.py:257
  3.3 0.3 split.2
  3.6 1.8 collective-permute-start.12
  5.3 2.9 %collective-permute-start.13 = (bf16[4,32,2048]{2,1,0:T(8,128)(2,1)S(1)}, bf16[4,32,2048]{2,1,0:T(8,128)(2,1)S(1)}, u32[]{:S(2)}, u32[]{:S(2)}) collective-permute-start(bf16[4,32,2048]{2,1,0:T(8,128)(2,1)S(1)} %get-tuple-element.60), channel_id=1, source_target_pairs={{0,64},{8,72},{16,80},{24,88},{32,96},{40,104},{48,112},{56,120},{... | collective-permute-start | bytes 1572872 | tf_op jit(solution)/shard_map/ppermute | solution.py:60
  8.2 1.3 collective-permute-start.14
  9.6 1.5 collective-permute-start.15
  11.0 2.7 %collective-permute-start.16 = (bf16[4,32,2048]{2,1,0:T(8,128)(2,1)S(1)}, bf16[4,32,2048]{2,1,0:T(8,128)(2,1)S(1)}, u32[]{:S(2)}, u32[]{:S(2)}) collective-permute-start(bf16[4,32,2048]{2,1,0:T(8,128)(2,1)S(1)} %get-tuple-element.64), channel_id=1, source_target_pairs={{0,16},{8,24},{16,0},{24,8},{32,48},{40,56},{48,32},{56,40},{64,80... | collective-permute-start | bytes 1572872 | tf_op jit(solution)/shard_map/ppermute | solution.py:60
  13.8 4.9 %collective-permute-done.12.refs_5_.r_1_ = bf16[4,32,2048]{2,1,0:T(8,128)(2,1)S(1)} collective-permute-done((bf16[4,32,2048]{2,1,0:T(8,128)(2,1)S(1)}, bf16[4,32,2048]{2,1,0:T(8,128)(2,1)S(1)}, u32[]{:S(2)}, u32[]{:S(2)}) %collective-permute-start.12) | collective-permute-done | bytes 524320 | tf_op jit(solution)/shard_map/ppermute | solution.py:60
  18.7 2.8 %collective-permute-start.17 = (bf16[4,32,2048]{2,1,0:T(8,128)(2,1)S(1)}, bf16[4,32,2048]{2,1,0:T(8,128)(2,1)S(1)}, u32[]{:S(2)}, u32[]{:S(2)}) collective-permute-start(bf16[4,32,2048]{2,1,0:T(8,128)(2,1)S(1)} %get-tuple-element.65), channel_id=1, source_target_pairs={{0,24},{8,0},{16,8},{24,16},{32,56},{40,32},{48,40},{56,48},{64,88... | collective-permute-start | bytes 1572872 | tf_op jit(solution)/shard_map/ppermute | solution.py:60
  21.4 0.3 slice.7.x_ref
  21.7 0.3 split.3
  22.0 9.1 %collective-permute-done.13.refs_6_.r_2_ = bf16[4,32,2048]{2,1,0:T(8,128)(2,1)S(1)} collective-permute-done((bf16[4,32,2048]{2,1,0:T(8,128)(2,1)S(1)}, bf16[4,32,2048]{2,1,0:T(8,128)(2,1)S(1)}, u32[]{:S(2)}, u32[]{:S(2)}) %collective-permute-start.13) | collective-permute-done | bytes 524320 | tf_op jit(solution)/shard_map/ppermute | solution.py:60
  31.1 4.3 %collective-permute-start.1 = (bf16[4,32,2048]{2,1,0:T(8,128)(2,1)S(1)}, bf16[4,32,2048]{2,1,0:T(8,128)(2,1)S(1)}, u32[]{:S(2)}, u32[]{:S(2)}) collective-permute-start(bf16[4,32,2048]{2,1,0:T(8,128)(2,1)S(1)} %get-tuple-element.46), channel_id=1, source_target_pairs={{0,64},{8,72},{16,80},{24,88},{32,96},{40,104},{48,112},{56,120},{... | collective-permute-start | bytes 1572872 | tf_op jit(solution)/shard_map/ppermute | solution.py:60
  35.3 0.0 collective-permute-done.15.refs_1_.r_1_
  35.3 2.5 %collective-permute-start.2 = (bf16[4,32,2048]{2,1,0:T(8,128)(2,1)S(1)}, bf16[4,32,2048]{2,1,0:T(8,128)(2,1)S(1)}, u32[]{:S(2)}, u32[]{:S(2)}) collective-permute-start(bf16[4,32,2048]{2,1,0:T(8,128)(2,1)S(1)} %get-tuple-element.47), channel_id=1, source_target_pairs={{0,96},{8,104},{16,112},{24,120},{32,0},{40,8},{48,16},{56,24},{64... | collective-permute-start | bytes 1572872 | tf_op jit(solution)/shard_map/ppermute | solution.py:60
  37.9 2.3 %collective-permute-start.4 = (bf16[4,32,2048]{2,1,0:T(8,128)(2,1)S(1)}, bf16[4,32,2048]{2,1,0:T(8,128)(2,1)S(1)}, u32[]{:S(2)}, u32[]{:S(2)}) collective-permute-start(bf16[4,32,2048]{2,1,0:T(8,128)(2,1)S(1)} %get-tuple-element.50), channel_id=1, source_target_pairs={{0,16},{8,24},{16,0},{24,8},{32,48},{40,56},{48,32},{56,40},{64,80... | collective-permute-start | bytes 1572872 | tf_op jit(solution)/shard_map/ppermute | solution.py:60
  40.2 16.2 %collective-permute-done.refs_5_.r_1_ = bf16[4,32,2048]{2,1,0:T(8,128)(2,1)S(1)} collective-permute-done((bf16[4,32,2048]{2,1,0:T(8,128)(2,1)S(1)}, bf16[4,32,2048]{2,1,0:T(8,128)(2,1)S(1)}, u32[]{:S(2)}, u32[]{:S(2)}) %collective-permute-start) | collective-permute-done | bytes 524320 | tf_op jit(solution)/shard_map/ppermute | solution.py:60
  56.3 2.8 %collective-permute-start.5 = (bf16[4,32,2048]{2,1,0:T(8,128)(2,1)S(1)}, bf16[4,32,2048]{2,1,0:T(8,128)(2,1)S(1)}, u32[]{:S(2)}, u32[]{:S(2)}) collective-permute-start(bf16[4,32,2048]{2,1,0:T(8,128)(2,1)S(1)} %get-tuple-element.51), channel_id=1, source_target_pairs={{0,24},{8,0},{16,8},{24,16},{32,56},{40,32},{48,40},{56,48},{64,88... | collective-permute-start | bytes 1572872 | tf_op jit(solution)/shard_map/ppermute | solution.py:60
  59.1 0.2 regroup.3
  59.3 0.1 collective-permute-start.18
  59.4 2.3 %collective-permute-start.19 = (bf16[4,32,2048]{2,1,0:T(8,128)(2,1)S(1)}, bf16[4,32,2048]{2,1,0:T(8,128)(2,1)S(1)}, u32[]{:S(2)}, u32[]{:S(2)}) collective-permute-start(bf16[4,32,2048]{2,1,0:T(8,128)(2,1)S(1)} %get-tuple-element.67), channel_id=1, source_target_pairs={{0,16},{8,24},{16,0},{24,8},{32,48},{40,56},{48,32},{56,40},{64,80... | collective-permute-start | bytes 1572872 | tf_op jit(solution)/shard_map/ppermute | solution.py:60
  61.7 1.1 collective-permute-start.20
  62.8 0.0 collective-permute-done.4.refs_2_.r_2_
  62.8 1.1 collective-permute-start.21
  64.0 18.5 %collective-permute-done.5.refs_3_.r_3_ = bf16[4,32,2048]{2,1,0:T(8,128)(2,1)S(1)} collective-permute-done((bf16[4,32,2048]{2,1,0:T(8,128)(2,1)S(1)}, bf16[4,32,2048]{2,1,0:T(8,128)(2,1)S(1)}, u32[]{:S(2)}, u32[]{:S(2)}) %collective-permute-start.5) | collective-permute-done | bytes 524320 | tf_op jit(solution)/shard_map/ppermute | solution.py:60
  82.5 0.0 collective-permute-start.22
  82.5 0.2 regroup.2
  82.7 1.2 collective-permute-done.18.r_4_
  84.0 0.0 collective-permute-start.23
  84.0 0.0 collective-permute-done.19.r_5_
  84.0 2.0 %collective-permute-start.9 = (bf16[4,32,2048]{2,1,0:T(8,128)(2,1)S(1)}, bf16[4,32,2048]{2,1,0:T(8,128)(2,1)S(1)}, u32[]{:S(2)}, u32[]{:S(2)}) collective-permute-start(bf16[4,32,2048]{2,1,0:T(8,128)(2,1)S(1)} %get-tuple-element.55), channel_id=1, source_target_pairs={{0,32},{8,40},{16,48},{24,56},{32,64},{40,72},{48,80},{56,88},{64,... | collective-permute-start | bytes 1572872 | tf_op jit(solution)/shard_map/ppermute | solution.py:60
  86.0 5.0 %collective-permute-done.20.r_6_ = bf16[4,32,2048]{2,1,0:T(8,128)(2,1)S(1)} collective-permute-done((bf16[4,32,2048]{2,1,0:T(8,128)(2,1)S(1)}, bf16[4,32,2048]{2,1,0:T(8,128)(2,1)S(1)}, u32[]{:S(2)}, u32[]{:S(2)}) %collective-permute-start.20) | collective-permute-done | bytes 524320 | tf_op jit(solution)/shard_map/ppermute | solution.py:60
  91.0 6.6 %collective-permute-done.22.r_5_ = bf16[4,32,2048]{2,1,0:T(8,128)(2,1)S(1)} collective-permute-done((bf16[4,32,2048]{2,1,0:T(8,128)(2,1)S(1)}, bf16[4,32,2048]{2,1,0:T(8,128)(2,1)S(1)}, u32[]{:S(2)}, u32[]{:S(2)}) %collective-permute-start.22) | collective-permute-done | bytes 524320 | tf_op jit(solution)/shard_map/ppermute | solution.py:60
  97.7 4.4 %collective-permute-done.23.r_6_ = bf16[4,32,2048]{2,1,0:T(8,128)(2,1)S(1)} collective-permute-done((bf16[4,32,2048]{2,1,0:T(8,128)(2,1)S(1)}, bf16[4,32,2048]{2,1,0:T(8,128)(2,1)S(1)}, u32[]{:S(2)}, u32[]{:S(2)}) %collective-permute-start.23) | collective-permute-done | bytes 524320 | tf_op jit(solution)/shard_map/ppermute | solution.py:60
  102.1 11.2 %collective-permute-done.9.r_4_ = bf16[4,32,2048]{2,1,0:T(8,128)(2,1)S(1)} collective-permute-done((bf16[4,32,2048]{2,1,0:T(8,128)(2,1)S(1)}, bf16[4,32,2048]{2,1,0:T(8,128)(2,1)S(1)}, u32[]{:S(2)}, u32[]{:S(2)}) %collective-permute-start.9) | collective-permute-done | bytes 524320 | tf_op jit(solution)/shard_map/ppermute | solution.py:60
  113.3 0.0 collective-permute-start.8
  113.3 1.2 gram.4
  114.5 1.2 gram.5
  115.7 0.0 copy-start
  115.7 1.2 gram.6
  116.9 0.4 collective-permute-done.6.r_4_
  117.3 7.1 %collective-permute-done.8.r_6_ = bf16[4,32,2048]{2,1,0:T(8,128)(2,1)S(1)} collective-permute-done((bf16[4,32,2048]{2,1,0:T(8,128)(2,1)S(1)}, bf16[4,32,2048]{2,1,0:T(8,128)(2,1)S(1)}, u32[]{:S(2)}, u32[]{:S(2)}) %collective-permute-start.8) | collective-permute-done | bytes 524320 | tf_op jit(solution)/shard_map/ppermute | solution.py:60
  124.4 1.9 %gram.7 = (bf16[16,32,2048]{2,1,0:T(8,128)(2,1)S(1)}, f32[256,128]{1,0:T(8,128)S(1)}) custom-call(bf16[4,32,2048]{2,1,0:T(8,128)(2,1)S(1)} %get-tuple-element.44.refs_4_.r_0_, bf16[4,32,2048]{2,1,0:T(8,128)(2,1)S(1)} %collective-permute-done.refs_5_.r_1_, bf16[4,32,2048]{2,1,0:T(8,128)(2,1)S(1)} %collective-permute-done.1.refs_6_.r_2_, ...), custom_call_target="tpu_custom_call" | custom-call | flops 805306368 | bytes 4194304 | tf_op jit(solution)/shard_map/gram/pallas_call | solution.py:117
  126.4 18.5 %all_to_all.15 = f32[128,2,128]{2,1,0:T(2,128)S(1)} all-to-all(f32[128,2,128]{2,1,0:T(2,128)S(1)} %bitcast.10), channel_id=1, replica_groups=mesh['gx'=16,'yz'=8] {'gx','yz'}, dimensions={0} | all-to-all | bytes 262144 | tf_op jit(solution)/shard_map/all_to_all | solution.py:277
  144.9 14.2 %all_to_all.16 = f32[128,2,128]{2,1,0:T(2,128)S(1)} all-to-all(f32[128,2,128]{2,1,0:T(2,128)S(1)} %bitcast.8), channel_id=1, replica_groups=mesh['gx'=16,'yz'=8] {'gx','yz'}, dimensions={0} | all-to-all | bytes 262144 | tf_op jit(solution)/shard_map/all_to_all | solution.py:279
  159.1 8.1 %core.1 = (f32[64,512]{1,0:T(8,128)}, bf16[16,4,4,2048]{3,2,1,0:T(4,128)(2,1)S(1)}) custom-call(f32[256,128]{1,0:T(8,128)S(1)} %bitcast.6, bf16[16,32,2048]{2,1,0:T(8,128)(2,1)S(1)} %get-tuple-element.76.refs_0_, bf16[16,32,2048]{2,1,0:T(8,128)(2,1)S(1)} %get-tuple-element.77.refs_1_, bf16[16,32,2048]{2,1,0:T(8,128)(2,1)S(1)} %get-tuple-element.78.refs_2_, ...), custom_call_target="tpu_custom_call" | custom-call | tf_op jit(solution)/shard_map/core/pallas_call | solution.py:213
  167.2 20.1 %all_to_all.17.x_ref = bf16[16,4,4,2048]{3,2,1,0:T(4,128)(2,1)S(1)} all-to-all(bf16[16,4,4,2048]{3,2,1,0:T(4,128)(2,1)S(1)} %get-tuple-element.81), channel_id=1, replica_groups=mesh['gx'=16,'yz'=8] {'gx'}, dimensions={0} | all-to-all | bytes 2097152 | tf_op jit(solution)/shard_map/all_to_all | solution.py:281
  187.2 1.1 merge.1
  (20 shorter events, 0.1 us)
Async XLA Ops:
  0.6 20.8 %copy-start.1 = (bf16[4,32,32768]{2,1,0:T(8,128)(2,1)S(1)}, bf16[4,32,32768]{2,1,0:T(8,128)(2,1)}, u32[]{:S(2)}) copy-start(bf16[4,32,32768]{2,1,0:T(8,128)(2,1)} %param.2) | copy-start | bytes 25165828
  3.6 15.1 %collective-permute-start.12 = (bf16[4,32,2048]{2,1,0:T(8,128)(2,1)S(1)}, bf16[4,32,2048]{2,1,0:T(8,128)(2,1)S(1)}, u32[]{:S(2)}, u32[]{:S(2)}) collective-permute-start(bf16[4,32,2048]{2,1,0:T(8,128)(2,1)S(1)} %get-tuple-element.59), channel_id=1, source_target_pairs={{0,32},{8,40},{16,48},{24,56},{32,64},{40,72},{48,80},{56,88},{64,... | collective-permute-start | bytes 1572872 | tf_op jit(solution)/shard_map/ppermute | solution.py:60
  5.3 25.8 %collective-permute-start.13 = (bf16[4,32,2048]{2,1,0:T(8,128)(2,1)S(1)}, bf16[4,32,2048]{2,1,0:T(8,128)(2,1)S(1)}, u32[]{:S(2)}, u32[]{:S(2)}) collective-permute-start(bf16[4,32,2048]{2,1,0:T(8,128)(2,1)S(1)} %get-tuple-element.60), channel_id=1, source_target_pairs={{0,64},{8,72},{16,80},{24,88},{32,96},{40,104},{48,112},{56,120},{... | collective-permute-start | bytes 1572872 | tf_op jit(solution)/shard_map/ppermute | solution.py:60
  8.2 22.9 %collective-permute-start.14 = (bf16[4,32,2048]{2,1,0:T(8,128)(2,1)S(1)}, bf16[4,32,2048]{2,1,0:T(8,128)(2,1)S(1)}, u32[]{:S(2)}, u32[]{:S(2)}) collective-permute-start(bf16[4,32,2048]{2,1,0:T(8,128)(2,1)S(1)} %get-tuple-element.61), channel_id=1, source_target_pairs={{0,96},{8,104},{16,112},{24,120},{32,0},{40,8},{48,16},{56,24},{64... | collective-permute-start | bytes 1572872 | tf_op jit(solution)/shard_map/ppermute | solution.py:60
  9.6 25.8 %collective-permute-start.15 = (bf16[4,32,2048]{2,1,0:T(8,128)(2,1)S(1)}, bf16[4,32,2048]{2,1,0:T(8,128)(2,1)S(1)}, u32[]{:S(2)}, u32[]{:S(2)}) collective-permute-start(bf16[4,32,2048]{2,1,0:T(8,128)(2,1)S(1)} %get-tuple-element.63), channel_id=1, source_target_pairs={{0,8},{8,16},{16,24},{24,0},{32,40},{40,48},{48,56},{56,32},{64,72... | collective-permute-start | bytes 1572872 | tf_op jit(solution)/shard_map/ppermute | solution.py:60
  11.0 26.8 %collective-permute-start.16 = (bf16[4,32,2048]{2,1,0:T(8,128)(2,1)S(1)}, bf16[4,32,2048]{2,1,0:T(8,128)(2,1)S(1)}, u32[]{:S(2)}, u32[]{:S(2)}) collective-permute-start(bf16[4,32,2048]{2,1,0:T(8,128)(2,1)S(1)} %get-tuple-element.64), channel_id=1, source_target_pairs={{0,16},{8,24},{16,0},{24,8},{32,48},{40,56},{48,32},{56,40},{64,80... | collective-permute-start | bytes 1572872 | tf_op jit(solution)/shard_map/ppermute | solution.py:60
  18.7 19.2 %collective-permute-start.17 = (bf16[4,32,2048]{2,1,0:T(8,128)(2,1)S(1)}, bf16[4,32,2048]{2,1,0:T(8,128)(2,1)S(1)}, u32[]{:S(2)}, u32[]{:S(2)}) collective-permute-start(bf16[4,32,2048]{2,1,0:T(8,128)(2,1)S(1)} %get-tuple-element.65), channel_id=1, source_target_pairs={{0,24},{8,0},{16,8},{24,16},{32,56},{40,32},{48,40},{56,48},{64,88... | collective-permute-start | bytes 1572872 | tf_op jit(solution)/shard_map/ppermute | solution.py:60
  31.1 25.3 %collective-permute-start = (bf16[4,32,2048]{2,1,0:T(8,128)(2,1)S(1)}, bf16[4,32,2048]{2,1,0:T(8,128)(2,1)S(1)}, u32[]{:S(2)}, u32[]{:S(2)}) collective-permute-start(bf16[4,32,2048]{2,1,0:T(8,128)(2,1)S(1)} %get-tuple-element.45), channel_id=1, source_target_pairs={{0,32},{8,40},{16,48},{24,56},{32,64},{40,72},{48,80},{56,88},{64,... | collective-permute-start | bytes 1572872 | tf_op jit(solution)/shard_map/ppermute | solution.py:60
  31.1 28.2 %collective-permute-start.1 = (bf16[4,32,2048]{2,1,0:T(8,128)(2,1)S(1)}, bf16[4,32,2048]{2,1,0:T(8,128)(2,1)S(1)}, u32[]{:S(2)}, u32[]{:S(2)}) collective-permute-start(bf16[4,32,2048]{2,1,0:T(8,128)(2,1)S(1)} %get-tuple-element.46), channel_id=1, source_target_pairs={{0,64},{8,72},{16,80},{24,88},{32,96},{40,104},{48,112},{56,120},{... | collective-permute-start | bytes 1572872 | tf_op jit(solution)/shard_map/ppermute | solution.py:60
  35.3 24.1 %collective-permute-start.2 = (bf16[4,32,2048]{2,1,0:T(8,128)(2,1)S(1)}, bf16[4,32,2048]{2,1,0:T(8,128)(2,1)S(1)}, u32[]{:S(2)}, u32[]{:S(2)}) collective-permute-start(bf16[4,32,2048]{2,1,0:T(8,128)(2,1)S(1)} %get-tuple-element.47), channel_id=1, source_target_pairs={{0,96},{8,104},{16,112},{24,120},{32,0},{40,8},{48,16},{56,24},{64... | collective-permute-start | bytes 1572872 | tf_op jit(solution)/shard_map/ppermute | solution.py:60
  37.9 23.8 %collective-permute-start.3 = (bf16[4,32,2048]{2,1,0:T(8,128)(2,1)S(1)}, bf16[4,32,2048]{2,1,0:T(8,128)(2,1)S(1)}, u32[]{:S(2)}, u32[]{:S(2)}) collective-permute-start(bf16[4,32,2048]{2,1,0:T(8,128)(2,1)S(1)} %get-tuple-element.49), channel_id=1, source_target_pairs={{0,8},{8,16},{16,24},{24,0},{32,40},{40,48},{48,56},{56,32},{64,72... | collective-permute-start | bytes 1572872 | tf_op jit(solution)/shard_map/ppermute | solution.py:60
  37.9 24.9 %collective-permute-start.4 = (bf16[4,32,2048]{2,1,0:T(8,128)(2,1)S(1)}, bf16[4,32,2048]{2,1,0:T(8,128)(2,1)S(1)}, u32[]{:S(2)}, u32[]{:S(2)}) collective-permute-start(bf16[4,32,2048]{2,1,0:T(8,128)(2,1)S(1)} %get-tuple-element.50), channel_id=1, source_target_pairs={{0,16},{8,24},{16,0},{24,8},{32,48},{40,56},{48,32},{56,40},{64,80... | collective-permute-start | bytes 1572872 | tf_op jit(solution)/shard_map/ppermute | solution.py:60
  56.3 26.2 %collective-permute-start.5 = (bf16[4,32,2048]{2,1,0:T(8,128)(2,1)S(1)}, bf16[4,32,2048]{2,1,0:T(8,128)(2,1)S(1)}, u32[]{:S(2)}, u32[]{:S(2)}) collective-permute-start(bf16[4,32,2048]{2,1,0:T(8,128)(2,1)S(1)} %get-tuple-element.51), channel_id=1, source_target_pairs={{0,24},{8,0},{16,8},{24,16},{32,56},{40,32},{48,40},{56,48},{64,88... | collective-permute-start | bytes 1572872 | tf_op jit(solution)/shard_map/ppermute | solution.py:60
  59.3 24.6 %collective-permute-start.18 = (bf16[4,32,2048]{2,1,0:T(8,128)(2,1)S(1)}, bf16[4,32,2048]{2,1,0:T(8,128)(2,1)S(1)}, u32[]{:S(2)}, u32[]{:S(2)}) collective-permute-start(bf16[4,32,2048]{2,1,0:T(8,128)(2,1)S(1)} %get-tuple-element.66), channel_id=1, source_target_pairs={{0,8},{8,16},{16,24},{24,0},{32,40},{40,48},{48,56},{56,32},{64,72... | collective-permute-start | bytes 1572872 | tf_op jit(solution)/shard_map/ppermute | solution.py:60
  59.4 24.6 %collective-permute-start.19 = (bf16[4,32,2048]{2,1,0:T(8,128)(2,1)S(1)}, bf16[4,32,2048]{2,1,0:T(8,128)(2,1)S(1)}, u32[]{:S(2)}, u32[]{:S(2)}) collective-permute-start(bf16[4,32,2048]{2,1,0:T(8,128)(2,1)S(1)} %get-tuple-element.67), channel_id=1, source_target_pairs={{0,16},{8,24},{16,0},{24,8},{32,48},{40,56},{48,32},{56,40},{64,80... | collective-permute-start | bytes 1572872 | tf_op jit(solution)/shard_map/ppermute | solution.py:60
  61.7 29.4 %collective-permute-start.20 = (bf16[4,32,2048]{2,1,0:T(8,128)(2,1)S(1)}, bf16[4,32,2048]{2,1,0:T(8,128)(2,1)S(1)}, u32[]{:S(2)}, u32[]{:S(2)}) collective-permute-start(bf16[4,32,2048]{2,1,0:T(8,128)(2,1)S(1)} %get-tuple-element.68), channel_id=1, source_target_pairs={{0,24},{8,0},{16,8},{24,16},{32,56},{40,32},{48,40},{56,48},{64,88... | collective-permute-start | bytes 1572872 | tf_op jit(solution)/shard_map/ppermute | solution.py:60
  62.8 28.2 %collective-permute-start.21 = (bf16[4,32,2048]{2,1,0:T(8,128)(2,1)S(1)}, bf16[4,32,2048]{2,1,0:T(8,128)(2,1)S(1)}, u32[]{:S(2)}, u32[]{:S(2)}) collective-permute-start(bf16[4,32,2048]{2,1,0:T(8,128)(2,1)S(1)} %get-tuple-element.69), channel_id=1, source_target_pairs={{0,32},{8,40},{16,48},{24,56},{32,64},{40,72},{48,80},{56,88},{64,... | collective-permute-start | bytes 1572872 | tf_op jit(solution)/shard_map/ppermute | solution.py:60
  82.5 15.2 %collective-permute-start.22 = (bf16[4,32,2048]{2,1,0:T(8,128)(2,1)S(1)}, bf16[4,32,2048]{2,1,0:T(8,128)(2,1)S(1)}, u32[]{:S(2)}, u32[]{:S(2)}) collective-permute-start(bf16[4,32,2048]{2,1,0:T(8,128)(2,1)S(1)} %get-tuple-element.70), channel_id=1, source_target_pairs={{0,64},{8,72},{16,80},{24,88},{32,96},{40,104},{48,112},{56,120},{... | collective-permute-start | bytes 1572872 | tf_op jit(solution)/shard_map/ppermute | solution.py:60
  84.0 18.2 %collective-permute-start.23 = (bf16[4,32,2048]{2,1,0:T(8,128)(2,1)S(1)}, bf16[4,32,2048]{2,1,0:T(8,128)(2,1)S(1)}, u32[]{:S(2)}, u32[]{:S(2)}) collective-permute-start(bf16[4,32,2048]{2,1,0:T(8,128)(2,1)S(1)} %get-tuple-element.71), channel_id=1, source_target_pairs={{0,96},{8,104},{16,112},{24,120},{32,0},{40,8},{48,16},{56,24},{64... | collective-permute-start | bytes 1572872 | tf_op jit(solution)/shard_map/ppermute | solution.py:60
  84.0 29.4 %collective-permute-start.9 = (bf16[4,32,2048]{2,1,0:T(8,128)(2,1)S(1)}, bf16[4,32,2048]{2,1,0:T(8,128)(2,1)S(1)}, u32[]{:S(2)}, u32[]{:S(2)}) collective-permute-start(bf16[4,32,2048]{2,1,0:T(8,128)(2,1)S(1)} %get-tuple-element.55), channel_id=1, source_target_pairs={{0,32},{8,40},{16,48},{24,56},{32,64},{40,72},{48,80},{56,88},{64,... | collective-permute-start | bytes 1572872 | tf_op jit(solution)/shard_map/ppermute | solution.py:60
  91.0 24.7 %collective-permute-start.10 = (bf16[4,32,2048]{2,1,0:T(8,128)(2,1)S(1)}, bf16[4,32,2048]{2,1,0:T(8,128)(2,1)S(1)}, u32[]{:S(2)}, u32[]{:S(2)}) collective-permute-start(bf16[4,32,2048]{2,1,0:T(8,128)(2,1)S(1)} %get-tuple-element.56), channel_id=1, source_target_pairs={{0,64},{8,72},{16,80},{24,88},{32,96},{40,104},{48,112},{56,120},{... | collective-permute-start | bytes 1572872 | tf_op jit(solution)/shard_map/ppermute | solution.py:60
  91.0 24.7 %collective-permute-start.11 = (bf16[4,32,2048]{2,1,0:T(8,128)(2,1)S(1)}, bf16[4,32,2048]{2,1,0:T(8,128)(2,1)S(1)}, u32[]{:S(2)}, u32[]{:S(2)}) collective-permute-start(bf16[4,32,2048]{2,1,0:T(8,128)(2,1)S(1)} %get-tuple-element.57), channel_id=1, source_target_pairs={{0,96},{8,104},{16,112},{24,120},{32,0},{40,8},{48,16},{56,24},{64... | collective-permute-start | bytes 1572872 | tf_op jit(solution)/shard_map/ppermute | solution.py:60
  97.7 19.6 %collective-permute-start.6 = (bf16[4,32,2048]{2,1,0:T(8,128)(2,1)S(1)}, bf16[4,32,2048]{2,1,0:T(8,128)(2,1)S(1)}, u32[]{:S(2)}, u32[]{:S(2)}) collective-permute-start(bf16[4,32,2048]{2,1,0:T(8,128)(2,1)S(1)} %get-tuple-element.52), channel_id=1, source_target_pairs={{0,8},{8,16},{16,24},{24,0},{32,40},{40,48},{48,56},{56,32},{64,72... | collective-permute-start | bytes 1572872 | tf_op jit(solution)/shard_map/ppermute | solution.py:60
  102.1 15.2 %collective-permute-start.7 = (bf16[4,32,2048]{2,1,0:T(8,128)(2,1)S(1)}, bf16[4,32,2048]{2,1,0:T(8,128)(2,1)S(1)}, u32[]{:S(2)}, u32[]{:S(2)}) collective-permute-start(bf16[4,32,2048]{2,1,0:T(8,128)(2,1)S(1)} %get-tuple-element.53), channel_id=1, source_target_pairs={{0,16},{8,24},{16,0},{24,8},{32,48},{40,56},{48,32},{56,40},{64,80... | collective-permute-start | bytes 1572872 | tf_op jit(solution)/shard_map/ppermute | solution.py:60
  113.3 11.1 %collective-permute-start.8 = (bf16[4,32,2048]{2,1,0:T(8,128)(2,1)S(1)}, bf16[4,32,2048]{2,1,0:T(8,128)(2,1)S(1)}, u32[]{:S(2)}, u32[]{:S(2)}) collective-permute-start(bf16[4,32,2048]{2,1,0:T(8,128)(2,1)S(1)} %get-tuple-element.54), channel_id=1, source_target_pairs={{0,24},{8,0},{16,8},{24,16},{32,56},{40,32},{48,40},{56,48},{64,88... | collective-permute-start | bytes 1572872 | tf_op jit(solution)/shard_map/ppermute | solution.py:60
  115.7 8.7 %copy-start = (f32[512,64]{0,1:T(8,128)S(1)}, f32[512,64]{0,1:T(8,128)}, u32[]{:S(2)}) copy-start(f32[512,64]{0,1:T(8,128)} %param.3) | copy-start | bytes 393220

commit v4 on v3

--- a/solution.py
+++ b/solution.py
@@ -5,8 +5,8 @@
 from jax.experimental import pallas as pl
 from jax.experimental.pallas import tpu as pltpu
 
-HIGH = lax.Precision.HIGHEST
 F32 = jnp.float32
+CUTS = {0: 1, 2: 2}
 BF16 = jnp.bfloat16
 VM = pl.BlockSpec(memory_space=pltpu.VMEM)
 ANY = pl.BlockSpec(memory_space=pl.ANY)
@@ -15,6 +15,19 @@
 def nt(a, b, precision=None):
     return lax.dot_general(a, b, (((1,), (1,)), ((), ())), precision=precision,
                            preferred_element_type=F32)
+
+
+def nn(a, b):
+    return jnp.dot(a, b, preferred_element_type=F32)
+
+
+def cut3(v):
+    terms = []
+    for _ in range(3):
+        t = v.astype(BF16)
+        terms.append(t)
+        v = v - t.astype(F32)
+    return terms
 
 
 def place():
@@ -51,6 +64,32 @@
     return list(outs[:4]), list(outs[4:])
 
 
+def fetch_split_kernel(first, x_ref, *refs):
+    outs, (buf, sem) = refs[:8], refs[8:]
+    loads = [pltpu.make_async_copy(x_ref.at[first + k], buf.at[k], sem.at[k]) for k in range(2)]
+    for c in loads:
+        c.start()
+    for c in loads:
+        c.wait()
+    split_kernel(buf, *outs)
+
+
+def fetch_split_pair(fields, first, parts):
+    _, m, n = fields.shape
+    out = jax.ShapeDtypeStruct((4, m, n // parts), fields.dtype)
+    outs = pl.pallas_call(
+        lambda *r: fetch_split_kernel(first, *r),
+        in_specs=[ANY],
+        out_specs=[VM] * 8,
+        out_shape=[out] * 8,
+        scratch_shapes=[pltpu.VMEM((2, m, n), fields.dtype), pltpu.SemaphoreType.DMA((2,))],
+        compiler_params=pltpu.CompilerParams(vmem_limit_bytes=50 << 20),
+        cost_estimate=pl.CostEstimate(flops=0, transcendentals=0, bytes_accessed=8 * m * n),
+        name="fetch_split",
+    )(fields)
+    return list(outs[:4]), list(outs[4:])
+
+
 def shift(v, along, d):
     step = 1 if along == "x" else 4
     pairs = []
@@ -60,68 +99,87 @@
     return lax.ppermute(v, "gx", pairs)
 
 
-def regroup_kernel(*refs):
+def regroup_kernel(cuts, *refs):
+    outs = list(refs[8:])
     for k in range(2):
-        got, out = refs[4 * k:4 * k + 4], refs[8 + 3 * k:11 + 3 * k]
-        for q in range(1, 4):
-            for d in range(4):
-                out[q - 1][d] = got[d][q]
-
-
-def regroup(one, two):
-    out = jax.ShapeDtypeStruct(one[0].shape, one[0].dtype)
+        got = refs[4 * k:4 * k + 4]
+        w = got[0].shape[-1] // cuts
+        for h in range(cuts):
+            for q in range(1, 4):
+                out = outs.pop(0)
+                for d in range(4):
+                    out[d] = got[d][q, :, h * w:(h + 1) * w]
+
+
+def regroup(one, two, cuts):
+    n, m, w = one[0].shape
+    out = jax.ShapeDtypeStruct((n, m, w // cuts), one[0].dtype)
     outs = pl.pallas_call(
-        regroup_kernel,
+        lambda *r: regroup_kernel(cuts, *r),
         in_specs=[VM] * 8,
-        out_specs=[VM] * 6,
-        out_shape=[out] * 6,
+        out_specs=[VM] * (6 * cuts),
+        out_shape=[out] * (6 * cuts),
         compiler_params=pltpu.CompilerParams(vmem_limit_bytes=6 << 20),
-        cost_estimate=pl.CostEstimate(flops=0, transcendentals=0, bytes_accessed=4 * out.size),
+        cost_estimate=pl.CostEstimate(flops=0, transcendentals=0, bytes_accessed=4 * one[0].size),
         name="regroup",
     )(*one, *two)
-    return outs[:3], outs[3:]
-
-
-def gram_kernel(first, scale, *refs):
-    blocks, rest = refs[:7], list(refs[7:])
-    acc = rest.pop(0) if len(rest) > 2 else None
-    t_ref = rest.pop(0) if len(rest) > 2 else None
-    p_ref, o_ref = rest
-    parts, m, w = p_ref.shape
+    return [[outs[3 * (cuts * k + h):3 * (cuts * k + h) + 3] for k in range(2)] for h in range(cuts)]
+
+
+def gram_kernel(cut, scale, *refs):
+    blocks, rest = (refs[:7], refs[7:14]), list(refs[14:])
+    acc = rest.pop(0) if len(rest) > 3 else None
+    t_ref = rest.pop(0) if len(rest) > 3 else None
+    p_refs, o_ref = rest[:2], rest[2]
+    parts, m, w = p_refs[0].shape
     x, y = place()
-    for d1 in range(4):
-        for d2 in range(4):
-            g = member(x - d1, y - d2) if first == "x" else member(x - d2, y - d1)
-            p_ref[g] = blocks[d1][0] if d2 == 0 else blocks[3 + d2][d1]
     h = parts * m // 2
-    top = p_ref[:parts // 2].reshape(h, w)
-    low = p_ref[parts // 2:].reshape(h, w)
-    gram = [nt(p, q) for p, q in ((top, top), (top, low), (low, low))]
-    if acc is not None:
-        gram = [g + acc[k] for k, g in enumerate(gram)]
+    gram = None if acc is None else [acc[k] for k in range(3)]
+    for k in range(2):
+        for d1 in range(4):
+            for d2 in range(4):
+                g = member(x - d2, y - d1) if k else member(x - d1, y - d2)
+                if d2 == 0:
+                    p_refs[k][g] = blocks[k][d1][0, :, cut * w:(cut + 1) * w]
+                else:
+                    p_refs[k][g] = blocks[k][3 + d2][d1]
+    for k in range(2):
+        top = p_refs[k][:parts // 2].reshape(h, w)
+        low = p_refs[k][parts // 2:].reshape(h, w)
+        more = [nt(p, q) for p, q in ((top, top), (top, low), (low, low))]
+        gram = more if gram is None else [p + q for p, q in zip(gram, more)]
     if t_ref is None:
         for k in range(3):
             o_ref[k] = gram[k]
         return
-    gram = jnp.concatenate([jnp.concatenate(gram[:2], axis=1),
-                            jnp.concatenate([gram[1].T, gram[2]], axis=1)], axis=0)
-    sk = jnp.dot(t_ref[...], gram, precision=HIGH, preferred_element_type=F32) * scale
+    terms = cut3(t_ref[...])
+    one, two = (jnp.concatenate([t[:, k * h:(k + 1) * h] for t in terms], axis=0) for k in range(2))
+    (top, mid, low) = (cut3(g) for g in gram)
+
+    def times(t, g, dot):
+        r = dot(t, g[0]), dot(t[:128], g[1]), dot(t[:64], g[2])
+        return (r[0][128:] + r[1][64:] + r[2]) + (r[0][64:128] + r[1][:64]) + r[0][:64]
+
+    left = times(one, top, nn) + times(two, mid, nt)
+    right = times(one, mid, nn) + times(two, low, nn)
+    sk = jnp.concatenate([left, right], axis=1) * scale
     for c in range(4):
         o_ref[c * 64:(c + 1) * 64, :] = sk[:, c * 128:(c + 1) * 128]
 
 
-def add_gram(first, blocks, acc=None, test_t=None, scale=1.0):
-    _, m, w = blocks[0].shape
+def add_gram(blocks, cut, acc=None, test_t=None, scale=1.0):
+    _, m, w = blocks[-1].shape
     args = list(blocks) + [v for v in (acc, test_t) if v is not None]
     shape = (3, 256, 256) if test_t is None else (256, 128)
+    fibres = jax.ShapeDtypeStruct((16, m, w), BF16)
     return pl.pallas_call(
-        lambda *r: gram_kernel(first, scale, *r),
+        lambda *r: gram_kernel(cut, scale, *r),
         in_specs=[VM] * len(args),
-        out_specs=[VM, VM],
-        out_shape=[jax.ShapeDtypeStruct((16, m, w), BF16), jax.ShapeDtypeStruct(shape, F32)],
+        out_specs=[VM] * 3,
+        out_shape=[fibres, fibres, jax.ShapeDtypeStruct(shape, F32)],
         compiler_params=pltpu.CompilerParams(vmem_limit_bytes=16 << 20),
-        cost_estimate=pl.CostEstimate(flops=3 * 2 * 256 * 256 * w, transcendentals=0,
-                                      bytes_accessed=16 * m * w * 4),
+        cost_estimate=pl.CostEstimate(flops=6 * 2 * 256 * 256 * w, transcendentals=0,
+                                      bytes_accessed=32 * m * w * 4),
         name="gram",
     )(*args)
 
@@ -177,18 +235,33 @@
 
 
 def orthonormal_t(yt, step):
-    zero = jnp.zeros_like(yt)
-    aug = nt(yt, jnp.concatenate([zero, yt], axis=0), HIGH)
+    n = yt.shape[0]
+    terms = cut3(yt)
+    tall = jnp.concatenate(terms, axis=0)
+    nine = nt(tall, jnp.concatenate([tall, jnp.zeros_like(terms[0])], axis=0))
+    rows = (nine[2 * n:] + nine[n:2 * n]) + nine[:n]
+    near, far = rows[:, :2 * n], rows[:, 2 * n:]
+    aug = (far + pltpu.roll(far, n, 1)) + (near + pltpu.roll(near, n, 1))
     i = lax.broadcasted_iota(jnp.int32, aug.shape, 0)
     j = lax.broadcasted_iota(jnp.int32, aug.shape, 1)
-    aug = jnp.where(i == j, 1.0, aug)
-    return jnp.dot(inverse_lower(aug, step), yt, precision=HIGH, preferred_element_type=F32)
+    aug = jnp.where(j < n, (i == j).astype(F32), aug)
+    inv = cut3(inverse_lower(aug, step))
+    tall = jnp.concatenate(inv, axis=0)
+    r = nn(tall, terms[0]), nn(tall[:2 * n], terms[1]), nn(tall[:n], terms[2])
+    return (r[0][2 * n:] + r[1][n:] + r[2]) + (r[0][n:2 * n] + r[1][:n]) + r[0][:n]
+
+
+def cells_of(x_refs, k, at):
+    if k < 2:
+        return x_refs[k], at
+    w = x_refs[2].shape[-1]
+    return x_refs[2 + k - 2 + 2 * (at // w)], at % w
 
 
 def core_kernel(y_ref, *refs):
     x_refs, (f_ref, o_ref) = refs[:-2], refs[-2:]
-    s = len(x_refs)
-    parts, m, w = x_refs[0].shape
+    _, _, s, w = o_ref.shape
+    parts, m, _ = x_refs[0].shape
     yt = jnp.concatenate([y_ref[c * 64:(c + 1) * 64, :] for c in range(4)], axis=1)
     ft = orthonormal_t(orthonormal_t(yt, 8), 8)
     f_ref[...] = ft
@@ -201,18 +274,18 @@
     for c in range(w // step):
         acc = None
         for k in range(s):
-            x = x_refs[k][:, :, c * step:(c + 1) * step].reshape(parts * m, step)
+            x_ref, at = cells_of(x_refs, k, c * step)
+            x = x_ref[:, :, at:at + step].reshape(parts * m, step)
             t = jnp.dot(wide[k], x, preferred_element_type=F32)
             acc = t if acc is None else acc + t
         o_ref[:, :, :, c * step:(c + 1) * step] = acc.astype(BF16).reshape(o_ref.shape[:3] + (step,))
 
 
-def core_blocks(full, pieces):
-    s = len(pieces)
+def core_blocks(full, pieces, s):
     parts, _, w = pieces[0].shape
     return pl.pallas_call(
         core_kernel,
-        in_specs=[VM] * (1 + s),
+        in_specs=[VM] * (1 + len(pieces)),
         out_specs=[VM, VM],
         out_shape=[jax.ShapeDtypeStruct((64, 512), F32),
                    jax.ShapeDtypeStruct((parts, 64 // parts, s, w), BF16)],
@@ -251,33 +324,31 @@
     scale = 1.0 / (s * n * lax.axis_size("yz"))
     order = ("x", "y", "x", "y")
     near = [None] * s
-    for k in (0, 2):
-        if k:
-            fields, near[0][0] = lax.optimization_barrier((fields, near[0][0]))
-        near[k], near[k + 1] = split_pair(fields[k:k + 2], parts)
+    near[0], near[1] = split_pair(fields[:2], parts)
+    near[2], near[3] = fetch_split_pair(fields, 2, parts)
     for k in (0, 2):
         far = [[near[k + i][0]] + [None] * 3 for i in range(2)]
         for d in (1, 3, 2):
             for i in range(2):
                 far[i][d] = shift(near[k + i][d], order[k + i], d)
         near[k], near[k + 1] = far
-    blocks = [None] * s
+    blocks = {}
     for k in (0, 2):
-        sent = regroup(near[k], near[k + 1])
-        rest = [[None] * 3, [None] * 3]
-        for d in (1, 3, 2):
-            for i in range(2):
-                rest[i][d - 1] = shift(sent[i][d - 1], order[1 - i], d)
-        for i in range(2):
-            blocks[k + i] = list(near[k + i]) + rest[i]
-    pieces = [None] * s
-    part = None
-    for k in range(s):
-        pieces[k], part = add_gram(order[k], blocks[k], part, test_matrix.T if k == s - 1 else None, scale)
+        for h, sent in enumerate(regroup(near[k], near[k + 1], CUTS[k])):
+            rest = [[None] * 3, [None] * 3]
+            for d in (1, 3, 2):
+                for i in range(2):
+                    rest[i][d - 1] = shift(sent[i][d - 1], order[1 - i], d)
+            blocks[k, h] = near[k] + rest[0] + near[k + 1] + rest[1]
+    pieces, part = [], None
+    for (k, h), block in blocks.items():
+        last = (k, h) == (2, CUTS[2] - 1)
+        *more, part = add_gram(block, h, part, test_matrix.T if last else None, scale)
+        pieces += more
     part = lax.all_to_all(part.reshape(128, 2, 128), axes, split_axis=0, concat_axis=0, tiled=True)
     part = total(part.reshape(256, 128))
     full = lax.all_to_all(part.reshape(128, 2, 128), axes, split_axis=0, concat_axis=0, tiled=True)
-    ft, core = core_blocks(full.reshape(256, 128), pieces)
+    ft, core = core_blocks(full.reshape(256, 128), pieces, s)
     core = lax.all_to_all(core, "gx", split_axis=0, concat_axis=0, tiled=True)
     return (ft.T, merge_cells(core))
 

time: 189 us -> 200 us (1.058)
  starting transfers between devices: 31.5 us -> 64.8 us
  waiting for transfers between devices: 84.8 us -> 56.4 us
  blocking collectives: 52.7 us -> 57.1 us
  Pallas kernels: 15.6 us -> 17.9 us
    ppermute x24 -> x30, starting transfers between devices: 31.5 us -> 64.8 us  [shift(): return lax.ppermute(v, 'gx', pairs)]
    ppermute x24 -> x30, waiting for transfers between devices: 84.8 us -> 56.4 us  [shift(): return lax.ppermute(v, 'gx', pairs)]
    all_to_all x2, blocking collectives: 32.7 us -> 37.1 us  [body(): lax.all_to_all(part.reshape(128, 2, 128), axes, split_axis=0, concat_axis...]
    pallas_call x7, Pallas kernels: 13.9 us -> 16.5 us  [the longest x1 7.69 us: core_blocks(): pl.pallas_call(core_kernel, in_specs=[VM] * (1 + len(pieces)), out_specs=...]
  transfers between devices with their start and end apart: 24 -> 30, of which waited for: 11 -> 12; matrix products, arithmetic and copies ran while one was open for 0% -> 0% of each run, Pallas kernels for 2% -> 3%
where the time goes in v4:
time: 200 us
  starting transfers between devices  64.8 us (32%)
  blocking collectives  57.1 us (29%)
  waiting for transfers between devices  56.4 us (28%)
  Pallas kernels  17.9 us (9%)
  local copies, waits for them, and re-layouts  2.47 us (1%)
    ppermute x30, starting transfers between devices, shift(): return lax.ppermute(v, 'gx', pairs)  64.8 us
    ppermute x30, waiting for transfers between devices, shift(): return lax.ppermute(v, 'gx', pairs)  56.4 us
    all_to_all x2, blocking collectives, body(): lax.all_to_all(part.reshape(128, 2, 128), axes, split_axis=0, concat_axis...  37.1 us
    all_to_all x1, blocking collectives, body(): core = lax.all_to_all(core, 'gx', split_axis=0, concat_axis=0, tiled=True)  20 us
    pallas_call x1, Pallas kernels, core_blocks(): pl.pallas_call(core_kernel, in_specs=[VM] * (1 + len(pieces)), out_specs=...  7.69 us
    pallas_call x3, Pallas kernels, add_gram(): pl.pallas_call(lambda *r: gram_kernel(cut, scale, *r), in_specs=[VM] * le...  5.06 us
  transfers between devices with their start and end apart: 30, of which 12 were waited for; matrix products, arithmetic and copies ran while one was open for 0% of the time, Pallas kernels for 3%

profile of v4, /device:TPU:0, one launch (start us, length us, event | category | flops | bytes accessed | tf_op | source)
XLA Modules:
  0.0 199.6 jit_solution(17901891766008622685)
XLA Ops:
  0.6 2.5 %slice.3.x_ref = bf16[2,32,32768]{2,1,0:T(8,128)(2,1)S(1)} slice(bf16[4,32,32768]{2,1,0:T(8,128)(2,1)} %r_0_.1), slice={[0:2], [0:32], [0:32768]} | slice | bytes 8388608 | tf_op jit(solution)/shard_map/slice | solution.py:327
  3.4 1.7 collective-permute-start.18
  5.1 3.3 %fetch_split.1 = (bf16[4,32,2048]{2,1,0:T(8,128)(2,1)S(1)}, bf16[4,32,2048]{2,1,0:T(8,128)(2,1)S(1)}, bf16[4,32,2048]{2,1,0:T(8,128)(2,1)S(1)}, bf16[4,32,2048]{...) custom-call(bf16[4,32,32768]{2,1,0:T(8,128)(2,1)} %r_0_.1), custom_call_target="tpu_custom_call" | custom-call | bytes 8388608 | tf_op jit(solution)/shard_map/fetch_split/pallas_call | solution.py:80
  8.4 1.6 collective-permute-start
  9.9 1.6 collective-permute-start.1
  11.5 2.3 %collective-permute-start.2 = (bf16[4,32,2048]{2,1,0:T(8,128)(2,1)S(1)}, bf16[4,32,2048]{2,1,0:T(8,128)(2,1)S(1)}, u32[]{:S(2)}, u32[]{:S(2)}) collective-permute-start(bf16[4,32,2048]{2,1,0:T(8,128)(2,1)S(1)} %get-tuple-element.50), channel_id=1, source_target_pairs={{0,24},{8,0},{16,8},{24,16},{32,56},{40,32},{48,40},{56,48},{64,88... | collective-permute-start | bytes 1572872 | tf_op jit(solution)/shard_map/ppermute | solution.py:99
  13.8 1.6 collective-permute-start.3
  15.4 4.1 %collective-permute-done.18.r_1_ = bf16[4,32,2048]{2,1,0:T(8,128)(2,1)S(1)} collective-permute-done((bf16[4,32,2048]{2,1,0:T(8,128)(2,1)S(1)}, bf16[4,32,2048]{2,1,0:T(8,128)(2,1)S(1)}, u32[]{:S(2)}, u32[]{:S(2)}) %collective-permute-start.18) | collective-permute-done | bytes 524320 | tf_op jit(solution)/shard_map/ppermute | solution.py:99
  19.5 3.3 %collective-permute-start.4 = (bf16[4,32,2048]{2,1,0:T(8,128)(2,1)S(1)}, bf16[4,32,2048]{2,1,0:T(8,128)(2,1)S(1)}, u32[]{:S(2)}, u32[]{:S(2)}) collective-permute-start(bf16[4,32,2048]{2,1,0:T(8,128)(2,1)S(1)} %get-tuple-element.53), channel_id=1, source_target_pairs={{0,64},{8,72},{16,80},{24,88},{32,96},{40,104},{48,112},{56,120},{... | collective-permute-start | bytes 1572872 | tf_op jit(solution)/shard_map/ppermute | solution.py:99
  22.8 6.7 %collective-permute-done.r_1_ = bf16[4,32,2048]{2,1,0:T(8,128)(2,1)S(1)} collective-permute-done((bf16[4,32,2048]{2,1,0:T(8,128)(2,1)S(1)}, bf16[4,32,2048]{2,1,0:T(8,128)(2,1)S(1)}, u32[]{:S(2)}, u32[]{:S(2)}) %collective-permute-start) | collective-permute-done | bytes 524320 | tf_op jit(solution)/shard_map/ppermute | solution.py:99
  29.5 3.3 %collective-permute-start.5 = (bf16[4,32,2048]{2,1,0:T(8,128)(2,1)}, bf16[4,32,2048]{2,1,0:T(8,128)(2,1)S(1)}, u32[]{:S(2)}, u32[]{:S(2)}) collective-permute-start(bf16[4,32,2048]{2,1,0:T(8,128)(2,1)} %get-tuple-element.54), channel_id=1, source_target_pairs={{0,96},{8,104},{16,112},{24,120},{32,0},{40,8},{48,16},{56,24},{64... | collective-permute-start | bytes 1572872 | tf_op jit(solution)/shard_map/ppermute | solution.py:99
  32.8 9.1 %collective-permute-done.1.r_2_ = bf16[4,32,2048]{2,1,0:T(8,128)(2,1)S(1)} collective-permute-done((bf16[4,32,2048]{2,1,0:T(8,128)(2,1)S(1)}, bf16[4,32,2048]{2,1,0:T(8,128)(2,1)S(1)}, u32[]{:S(2)}, u32[]{:S(2)}) %collective-permute-start.1) | collective-permute-done | bytes 524320 | tf_op jit(solution)/shard_map/ppermute | solution.py:99
  41.9 0.8 collective-permute-start.19
  42.7 1.6 collective-permute-start.21
  44.4 2.9 %collective-permute-start.22 = (bf16[4,32,2048]{2,1,0:T(8,128)(2,1)S(1)}, bf16[4,32,2048]{2,1,0:T(8,128)(2,1)S(1)}, u32[]{:S(2)}, u32[]{:S(2)}) collective-permute-start(bf16[4,32,2048]{2,1,0:T(8,128)(2,1)S(1)} %get-tuple-element.73), channel_id=1, source_target_pairs={{0,64},{8,72},{16,80},{24,88},{32,96},{40,104},{48,112},{56,120},{... | collective-permute-start | bytes 1572872 | tf_op jit(solution)/shard_map/ppermute | solution.py:99
  47.3 1.3 collective-permute-start.23
  48.9 7.4 %collective-permute-done.19.r_2_ = bf16[4,32,2048]{2,1,0:T(8,128)(2,1)S(1)} collective-permute-done((bf16[4,32,2048]{2,1,0:T(8,128)(2,1)S(1)}, bf16[4,32,2048]{2,1,0:T(8,128)(2,1)S(1)}, u32[]{:S(2)}, u32[]{:S(2)}) %collective-permute-start.19) | collective-permute-done | bytes 524320 | tf_op jit(solution)/shard_map/ppermute | solution.py:99
  56.2 1.6 collective-permute-start.6
  57.8 1.6 collective-permute-start.12
  59.4 8.9 %collective-permute-start.13 = (bf16[4,32,1024]{2,1,0:T(8,128)(2,1)S(1)}, bf16[4,32,1024]{2,1,0:T(8,128)(2,1)S(1)}, u32[]{:S(2)}, u32[]{:S(2)}) collective-permute-start(bf16[4,32,1024]{2,1,0:T(8,128)(2,1)S(1)} %get-tuple-element.62), channel_id=1, source_target_pairs={{0,64},{8,72},{16,80},{24,88},{32,96},{40,104},{48,112},{56,120},{... | collective-permute-start | bytes 786440 | tf_op jit(solution)/shard_map/ppermute | solution.py:99
  68.3 3.0 %collective-permute-done.22.r_6_.r_9_ = bf16[4,32,2048]{2,1,0:T(8,128)(2,1)S(1)} collective-permute-done((bf16[4,32,2048]{2,1,0:T(8,128)(2,1)S(1)}, bf16[4,32,2048]{2,1,0:T(8,128)(2,1)S(1)}, u32[]{:S(2)}, u32[]{:S(2)}) %collective-permute-start.22) | collective-permute-done | bytes 524320 | tf_op jit(solution)/shard_map/ppermute | solution.py:99
  71.5 0.8 collective-permute-start.24
  72.3 2.5 %collective-permute-start.14 = (bf16[4,32,1024]{2,1,0:T(8,128)(2,1)S(1)}, bf16[4,32,1024]{2,1,0:T(8,128)(2,1)S(1)}, u32[]{:S(2)}, u32[]{:S(2)}) collective-permute-start(bf16[4,32,1024]{2,1,0:T(8,128)(2,1)S(1)} %get-tuple-element.63), channel_id=1, source_target_pairs={{0,96},{8,104},{16,112},{24,120},{32,0},{40,8},{48,16},{56,24},{64... | collective-permute-start | bytes 786440 | tf_op jit(solution)/shard_map/ppermute | solution.py:99
  74.9 2.8 %collective-permute-start.15 = (bf16[4,32,1024]{2,1,0:T(8,128)(2,1)S(1)}, bf16[4,32,1024]{2,1,0:T(8,128)(2,1)S(1)}, u32[]{:S(2)}, u32[]{:S(2)}) collective-permute-start(bf16[4,32,1024]{2,1,0:T(8,128)(2,1)S(1)} %get-tuple-element.64), channel_id=1, source_target_pairs={{0,8},{8,16},{16,24},{24,0},{32,40},{40,48},{48,56},{56,32},{64,72... | collective-permute-start | bytes 786440 | tf_op jit(solution)/shard_map/ppermute | solution.py:99
  77.6 5.0 %collective-permute-done.12.r_4_ = bf16[4,32,1024]{2,1,0:T(8,128)(2,1)S(1)} collective-permute-done((bf16[4,32,1024]{2,1,0:T(8,128)(2,1)S(1)}, bf16[4,32,1024]{2,1,0:T(8,128)(2,1)S(1)}, u32[]{:S(2)}, u32[]{:S(2)}) %collective-permute-start.12) | collective-permute-done | bytes 262176 | tf_op jit(solution)/shard_map/ppermute | solution.py:99
  82.6 1.6 collective-permute-start.16
  84.3 4.0 %collective-permute-done.13.r_5_ = bf16[4,32,1024]{2,1,0:T(8,128)(2,1)S(1)} collective-permute-done((bf16[4,32,1024]{2,1,0:T(8,128)(2,1)S(1)}, bf16[4,32,1024]{2,1,0:T(8,128)(2,1)S(1)}, u32[]{:S(2)}, u32[]{:S(2)}) %collective-permute-start.13) | collective-permute-done | bytes 262176 | tf_op jit(solution)/shard_map/ppermute | solution.py:99
  88.2 3.1 %collective-permute-start.17 = (bf16[4,32,1024]{2,1,0:T(8,128)(2,1)S(1)}, bf16[4,32,1024]{2,1,0:T(8,128)(2,1)S(1)}, u32[]{:S(2)}, u32[]{:S(2)}) collective-permute-start(bf16[4,32,1024]{2,1,0:T(8,128)(2,1)S(1)} %get-tuple-element.66), channel_id=1, source_target_pairs={{0,24},{8,0},{16,8},{24,16},{32,56},{40,32},{48,40},{56,48},{64,88... | collective-permute-start | bytes 786440 | tf_op jit(solution)/shard_map/ppermute | solution.py:99
  91.4 2.1 %collective-permute-start.25 = (bf16[4,32,2048]{2,1,0:T(8,128)(2,1)S(1)}, bf16[4,32,2048]{2,1,0:T(8,128)(2,1)S(1)}, u32[]{:S(2)}, u32[]{:S(2)}) collective-permute-start(bf16[4,32,2048]{2,1,0:T(8,128)(2,1)S(1)} %get-tuple-element.76), channel_id=1, source_target_pairs={{0,64},{8,72},{16,80},{24,88},{32,96},{40,104},{48,112},{56,120},{... | collective-permute-start | bytes 1572872 | tf_op jit(solution)/shard_map/ppermute | solution.py:99
  93.5 2.6 %collective-permute-start.27 = (bf16[4,32,2048]{2,1,0:T(8,128)(2,1)S(1)}, bf16[4,32,2048]{2,1,0:T(8,128)(2,1)S(1)}, u32[]{:S(2)}, u32[]{:S(2)}) collective-permute-start(bf16[4,32,2048]{2,1,0:T(8,128)(2,1)S(1)} %get-tuple-element.78), channel_id=1, source_target_pairs={{0,8},{8,16},{16,24},{24,0},{32,40},{40,48},{48,56},{56,32},{64,72... | collective-permute-start | bytes 1572872 | tf_op jit(solution)/shard_map/ppermute | solution.py:99
  96.1 5.9 %collective-permute-done.17.r_13_ = bf16[4,32,1024]{2,1,0:T(8,128)(2,1)S(1)} collective-permute-done((bf16[4,32,1024]{2,1,0:T(8,128)(2,1)S(1)}, bf16[4,32,1024]{2,1,0:T(8,128)(2,1)S(1)}, u32[]{:S(2)}, u32[]{:S(2)}) %collective-permute-start.17) | collective-permute-done | bytes 262176 | tf_op jit(solution)/shard_map/ppermute | solution.py:99
  102.0 2.7 %collective-permute-start.28 = (bf16[4,32,2048]{2,1,0:T(8,128)(2,1)S(1)}, bf16[4,32,2048]{2,1,0:T(8,128)(2,1)S(1)}, u32[]{:S(2)}, u32[]{:S(2)}) collective-permute-start(bf16[4,32,2048]{2,1,0:T(8,128)(2,1)S(1)} %get-tuple-element.79), channel_id=1, source_target_pairs={{0,16},{8,24},{16,0},{24,8},{32,48},{40,56},{48,32},{56,40},{64,80... | collective-permute-start | bytes 1572872 | tf_op jit(solution)/shard_map/ppermute | solution.py:99
  104.7 3.1 %collective-permute-start.29 = (bf16[4,32,2048]{2,1,0:T(8,128)(2,1)S(1)}, bf16[4,32,2048]{2,1,0:T(8,128)(2,1)S(1)}, u32[]{:S(2)}, u32[]{:S(2)}) collective-permute-start(bf16[4,32,2048]{2,1,0:T(8,128)(2,1)S(1)} %get-tuple-element.80), channel_id=1, source_target_pairs={{0,24},{8,0},{16,8},{24,16},{32,56},{40,32},{48,40},{56,48},{64,88... | collective-permute-start | bytes 1572872 | tf_op jit(solution)/shard_map/ppermute | solution.py:99
  107.8 0.6 collective-permute-done.25.r_5_
  108.4 3.6 %collective-permute-start.7 = (bf16[4,32,1024]{2,1,0:T(8,128)(2,1)S(1)}, bf16[4,32,1024]{2,1,0:T(8,128)(2,1)S(1)}, u32[]{:S(2)}, u32[]{:S(2)}) collective-permute-start(bf16[4,32,1024]{2,1,0:T(8,128)(2,1)S(1)} %get-tuple-element.56), channel_id=1, source_target_pairs={{0,64},{8,72},{16,80},{24,88},{32,96},{40,104},{48,112},{56,120},{... | collective-permute-start | bytes 786440 | tf_op jit(solution)/shard_map/ppermute | solution.py:99
  112.4 2.4 %collective-permute-done.27.r_11_ = bf16[4,32,2048]{2,1,0:T(8,128)(2,1)S(1)} collective-permute-done((bf16[4,32,2048]{2,1,0:T(8,128)(2,1)S(1)}, bf16[4,32,2048]{2,1,0:T(8,128)(2,1)S(1)}, u32[]{:S(2)}, u32[]{:S(2)}) %collective-permute-start.27) | collective-permute-done | bytes 524320 | tf_op jit(solution)/shard_map/ppermute | solution.py:99
  114.9 2.7 %collective-permute-start.10 = (bf16[4,32,1024]{2,1,0:T(8,128)(2,1)S(1)}, bf16[4,32,1024]{2,1,0:T(8,128)(2,1)S(1)}, u32[]{:S(2)}, u32[]{:S(2)}) collective-permute-start(bf16[4,32,1024]{2,1,0:T(8,128)(2,1)S(1)} %get-tuple-element.59), channel_id=1, source_target_pairs={{0,16},{8,24},{16,0},{24,8},{32,48},{40,56},{48,32},{56,40},{64,80... | collective-permute-start | bytes 786440 | tf_op jit(solution)/shard_map/ppermute | solution.py:99
  117.6 7.6 %collective-permute-done.29.r_13_ = bf16[4,32,2048]{2,1,0:T(8,128)(2,1)S(1)} collective-permute-done((bf16[4,32,2048]{2,1,0:T(8,128)(2,1)S(1)}, bf16[4,32,2048]{2,1,0:T(8,128)(2,1)S(1)}, u32[]{:S(2)}, u32[]{:S(2)}) %collective-permute-start.29) | collective-permute-done | bytes 524320 | tf_op jit(solution)/shard_map/ppermute | solution.py:99
  125.1 2.6 %collective-permute-start.11 = (bf16[4,32,1024]{2,1,0:T(8,128)(2,1)S(1)}, bf16[4,32,1024]{2,1,0:T(8,128)(2,1)S(1)}, u32[]{:S(2)}, u32[]{:S(2)}) collective-permute-start(bf16[4,32,1024]{2,1,0:T(8,128)(2,1)S(1)} %get-tuple-element.60), channel_id=1, source_target_pairs={{0,24},{8,0},{16,8},{24,16},{32,56},{40,32},{48,40},{56,48},{64,88... | collective-permute-start | bytes 786440 | tf_op jit(solution)/shard_map/ppermute | solution.py:99
  127.8 2.1 %gram.3 = (bf16[16,32,2048]{2,1,0:T(8,128)(2,1)S(1)}, bf16[16,32,2048]{2,1,0:T(8,128)(2,1)S(1)}, f32[3,256,256]{2,1,0:T(8,128)S(1)}) custom-call(bf16[4,32,2048]{2,1,0:T(8,128)(2,1)S(1)} %get-tuple-element.67.r_0_, bf16[4,32,2048]{2,1,0:T(8,128)(2,1)S(1)} %collective-permute-done.18.r_1_, bf16[4,32,2048]{2,1,0:T(8,128)(2,1)S(1)} %collective-permute-done.19.r_2_, ...), custom_call_target="tpu_custom_call" | custom-call | flops 1610612736 | bytes 8388608 | tf_op jit(solution)/shard_map/gram/pallas_call | solution.py:175
  129.9 1.1 gram.4
  131.1 0.6 collective-permute-done.11.r_13_
  131.7 1.8 gram.5
  133.5 22.9 %all_to_all.15 = f32[128,2,128]{2,1,0:T(2,128)S(1)} all-to-all(f32[128,2,128]{2,1,0:T(2,128)S(1)} %bitcast.10), channel_id=1, replica_groups=mesh['gx'=16,'yz'=8] {'gx','yz'}, dimensions={0} | all-to-all | bytes 262144 | tf_op jit(solution)/shard_map/all_to_all | solution.py:348
  156.5 14.2 %all_to_all.16 = f32[128,2,128]{2,1,0:T(2,128)S(1)} all-to-all(f32[128,2,128]{2,1,0:T(2,128)S(1)} %bitcast.8), channel_id=1, replica_groups=mesh['gx'=16,'yz'=8] {'gx','yz'}, dimensions={0} | all-to-all | bytes 262144 | tf_op jit(solution)/shard_map/all_to_all | solution.py:350
  170.7 7.7 %core.1 = (f32[64,512]{1,0:T(8,128)}, bf16[16,4,4,2048]{3,2,1,0:T(4,128)(2,1)S(1)}) custom-call(f32[256,128]{1,0:T(8,128)S(1)} %bitcast.6, bf16[16,32,2048]{2,1,0:T(8,128)(2,1)S(1)} %get-tuple-element.84.refs_0_, bf16[16,32,2048]{2,1,0:T(8,128)(2,1)S(1)} %get-tuple-element.85.refs_1_, bf16[16,32,1024]{2,1,0:T(8,128)(2,1)S(1)} %get-tuple-element.86.refs_2_, ...), custom_call_target="tpu_custom_call" | custom-call | tf_op jit(solution)/shard_map/core/pallas_call | solution.py:286
  178.3 20.0 %all_to_all.17.x_ref = bf16[16,4,4,2048]{3,2,1,0:T(4,128)(2,1)S(1)} all-to-all(bf16[16,4,4,2048]{3,2,1,0:T(4,128)(2,1)S(1)} %get-tuple-element.91), channel_id=1, replica_groups=mesh['gx'=16,'yz'=8] {'gx'}, dimensions={0} | all-to-all | bytes 2097152 | tf_op jit(solution)/shard_map/all_to_all | solution.py:352
  198.4 1.1 merge.1
  (28 shorter events, 1.2 us)
Async XLA Ops:
  3.4 16.1 %collective-permute-start.18 = (bf16[4,32,2048]{2,1,0:T(8,128)(2,1)S(1)}, bf16[4,32,2048]{2,1,0:T(8,128)(2,1)S(1)}, u32[]{:S(2)}, u32[]{:S(2)}) collective-permute-start(bf16[4,32,2048]{2,1,0:T(8,128)(2,1)S(1)} %get-tuple-element.68), channel_id=1, source_target_pairs={{0,8},{8,16},{16,24},{24,0},{32,40},{40,48},{48,56},{56,32},{64,72... | collective-permute-start | bytes 1572872 | tf_op jit(solution)/shard_map/ppermute | solution.py:99
  8.4 21.1 %collective-permute-start = (bf16[4,32,2048]{2,1,0:T(8,128)(2,1)S(1)}, bf16[4,32,2048]{2,1,0:T(8,128)(2,1)S(1)}, u32[]{:S(2)}, u32[]{:S(2)}) collective-permute-start(bf16[4,32,2048]{2,1,0:T(8,128)(2,1)S(1)} %get-tuple-element.48), channel_id=1, source_target_pairs={{0,8},{8,16},{16,24},{24,0},{32,40},{40,48},{48,56},{56,32},{64,72... | collective-permute-start | bytes 1572872 | tf_op jit(solution)/shard_map/ppermute | solution.py:99
  9.9 32.0 %collective-permute-start.1 = (bf16[4,32,2048]{2,1,0:T(8,128)(2,1)S(1)}, bf16[4,32,2048]{2,1,0:T(8,128)(2,1)S(1)}, u32[]{:S(2)}, u32[]{:S(2)}) collective-permute-start(bf16[4,32,2048]{2,1,0:T(8,128)(2,1)S(1)} %get-tuple-element.49), channel_id=1, source_target_pairs={{0,16},{8,24},{16,0},{24,8},{32,48},{40,56},{48,32},{56,40},{64,80... | collective-permute-start | bytes 1572872 | tf_op jit(solution)/shard_map/ppermute | solution.py:99
  11.5 31.2 %collective-permute-start.2 = (bf16[4,32,2048]{2,1,0:T(8,128)(2,1)S(1)}, bf16[4,32,2048]{2,1,0:T(8,128)(2,1)S(1)}, u32[]{:S(2)}, u32[]{:S(2)}) collective-permute-start(bf16[4,32,2048]{2,1,0:T(8,128)(2,1)S(1)} %get-tuple-element.50), channel_id=1, source_target_pairs={{0,24},{8,0},{16,8},{24,16},{32,56},{40,32},{48,40},{56,48},{64,88... | collective-permute-start | bytes 1572872 | tf_op jit(solution)/shard_map/ppermute | solution.py:99
  13.8 28.9 %collective-permute-start.3 = (bf16[4,32,2048]{2,1,0:T(8,128)(2,1)S(1)}, bf16[4,32,2048]{2,1,0:T(8,128)(2,1)S(1)}, u32[]{:S(2)}, u32[]{:S(2)}) collective-permute-start(bf16[4,32,2048]{2,1,0:T(8,128)(2,1)S(1)} %get-tuple-element.52), channel_id=1, source_target_pairs={{0,32},{8,40},{16,48},{24,56},{32,64},{40,72},{48,80},{56,88},{64,... | collective-permute-start | bytes 1572872 | tf_op jit(solution)/shard_map/ppermute | solution.py:99
  19.5 24.9 %collective-permute-start.4 = (bf16[4,32,2048]{2,1,0:T(8,128)(2,1)S(1)}, bf16[4,32,2048]{2,1,0:T(8,128)(2,1)S(1)}, u32[]{:S(2)}, u32[]{:S(2)}) collective-permute-start(bf16[4,32,2048]{2,1,0:T(8,128)(2,1)S(1)} %get-tuple-element.53), channel_id=1, source_target_pairs={{0,64},{8,72},{16,80},{24,88},{32,96},{40,104},{48,112},{56,120},{... | collective-permute-start | bytes 1572872 | tf_op jit(solution)/shard_map/ppermute | solution.py:99
  29.5 17.8 %collective-permute-start.5 = (bf16[4,32,2048]{2,1,0:T(8,128)(2,1)}, bf16[4,32,2048]{2,1,0:T(8,128)(2,1)S(1)}, u32[]{:S(2)}, u32[]{:S(2)}) collective-permute-start(bf16[4,32,2048]{2,1,0:T(8,128)(2,1)} %get-tuple-element.54), channel_id=1, source_target_pairs={{0,96},{8,104},{16,112},{24,120},{32,0},{40,8},{48,16},{56,24},{64... | collective-permute-start | bytes 1572872 | tf_op jit(solution)/shard_map/ppermute | solution.py:99
  41.9 14.3 %collective-permute-start.19 = (bf16[4,32,2048]{2,1,0:T(8,128)(2,1)S(1)}, bf16[4,32,2048]{2,1,0:T(8,128)(2,1)S(1)}, u32[]{:S(2)}, u32[]{:S(2)}) collective-permute-start(bf16[4,32,2048]{2,1,0:T(8,128)(2,1)S(1)} %get-tuple-element.69), channel_id=1, source_target_pairs={{0,16},{8,24},{16,0},{24,8},{32,48},{40,56},{48,32},{56,40},{64,80... | collective-permute-start | bytes 1572872 | tf_op jit(solution)/shard_map/ppermute | solution.py:99
  42.7 15.1 %collective-permute-start.20 = (bf16[4,32,2048]{2,1,0:T(8,128)(2,1)S(1)}, bf16[4,32,2048]{2,1,0:T(8,128)(2,1)S(1)}, u32[]{:S(2)}, u32[]{:S(2)}) collective-permute-start(bf16[4,32,2048]{2,1,0:T(8,128)(2,1)S(1)} %get-tuple-element.70), channel_id=1, source_target_pairs={{0,24},{8,0},{16,8},{24,16},{32,56},{40,32},{48,40},{56,48},{64,88... | collective-permute-start | bytes 1572872 | tf_op jit(solution)/shard_map/ppermute | solution.py:99
  42.7 16.6 %collective-permute-start.21 = (bf16[4,32,2048]{2,1,0:T(8,128)(2,1)S(1)}, bf16[4,32,2048]{2,1,0:T(8,128)(2,1)S(1)}, u32[]{:S(2)}, u32[]{:S(2)}) collective-permute-start(bf16[4,32,2048]{2,1,0:T(8,128)(2,1)S(1)} %get-tuple-element.72), channel_id=1, source_target_pairs={{0,32},{8,40},{16,48},{24,56},{32,64},{40,72},{48,80},{56,88},{64,... | collective-permute-start | bytes 1572872 | tf_op jit(solution)/shard_map/ppermute | solution.py:99
  44.4 26.9 %collective-permute-start.22 = (bf16[4,32,2048]{2,1,0:T(8,128)(2,1)S(1)}, bf16[4,32,2048]{2,1,0:T(8,128)(2,1)S(1)}, u32[]{:S(2)}, u32[]{:S(2)}) collective-permute-start(bf16[4,32,2048]{2,1,0:T(8,128)(2,1)S(1)} %get-tuple-element.73), channel_id=1, source_target_pairs={{0,64},{8,72},{16,80},{24,88},{32,96},{40,104},{48,112},{56,120},{... | collective-permute-start | bytes 1572872 | tf_op jit(solution)/shard_map/ppermute | solution.py:99
  47.3 24.0 %collective-permute-start.23 = (bf16[4,32,2048]{2,1,0:T(8,128)(2,1)S(1)}, bf16[4,32,2048]{2,1,0:T(8,128)(2,1)S(1)}, u32[]{:S(2)}, u32[]{:S(2)}) collective-permute-start(bf16[4,32,2048]{2,1,0:T(8,128)(2,1)S(1)} %get-tuple-element.74), channel_id=1, source_target_pairs={{0,96},{8,104},{16,112},{24,120},{32,0},{40,8},{48,16},{56,24},{64... | collective-permute-start | bytes 1572872 | tf_op jit(solution)/shard_map/ppermute | solution.py:99
  56.2 18.6 %collective-permute-start.6 = (bf16[4,32,1024]{2,1,0:T(8,128)(2,1)S(1)}, bf16[4,32,1024]{2,1,0:T(8,128)(2,1)S(1)}, u32[]{:S(2)}, u32[]{:S(2)}) collective-permute-start(bf16[4,32,1024]{2,1,0:T(8,128)(2,1)S(1)} %get-tuple-element.55), channel_id=1, source_target_pairs={{0,32},{8,40},{16,48},{24,56},{32,64},{40,72},{48,80},{56,88},{64,... | collective-permute-start | bytes 786440 | tf_op jit(solution)/shard_map/ppermute | solution.py:99
  57.8 24.8 %collective-permute-start.12 = (bf16[4,32,1024]{2,1,0:T(8,128)(2,1)S(1)}, bf16[4,32,1024]{2,1,0:T(8,128)(2,1)S(1)}, u32[]{:S(2)}, u32[]{:S(2)}) collective-permute-start(bf16[4,32,1024]{2,1,0:T(8,128)(2,1)S(1)} %get-tuple-element.61), channel_id=1, source_target_pairs={{0,32},{8,40},{16,48},{24,56},{32,64},{40,72},{48,80},{56,88},{64,... | collective-permute-start | bytes 786440 | tf_op jit(solution)/shard_map/ppermute | solution.py:99
  59.4 28.9 %collective-permute-start.13 = (bf16[4,32,1024]{2,1,0:T(8,128)(2,1)S(1)}, bf16[4,32,1024]{2,1,0:T(8,128)(2,1)S(1)}, u32[]{:S(2)}, u32[]{:S(2)}) collective-permute-start(bf16[4,32,1024]{2,1,0:T(8,128)(2,1)S(1)} %get-tuple-element.62), channel_id=1, source_target_pairs={{0,64},{8,72},{16,80},{24,88},{32,96},{40,104},{48,112},{56,120},{... | collective-permute-start | bytes 786440 | tf_op jit(solution)/shard_map/ppermute | solution.py:99
  71.5 33.2 %collective-permute-start.24 = (bf16[4,32,2048]{2,1,0:T(8,128)(2,1)S(1)}, bf16[4,32,2048]{2,1,0:T(8,128)(2,1)S(1)}, u32[]{:S(2)}, u32[]{:S(2)}) collective-permute-start(bf16[4,32,2048]{2,1,0:T(8,128)(2,1)S(1)} %get-tuple-element.75), channel_id=1, source_target_pairs={{0,32},{8,40},{16,48},{24,56},{32,64},{40,72},{48,80},{56,88},{64,... | collective-permute-start | bytes 1572872 | tf_op jit(solution)/shard_map/ppermute | solution.py:99
  72.3 19.1 %collective-permute-start.14 = (bf16[4,32,1024]{2,1,0:T(8,128)(2,1)S(1)}, bf16[4,32,1024]{2,1,0:T(8,128)(2,1)S(1)}, u32[]{:S(2)}, u32[]{:S(2)}) collective-permute-start(bf16[4,32,1024]{2,1,0:T(8,128)(2,1)S(1)} %get-tuple-element.63), channel_id=1, source_target_pairs={{0,96},{8,104},{16,112},{24,120},{32,0},{40,8},{48,16},{56,24},{64... | collective-permute-start | bytes 786440 | tf_op jit(solution)/shard_map/ppermute | solution.py:99
  74.9 18.7 %collective-permute-start.15 = (bf16[4,32,1024]{2,1,0:T(8,128)(2,1)S(1)}, bf16[4,32,1024]{2,1,0:T(8,128)(2,1)S(1)}, u32[]{:S(2)}, u32[]{:S(2)}) collective-permute-start(bf16[4,32,1024]{2,1,0:T(8,128)(2,1)S(1)} %get-tuple-element.64), channel_id=1, source_target_pairs={{0,8},{8,16},{16,24},{24,0},{32,40},{40,48},{48,56},{56,32},{64,72... | collective-permute-start | bytes 786440 | tf_op jit(solution)/shard_map/ppermute | solution.py:99
  82.6 10.9 %collective-permute-start.16 = (bf16[4,32,1024]{2,1,0:T(8,128)(2,1)S(1)}, bf16[4,32,1024]{2,1,0:T(8,128)(2,1)S(1)}, u32[]{:S(2)}, u32[]{:S(2)}) collective-permute-start(bf16[4,32,1024]{2,1,0:T(8,128)(2,1)S(1)} %get-tuple-element.65), channel_id=1, source_target_pairs={{0,16},{8,24},{16,0},{24,8},{32,48},{40,56},{48,32},{56,40},{64,80... | collective-permute-start | bytes 786440 | tf_op jit(solution)/shard_map/ppermute | solution.py:99
  88.2 13.8 %collective-permute-start.17 = (bf16[4,32,1024]{2,1,0:T(8,128)(2,1)S(1)}, bf16[4,32,1024]{2,1,0:T(8,128)(2,1)S(1)}, u32[]{:S(2)}, u32[]{:S(2)}) collective-permute-start(bf16[4,32,1024]{2,1,0:T(8,128)(2,1)S(1)} %get-tuple-element.66), channel_id=1, source_target_pairs={{0,24},{8,0},{16,8},{24,16},{32,56},{40,32},{48,40},{56,48},{64,88... | collective-permute-start | bytes 786440 | tf_op jit(solution)/shard_map/ppermute | solution.py:99
  91.4 17.0 %collective-permute-start.25 = (bf16[4,32,2048]{2,1,0:T(8,128)(2,1)S(1)}, bf16[4,32,2048]{2,1,0:T(8,128)(2,1)S(1)}, u32[]{:S(2)}, u32[]{:S(2)}) collective-permute-start(bf16[4,32,2048]{2,1,0:T(8,128)(2,1)S(1)} %get-tuple-element.76), channel_id=1, source_target_pairs={{0,64},{8,72},{16,80},{24,88},{32,96},{40,104},{48,112},{56,120},{... | collective-permute-start | bytes 1572872 | tf_op jit(solution)/shard_map/ppermute | solution.py:99
  93.5 18.5 %collective-permute-start.26 = (bf16[4,32,2048]{2,1,0:T(8,128)(2,1)S(1)}, bf16[4,32,2048]{2,1,0:T(8,128)(2,1)S(1)}, u32[]{:S(2)}, u32[]{:S(2)}) collective-permute-start(bf16[4,32,2048]{2,1,0:T(8,128)(2,1)S(1)} %get-tuple-element.77), channel_id=1, source_target_pairs={{0,96},{8,104},{16,112},{24,120},{32,0},{40,8},{48,16},{56,24},{64... | collective-permute-start | bytes 1572872 | tf_op jit(solution)/shard_map/ppermute | solution.py:99
  93.5 21.3 %collective-permute-start.27 = (bf16[4,32,2048]{2,1,0:T(8,128)(2,1)S(1)}, bf16[4,32,2048]{2,1,0:T(8,128)(2,1)S(1)}, u32[]{:S(2)}, u32[]{:S(2)}) collective-permute-start(bf16[4,32,2048]{2,1,0:T(8,128)(2,1)S(1)} %get-tuple-element.78), channel_id=1, source_target_pairs={{0,8},{8,16},{16,24},{24,0},{32,40},{40,48},{48,56},{56,32},{64,72... | collective-permute-start | bytes 1572872 | tf_op jit(solution)/shard_map/ppermute | solution.py:99
  102.0 12.8 %collective-permute-start.28 = (bf16[4,32,2048]{2,1,0:T(8,128)(2,1)S(1)}, bf16[4,32,2048]{2,1,0:T(8,128)(2,1)S(1)}, u32[]{:S(2)}, u32[]{:S(2)}) collective-permute-start(bf16[4,32,2048]{2,1,0:T(8,128)(2,1)S(1)} %get-tuple-element.79), channel_id=1, source_target_pairs={{0,16},{8,24},{16,0},{24,8},{32,48},{40,56},{48,32},{56,40},{64,80... | collective-permute-start | bytes 1572872 | tf_op jit(solution)/shard_map/ppermute | solution.py:99
  104.7 20.4 %collective-permute-start.29 = (bf16[4,32,2048]{2,1,0:T(8,128)(2,1)S(1)}, bf16[4,32,2048]{2,1,0:T(8,128)(2,1)S(1)}, u32[]{:S(2)}, u32[]{:S(2)}) collective-permute-start(bf16[4,32,2048]{2,1,0:T(8,128)(2,1)S(1)} %get-tuple-element.80), channel_id=1, source_target_pairs={{0,24},{8,0},{16,8},{24,16},{32,56},{40,32},{48,40},{56,48},{64,88... | collective-permute-start | bytes 1572872 | tf_op jit(solution)/shard_map/ppermute | solution.py:99
  108.4 22.6 %collective-permute-start.7 = (bf16[4,32,1024]{2,1,0:T(8,128)(2,1)S(1)}, bf16[4,32,1024]{2,1,0:T(8,128)(2,1)S(1)}, u32[]{:S(2)}, u32[]{:S(2)}) collective-permute-start(bf16[4,32,1024]{2,1,0:T(8,128)(2,1)S(1)} %get-tuple-element.56), channel_id=1, source_target_pairs={{0,64},{8,72},{16,80},{24,88},{32,96},{40,104},{48,112},{56,120},{... | collective-permute-start | bytes 786440 | tf_op jit(solution)/shard_map/ppermute | solution.py:99
  112.0 19.1 %collective-permute-start.8 = (bf16[4,32,1024]{2,1,0:T(8,128)(2,1)S(1)}, bf16[4,32,1024]{2,1,0:T(8,128)(2,1)S(1)}, u32[]{:S(2)}, u32[]{:S(2)}) collective-permute-start(bf16[4,32,1024]{2,1,0:T(8,128)(2,1)S(1)} %get-tuple-element.57), channel_id=1, source_target_pairs={{0,96},{8,104},{16,112},{24,120},{32,0},{40,8},{48,16},{56,24},{64... | collective-permute-start | bytes 786440 | tf_op jit(solution)/shard_map/ppermute | solution.py:99
  114.9 16.2 %collective-permute-start.9 = (bf16[4,32,1024]{2,1,0:T(8,128)(2,1)S(1)}, bf16[4,32,1024]{2,1,0:T(8,128)(2,1)S(1)}, u32[]{:S(2)}, u32[]{:S(2)}) collective-permute-start(bf16[4,32,1024]{2,1,0:T(8,128)(2,1)S(1)} %get-tuple-element.58), channel_id=1, source_target_pairs={{0,8},{8,16},{16,24},{24,0},{32,40},{40,48},{48,56},{56,32},{64,72... | collective-permute-start | bytes 786440 | tf_op jit(solution)/shard_map/ppermute | solution.py:99
  114.9 16.2 %collective-permute-start.10 = (bf16[4,32,1024]{2,1,0:T(8,128)(2,1)S(1)}, bf16[4,32,1024]{2,1,0:T(8,128)(2,1)S(1)}, u32[]{:S(2)}, u32[]{:S(2)}) collective-permute-start(bf16[4,32,1024]{2,1,0:T(8,128)(2,1)S(1)} %get-tuple-element.59), channel_id=1, source_target_pairs={{0,16},{8,24},{16,0},{24,8},{32,48},{40,56},{48,32},{56,40},{64,80... | collective-permute-start | bytes 786440 | tf_op jit(solution)/shard_map/ppermute | solution.py:99
  125.1 6.5 %collective-permute-start.11 = (bf16[4,32,1024]{2,1,0:T(8,128)(2,1)S(1)}, bf16[4,32,1024]{2,1,0:T(8,128)(2,1)S(1)}, u32[]{:S(2)}, u32[]{:S(2)}) collective-permute-start(bf16[4,32,1024]{2,1,0:T(8,128)(2,1)S(1)} %get-tuple-element.60), channel_id=1, source_target_pairs={{0,24},{8,0},{16,8},{24,16},{32,56},{40,32},{48,40},{56,48},{64,88... | collective-permute-start | bytes 786440 | tf_op jit(solution)/shard_map/ppermute | solution.py:99
  129.9 1.8 copy-start

commit v5 on v4

--- a/solution.py
+++ b/solution.py
@@ -6,7 +6,7 @@
 from jax.experimental.pallas import tpu as pltpu
 
 F32 = jnp.float32
-CUTS = {0: 1, 2: 2}
+CUTS = {0: (0, 4), 2: (0, 3, 4)}
 BF16 = jnp.bfloat16
 VM = pl.BlockSpec(memory_space=pltpu.VMEM)
 ANY = pl.BlockSpec(memory_space=pl.ANY)
@@ -99,31 +99,36 @@
     return lax.ppermute(v, "gx", pairs)
 
 
+def pieces_of(cuts, w):
+    return [(p * w // 4, q * w // 4) for p, q in zip(cuts, cuts[1:])]
+
+
 def regroup_kernel(cuts, *refs):
     outs = list(refs[8:])
     for k in range(2):
         got = refs[4 * k:4 * k + 4]
-        w = got[0].shape[-1] // cuts
-        for h in range(cuts):
+        for lo, hi in pieces_of(cuts, got[0].shape[-1]):
             for q in range(1, 4):
                 out = outs.pop(0)
                 for d in range(4):
-                    out[d] = got[d][q, :, h * w:(h + 1) * w]
+                    out[d] = got[d][q, :, lo:hi]
 
 
 def regroup(one, two, cuts):
     n, m, w = one[0].shape
-    out = jax.ShapeDtypeStruct((n, m, w // cuts), one[0].dtype)
+    count = len(cuts) - 1
+    shapes = [jax.ShapeDtypeStruct((n, m, hi - lo), one[0].dtype)
+              for lo, hi in pieces_of(cuts, w) for _ in range(3)]
     outs = pl.pallas_call(
         lambda *r: regroup_kernel(cuts, *r),
         in_specs=[VM] * 8,
-        out_specs=[VM] * (6 * cuts),
-        out_shape=[out] * (6 * cuts),
+        out_specs=[VM] * (6 * count),
+        out_shape=shapes * 2,
         compiler_params=pltpu.CompilerParams(vmem_limit_bytes=6 << 20),
         cost_estimate=pl.CostEstimate(flops=0, transcendentals=0, bytes_accessed=4 * one[0].size),
         name="regroup",
     )(*one, *two)
-    return [[outs[3 * (cuts * k + h):3 * (cuts * k + h) + 3] for k in range(2)] for h in range(cuts)]
+    return [[outs[3 * (count * k + h):3 * (count * k + h) + 3] for k in range(2)] for h in range(count)]
 
 
 def gram_kernel(cut, scale, *refs):
@@ -140,7 +145,7 @@
             for d2 in range(4):
                 g = member(x - d2, y - d1) if k else member(x - d1, y - d2)
                 if d2 == 0:
-                    p_refs[k][g] = blocks[k][d1][0, :, cut * w:(cut + 1) * w]
+                    p_refs[k][g] = blocks[k][d1][0, :, cut:cut + w]
                 else:
                     p_refs[k][g] = blocks[k][3 + d2][d1]
     for k in range(2):
@@ -255,7 +260,7 @@
     if k < 2:
         return x_refs[k], at
     w = x_refs[2].shape[-1]
-    return x_refs[2 + k - 2 + 2 * (at // w)], at % w
+    return (x_refs[k], at) if at < w else (x_refs[k + 2], at - w)
 
 
 def core_kernel(y_ref, *refs):
@@ -320,6 +325,7 @@
 def body(fields, test_matrix):
     s, _, n = fields.shape
     parts = lax.axis_size("gx")
+    w = n // parts
     axes = ("gx", "yz")
     scale = 1.0 / (s * n * lax.axis_size("yz"))
     order = ("x", "y", "x", "y")
@@ -342,8 +348,8 @@
             blocks[k, h] = near[k] + rest[0] + near[k + 1] + rest[1]
     pieces, part = [], None
     for (k, h), block in blocks.items():
-        last = (k, h) == (2, CUTS[2] - 1)
-        *more, part = add_gram(block, h, part, test_matrix.T if last else None, scale)
+        last = (k, h) == (2, len(CUTS[2]) - 2)
+        *more, part = add_gram(block, pieces_of(CUTS[k], w)[h][0], part, test_matrix.T if last else None, scale)
         pieces += more
     part = lax.all_to_all(part.reshape(128, 2, 128), axes, split_axis=0, concat_axis=0, tiled=True)
     part = total(part.reshape(256, 128))

time: 200 us -> 207 us (1.035)
  waiting for transfers between devices: 56.4 us -> 74.7 us
  starting transfers between devices: 64.8 us -> 56 us
  blocking collectives: 57.1 us -> 54.8 us
    ppermute x30, waiting for transfers between devices: 56.4 us -> 74.7 us  [shift(): return lax.ppermute(v, 'gx', pairs)]
    ppermute x30, starting transfers between devices: 64.8 us -> 56 us  [shift(): return lax.ppermute(v, 'gx', pairs)]
    all_to_all x2, blocking collectives: 37.1 us -> 34.8 us  [body(): lax.all_to_all(part.reshape(128, 2, 128), axes, split_axis=0, concat_axis...]
  transfers between devices with their start and end apart: 30 -> 30, of which waited for: 12 -> 12; matrix products, arithmetic and copies ran while one was open for 0% -> 0% of each run, Pallas kernels for 3% -> 4%
where the time goes in v5:
time: 207 us; the launch traced here: 206 us
  waiting for transfers between devices  74.7 us (36%)
  starting transfers between devices  56 us (27%)
  blocking collectives  54.8 us (26%)
  Pallas kernels  17.6 us (9%)
  local copies, waits for them, and re-layouts  2.47 us (1%)
    ppermute x30, waiting for transfers between devices, shift(): return lax.ppermute(v, 'gx', pairs)  74.7 us
    ppermute x30, starting transfers between devices, shift(): return lax.ppermute(v, 'gx', pairs)  56 us
    all_to_all x2, blocking collectives, body(): lax.all_to_all(part.reshape(128, 2, 128), axes, split_axis=0, concat_axis...  34.8 us
    all_to_all x1, blocking collectives, body(): core = lax.all_to_all(core, 'gx', split_axis=0, concat_axis=0, tiled=True)  20 us
    pallas_call x1, Pallas kernels, core_blocks(): pl.pallas_call(core_kernel, in_specs=[VM] * (1 + len(pieces)), out_specs=...  7.71 us
    pallas_call x3, Pallas kernels, add_gram(): pl.pallas_call(lambda *r: gram_kernel(cut, scale, *r), in_specs=[VM] * le...  4.78 us
  transfers between devices with their start and end apart: 30, of which 12 were waited for; matrix products, arithmetic and copies ran while one was open for 0% of the time, Pallas kernels for 4%

profile of v5, /device:TPU:0, one launch (start us, length us, event | category | flops | bytes accessed | tf_op | source)
XLA Modules:
  0.0 206.5 jit_solution(17988119437771678554)
XLA Ops:
  0.6 2.5 %slice.3.x_ref = bf16[2,32,32768]{2,1,0:T(8,128)(2,1)S(1)} slice(bf16[4,32,32768]{2,1,0:T(8,128)(2,1)} %r_0_.1), slice={[0:2], [0:32], [0:32768]} | slice | bytes 8388608 | tf_op jit(solution)/shard_map/slice | solution.py:333
  3.1 0.3 split.1
  3.4 1.7 collective-permute-start.18
  5.1 3.3 %fetch_split.1 = (bf16[4,32,2048]{2,1,0:T(8,128)(2,1)S(1)}, bf16[4,32,2048]{2,1,0:T(8,128)(2,1)S(1)}, bf16[4,32,2048]{2,1,0:T(8,128)(2,1)S(1)}, bf16[4,32,2048]{...) custom-call(bf16[4,32,32768]{2,1,0:T(8,128)(2,1)} %r_0_.1), custom_call_target="tpu_custom_call" | custom-call | bytes 8388608 | tf_op jit(solution)/shard_map/fetch_split/pallas_call | solution.py:80
  8.4 1.6 collective-permute-start
  9.9 1.6 collective-permute-start.1
  11.5 2.3 %collective-permute-start.2 = (bf16[4,32,2048]{2,1,0:T(8,128)(2,1)S(1)}, bf16[4,32,2048]{2,1,0:T(8,128)(2,1)S(1)}, u32[]{:S(2)}, u32[]{:S(2)}) collective-permute-start(bf16[4,32,2048]{2,1,0:T(8,128)(2,1)S(1)} %get-tuple-element.50), channel_id=1, source_target_pairs={{0,24},{8,0},{16,8},{24,16},{32,56},{40,32},{48,40},{56,48},{64,88... | collective-permute-start | bytes 1572872 | tf_op jit(solution)/shard_map/ppermute | solution.py:99
  13.8 1.6 collective-permute-start.3
  15.4 4.1 %collective-permute-done.18.r_1_ = bf16[4,32,2048]{2,1,0:T(8,128)(2,1)S(1)} collective-permute-done((bf16[4,32,2048]{2,1,0:T(8,128)(2,1)S(1)}, bf16[4,32,2048]{2,1,0:T(8,128)(2,1)S(1)}, u32[]{:S(2)}, u32[]{:S(2)}) %collective-permute-start.18) | collective-permute-done | bytes 524320 | tf_op jit(solution)/shard_map/ppermute | solution.py:99
  19.5 3.3 %collective-permute-start.4 = (bf16[4,32,2048]{2,1,0:T(8,128)(2,1)S(1)}, bf16[4,32,2048]{2,1,0:T(8,128)(2,1)S(1)}, u32[]{:S(2)}, u32[]{:S(2)}) collective-permute-start(bf16[4,32,2048]{2,1,0:T(8,128)(2,1)S(1)} %get-tuple-element.53), channel_id=1, source_target_pairs={{0,64},{8,72},{16,80},{24,88},{32,96},{40,104},{48,112},{56,120},{... | collective-permute-start | bytes 1572872 | tf_op jit(solution)/shard_map/ppermute | solution.py:99
  22.8 6.7 %collective-permute-done.r_1_ = bf16[4,32,2048]{2,1,0:T(8,128)(2,1)S(1)} collective-permute-done((bf16[4,32,2048]{2,1,0:T(8,128)(2,1)S(1)}, bf16[4,32,2048]{2,1,0:T(8,128)(2,1)S(1)}, u32[]{:S(2)}, u32[]{:S(2)}) %collective-permute-start) | collective-permute-done | bytes 524320 | tf_op jit(solution)/shard_map/ppermute | solution.py:99
  29.5 3.3 %collective-permute-start.5 = (bf16[4,32,2048]{2,1,0:T(8,128)(2,1)}, bf16[4,32,2048]{2,1,0:T(8,128)(2,1)S(1)}, u32[]{:S(2)}, u32[]{:S(2)}) collective-permute-start(bf16[4,32,2048]{2,1,0:T(8,128)(2,1)} %get-tuple-element.54), channel_id=1, source_target_pairs={{0,96},{8,104},{16,112},{24,120},{32,0},{40,8},{48,16},{56,24},{64... | collective-permute-start | bytes 1572872 | tf_op jit(solution)/shard_map/ppermute | solution.py:99
  32.8 9.1 %collective-permute-done.1.r_2_ = bf16[4,32,2048]{2,1,0:T(8,128)(2,1)S(1)} collective-permute-done((bf16[4,32,2048]{2,1,0:T(8,128)(2,1)S(1)}, bf16[4,32,2048]{2,1,0:T(8,128)(2,1)S(1)}, u32[]{:S(2)}, u32[]{:S(2)}) %collective-permute-start.1) | collective-permute-done | bytes 524320 | tf_op jit(solution)/shard_map/ppermute | solution.py:99
  41.9 0.8 collective-permute-start.19
  42.7 1.6 collective-permute-start.21
  44.4 2.9 %collective-permute-start.22 = (bf16[4,32,2048]{2,1,0:T(8,128)(2,1)S(1)}, bf16[4,32,2048]{2,1,0:T(8,128)(2,1)S(1)}, u32[]{:S(2)}, u32[]{:S(2)}) collective-permute-start(bf16[4,32,2048]{2,1,0:T(8,128)(2,1)S(1)} %get-tuple-element.73), channel_id=1, source_target_pairs={{0,64},{8,72},{16,80},{24,88},{32,96},{40,104},{48,112},{56,120},{... | collective-permute-start | bytes 1572872 | tf_op jit(solution)/shard_map/ppermute | solution.py:99
  47.3 1.3 collective-permute-start.23
  48.9 7.4 %collective-permute-done.19.r_2_ = bf16[4,32,2048]{2,1,0:T(8,128)(2,1)S(1)} collective-permute-done((bf16[4,32,2048]{2,1,0:T(8,128)(2,1)S(1)}, bf16[4,32,2048]{2,1,0:T(8,128)(2,1)S(1)}, u32[]{:S(2)}, u32[]{:S(2)}) %collective-permute-start.19) | collective-permute-done | bytes 524320 | tf_op jit(solution)/shard_map/ppermute | solution.py:99
  56.2 1.6 collective-permute-start.12
  57.8 2.9 %collective-permute-start.13 = (bf16[4,32,1536]{2,1,0:T(8,128)(2,1)S(1)}, bf16[4,32,1536]{2,1,0:T(8,128)(2,1)S(1)}, u32[]{:S(2)}, u32[]{:S(2)}) collective-permute-start(bf16[4,32,1536]{2,1,0:T(8,128)(2,1)S(1)} %get-tuple-element.62), channel_id=1, source_target_pairs={{0,64},{8,72},{16,80},{24,88},{32,96},{40,104},{48,112},{56,120},{... | collective-permute-start | bytes 1179656 | tf_op jit(solution)/shard_map/ppermute | solution.py:99
  60.7 4.6 %collective-permute-start.6 = (bf16[4,32,512]{2,1,0:T(8,128)(2,1)S(1)}, bf16[4,32,512]{2,1,0:T(8,128)(2,1)S(1)}, u32[]{:S(2)}, u32[]{:S(2)}) collective-permute-start(bf16[4,32,512]{2,1,0:T(8,128)(2,1)S(1)} %get-tuple-element.55), channel_id=1, source_target_pairs={{0,32},{8,40},{16,48},{24,56},{32,64},{40,72},{48,80},{56,88},{64,... | collective-permute-start | bytes 393224 | tf_op jit(solution)/shard_map/ppermute | solution.py:99
  65.3 6.1 %collective-permute-done.22.r_6_.r_9_ = bf16[4,32,2048]{2,1,0:T(8,128)(2,1)S(1)} collective-permute-done((bf16[4,32,2048]{2,1,0:T(8,128)(2,1)S(1)}, bf16[4,32,2048]{2,1,0:T(8,128)(2,1)S(1)}, u32[]{:S(2)}, u32[]{:S(2)}) %collective-permute-start.22) | collective-permute-done | bytes 524320 | tf_op jit(solution)/shard_map/ppermute | solution.py:99
  71.5 0.8 collective-permute-start.24
  72.3 2.5 %collective-permute-start.14 = (bf16[4,32,1536]{2,1,0:T(8,128)(2,1)S(1)}, bf16[4,32,1536]{2,1,0:T(8,128)(2,1)S(1)}, u32[]{:S(2)}, u32[]{:S(2)}) collective-permute-start(bf16[4,32,1536]{2,1,0:T(8,128)(2,1)S(1)} %get-tuple-element.63), channel_id=1, source_target_pairs={{0,96},{8,104},{16,112},{24,120},{32,0},{40,8},{48,16},{56,24},{64... | collective-permute-start | bytes 1179656 | tf_op jit(solution)/shard_map/ppermute | solution.py:99
  74.9 13.9 %collective-permute-done.6.r_4_ = bf16[4,32,512]{2,1,0:T(8,128)(2,1)S(1)} collective-permute-done((bf16[4,32,512]{2,1,0:T(8,128)(2,1)S(1)}, bf16[4,32,512]{2,1,0:T(8,128)(2,1)S(1)}, u32[]{:S(2)}, u32[]{:S(2)}) %collective-permute-start.6) | collective-permute-done | bytes 131104 | tf_op jit(solution)/shard_map/ppermute | solution.py:99
  88.8 2.9 %collective-permute-start.15 = (bf16[4,32,1536]{2,1,0:T(8,128)(2,1)S(1)}, bf16[4,32,1536]{2,1,0:T(8,128)(2,1)S(1)}, u32[]{:S(2)}, u32[]{:S(2)}) collective-permute-start(bf16[4,32,1536]{2,1,0:T(8,128)(2,1)S(1)} %get-tuple-element.64), channel_id=1, source_target_pairs={{0,8},{8,16},{16,24},{24,0},{32,40},{40,48},{48,56},{56,32},{64,72... | collective-permute-start | bytes 1179656 | tf_op jit(solution)/shard_map/ppermute | solution.py:99
  91.7 2.7 %collective-permute-start.16 = (bf16[4,32,1536]{2,1,0:T(8,128)(2,1)S(1)}, bf16[4,32,1536]{2,1,0:T(8,128)(2,1)S(1)}, u32[]{:S(2)}, u32[]{:S(2)}) collective-permute-start(bf16[4,32,1536]{2,1,0:T(8,128)(2,1)S(1)} %get-tuple-element.65), channel_id=1, source_target_pairs={{0,16},{8,24},{16,0},{24,8},{32,48},{40,56},{48,32},{56,40},{64,80... | collective-permute-start | bytes 1179656 | tf_op jit(solution)/shard_map/ppermute | solution.py:99
  94.4 2.1 collective-permute-start.25
  96.5 5.3 %collective-permute-done.15.r_11_ = bf16[4,32,1536]{2,1,0:T(8,128)(2,1)S(1)} collective-permute-done((bf16[4,32,1536]{2,1,0:T(8,128)(2,1)S(1)}, bf16[4,32,1536]{2,1,0:T(8,128)(2,1)S(1)}, u32[]{:S(2)}, u32[]{:S(2)}) %collective-permute-start.15) | collective-permute-done | bytes 393248 | tf_op jit(solution)/shard_map/ppermute | solution.py:99
  101.7 2.7 %collective-permute-start.26 = (bf16[4,32,2048]{2,1,0:T(8,128)(2,1)S(1)}, bf16[4,32,2048]{2,1,0:T(8,128)(2,1)S(1)}, u32[]{:S(2)}, u32[]{:S(2)}) collective-permute-start(bf16[4,32,2048]{2,1,0:T(8,128)(2,1)S(1)} %get-tuple-element.77), channel_id=1, source_target_pairs={{0,96},{8,104},{16,112},{24,120},{32,0},{40,8},{48,16},{56,24},{64... | collective-permute-start | bytes 1572872 | tf_op jit(solution)/shard_map/ppermute | solution.py:99
  104.5 6.2 %collective-permute-done.16.r_12_ = bf16[4,32,1536]{2,1,0:T(8,128)(2,1)S(1)} collective-permute-done((bf16[4,32,1536]{2,1,0:T(8,128)(2,1)S(1)}, bf16[4,32,1536]{2,1,0:T(8,128)(2,1)S(1)}, u32[]{:S(2)}, u32[]{:S(2)}) %collective-permute-start.16) | collective-permute-done | bytes 393248 | tf_op jit(solution)/shard_map/ppermute | solution.py:99
  110.7 3.3 %collective-permute-start.29 = (bf16[4,32,2048]{2,1,0:T(8,128)(2,1)S(1)}, bf16[4,32,2048]{2,1,0:T(8,128)(2,1)S(1)}, u32[]{:S(2)}, u32[]{:S(2)}) collective-permute-start(bf16[4,32,2048]{2,1,0:T(8,128)(2,1)S(1)} %get-tuple-element.80), channel_id=1, source_target_pairs={{0,24},{8,0},{16,8},{24,16},{32,56},{40,32},{48,40},{56,48},{64,88... | collective-permute-start | bytes 1572872 | tf_op jit(solution)/shard_map/ppermute | solution.py:99
  114.0 1.7 collective-permute-start.7
  115.7 2.8 %collective-permute-done.26.r_6_ = bf16[4,32,2048]{2,1,0:T(8,128)(2,1)S(1)} collective-permute-done((bf16[4,32,2048]{2,1,0:T(8,128)(2,1)S(1)}, bf16[4,32,2048]{2,1,0:T(8,128)(2,1)S(1)}, u32[]{:S(2)}, u32[]{:S(2)}) %collective-permute-start.26) | collective-permute-done | bytes 524320 | tf_op jit(solution)/shard_map/ppermute | solution.py:99
  118.4 2.7 %collective-permute-start.8 = (bf16[4,32,512]{2,1,0:T(8,128)(2,1)S(1)}, bf16[4,32,512]{2,1,0:T(8,128)(2,1)S(1)}, u32[]{:S(2)}, u32[]{:S(2)}) collective-permute-start(bf16[4,32,512]{2,1,0:T(8,128)(2,1)S(1)} %get-tuple-element.57), channel_id=1, source_target_pairs={{0,96},{8,104},{16,112},{24,120},{32,0},{40,8},{48,16},{56,24},{64... | collective-permute-start | bytes 393224 | tf_op jit(solution)/shard_map/ppermute | solution.py:99
  121.1 11.9 %collective-permute-done.27.r_11_ = bf16[4,32,2048]{2,1,0:T(8,128)(2,1)S(1)} collective-permute-done((bf16[4,32,2048]{2,1,0:T(8,128)(2,1)S(1)}, bf16[4,32,2048]{2,1,0:T(8,128)(2,1)S(1)}, u32[]{:S(2)}, u32[]{:S(2)}) %collective-permute-start.27) | collective-permute-done | bytes 524320 | tf_op jit(solution)/shard_map/ppermute | solution.py:99
  133.0 1.0 collective-permute-start.10
  134.1 2.5 %collective-permute-start.11 = (bf16[4,32,512]{2,1,0:T(8,128)(2,1)S(1)}, bf16[4,32,512]{2,1,0:T(8,128)(2,1)S(1)}, u32[]{:S(2)}, u32[]{:S(2)}) collective-permute-start(bf16[4,32,512]{2,1,0:T(8,128)(2,1)S(1)} %get-tuple-element.60), channel_id=1, source_target_pairs={{0,24},{8,0},{16,8},{24,16},{32,56},{40,32},{48,40},{56,48},{64,88... | collective-permute-start | bytes 393224 | tf_op jit(solution)/shard_map/ppermute | solution.py:99
  136.5 2.1 %gram.3 = (bf16[16,32,2048]{2,1,0:T(8,128)(2,1)S(1)}, bf16[16,32,2048]{2,1,0:T(8,128)(2,1)S(1)}, f32[3,256,256]{2,1,0:T(8,128)S(1)}) custom-call(bf16[4,32,2048]{2,1,0:T(8,128)(2,1)S(1)} %get-tuple-element.67.r_0_, bf16[4,32,2048]{2,1,0:T(8,128)(2,1)S(1)} %collective-permute-done.18.r_1_, bf16[4,32,2048]{2,1,0:T(8,128)(2,1)S(1)} %collective-permute-done.19.r_2_, ...), custom_call_target="tpu_custom_call" | custom-call | flops 1610612736 | bytes 8388608 | tf_op jit(solution)/shard_map/gram/pallas_call | solution.py:180
  138.6 1.6 gram.4
  140.3 0.4 collective-permute-done.9.r_11_
  140.6 0.9 collective-permute-done.11.r_13_
  141.5 1.1 gram.5
  142.6 20.6 %all_to_all.15 = f32[128,2,128]{2,1,0:T(2,128)S(1)} all-to-all(f32[128,2,128]{2,1,0:T(2,128)S(1)} %bitcast.10), channel_id=1, replica_groups=mesh['gx'=16,'yz'=8] {'gx','yz'}, dimensions={0} | all-to-all | bytes 262144 | tf_op jit(solution)/shard_map/all_to_all | solution.py:354
  163.3 14.2 %all_to_all.16 = f32[128,2,128]{2,1,0:T(2,128)S(1)} all-to-all(f32[128,2,128]{2,1,0:T(2,128)S(1)} %bitcast.8), channel_id=1, replica_groups=mesh['gx'=16,'yz'=8] {'gx','yz'}, dimensions={0} | all-to-all | bytes 262144 | tf_op jit(solution)/shard_map/all_to_all | solution.py:356
  177.5 7.7 %core.1 = (f32[64,512]{1,0:T(8,128)}, bf16[16,4,4,2048]{3,2,1,0:T(4,128)(2,1)S(1)}) custom-call(f32[256,128]{1,0:T(8,128)S(1)} %bitcast.6, bf16[16,32,2048]{2,1,0:T(8,128)(2,1)S(1)} %get-tuple-element.84.refs_0_, bf16[16,32,2048]{2,1,0:T(8,128)(2,1)S(1)} %get-tuple-element.85.refs_1_, bf16[16,32,1536]{2,1,0:T(8,128)(2,1)S(1)} %get-tuple-element.86.refs_2_, ...), custom_call_target="tpu_custom_call" | custom-call | tf_op jit(solution)/shard_map/core/pallas_call | solution.py:291
  185.2 20.0 %all_to_all.17.x_ref = bf16[16,4,4,2048]{3,2,1,0:T(4,128)(2,1)S(1)} all-to-all(bf16[16,4,4,2048]{3,2,1,0:T(4,128)(2,1)S(1)} %get-tuple-element.91), channel_id=1, replica_groups=mesh['gx'=16,'yz'=8] {'gx'}, dimensions={0} | all-to-all | bytes 2097152 | tf_op jit(solution)/shard_map/all_to_all | solution.py:358
  205.2 1.1 merge.1
  (28 shorter events, 0.5 us)
Async XLA Ops:
  3.4 16.1 %collective-permute-start.18 = (bf16[4,32,2048]{2,1,0:T(8,128)(2,1)S(1)}, bf16[4,32,2048]{2,1,0:T(8,128)(2,1)S(1)}, u32[]{:S(2)}, u32[]{:S(2)}) collective-permute-start(bf16[4,32,2048]{2,1,0:T(8,128)(2,1)S(1)} %get-tuple-element.68), channel_id=1, source_target_pairs={{0,8},{8,16},{16,24},{24,0},{32,40},{40,48},{48,56},{56,32},{64,72... | collective-permute-start | bytes 1572872 | tf_op jit(solution)/shard_map/ppermute | solution.py:99
  8.4 21.1 %collective-permute-start = (bf16[4,32,2048]{2,1,0:T(8,128)(2,1)S(1)}, bf16[4,32,2048]{2,1,0:T(8,128)(2,1)S(1)}, u32[]{:S(2)}, u32[]{:S(2)}) collective-permute-start(bf16[4,32,2048]{2,1,0:T(8,128)(2,1)S(1)} %get-tuple-element.48), channel_id=1, source_target_pairs={{0,8},{8,16},{16,24},{24,0},{32,40},{40,48},{48,56},{56,32},{64,72... | collective-permute-start | bytes 1572872 | tf_op jit(solution)/shard_map/ppermute | solution.py:99
  9.9 32.0 %collective-permute-start.1 = (bf16[4,32,2048]{2,1,0:T(8,128)(2,1)S(1)}, bf16[4,32,2048]{2,1,0:T(8,128)(2,1)S(1)}, u32[]{:S(2)}, u32[]{:S(2)}) collective-permute-start(bf16[4,32,2048]{2,1,0:T(8,128)(2,1)S(1)} %get-tuple-element.49), channel_id=1, source_target_pairs={{0,16},{8,24},{16,0},{24,8},{32,48},{40,56},{48,32},{56,40},{64,80... | collective-permute-start | bytes 1572872 | tf_op jit(solution)/shard_map/ppermute | solution.py:99
  11.5 31.2 %collective-permute-start.2 = (bf16[4,32,2048]{2,1,0:T(8,128)(2,1)S(1)}, bf16[4,32,2048]{2,1,0:T(8,128)(2,1)S(1)}, u32[]{:S(2)}, u32[]{:S(2)}) collective-permute-start(bf16[4,32,2048]{2,1,0:T(8,128)(2,1)S(1)} %get-tuple-element.50), channel_id=1, source_target_pairs={{0,24},{8,0},{16,8},{24,16},{32,56},{40,32},{48,40},{56,48},{64,88... | collective-permute-start | bytes 1572872 | tf_op jit(solution)/shard_map/ppermute | solution.py:99
  13.8 28.9 %collective-permute-start.3 = (bf16[4,32,2048]{2,1,0:T(8,128)(2,1)S(1)}, bf16[4,32,2048]{2,1,0:T(8,128)(2,1)S(1)}, u32[]{:S(2)}, u32[]{:S(2)}) collective-permute-start(bf16[4,32,2048]{2,1,0:T(8,128)(2,1)S(1)} %get-tuple-element.52), channel_id=1, source_target_pairs={{0,32},{8,40},{16,48},{24,56},{32,64},{40,72},{48,80},{56,88},{64,... | collective-permute-start | bytes 1572872 | tf_op jit(solution)/shard_map/ppermute | solution.py:99
  19.5 24.9 %collective-permute-start.4 = (bf16[4,32,2048]{2,1,0:T(8,128)(2,1)S(1)}, bf16[4,32,2048]{2,1,0:T(8,128)(2,1)S(1)}, u32[]{:S(2)}, u32[]{:S(2)}) collective-permute-start(bf16[4,32,2048]{2,1,0:T(8,128)(2,1)S(1)} %get-tuple-element.53), channel_id=1, source_target_pairs={{0,64},{8,72},{16,80},{24,88},{32,96},{40,104},{48,112},{56,120},{... | collective-permute-start | bytes 1572872 | tf_op jit(solution)/shard_map/ppermute | solution.py:99
  29.5 17.8 %collective-permute-start.5 = (bf16[4,32,2048]{2,1,0:T(8,128)(2,1)}, bf16[4,32,2048]{2,1,0:T(8,128)(2,1)S(1)}, u32[]{:S(2)}, u32[]{:S(2)}) collective-permute-start(bf16[4,32,2048]{2,1,0:T(8,128)(2,1)} %get-tuple-element.54), channel_id=1, source_target_pairs={{0,96},{8,104},{16,112},{24,120},{32,0},{40,8},{48,16},{56,24},{64... | collective-permute-start | bytes 1572872 | tf_op jit(solution)/shard_map/ppermute | solution.py:99
  41.9 14.3 %collective-permute-start.19 = (bf16[4,32,2048]{2,1,0:T(8,128)(2,1)S(1)}, bf16[4,32,2048]{2,1,0:T(8,128)(2,1)S(1)}, u32[]{:S(2)}, u32[]{:S(2)}) collective-permute-start(bf16[4,32,2048]{2,1,0:T(8,128)(2,1)S(1)} %get-tuple-element.69), channel_id=1, source_target_pairs={{0,16},{8,24},{16,0},{24,8},{32,48},{40,56},{48,32},{56,40},{64,80... | collective-permute-start | bytes 1572872 | tf_op jit(solution)/shard_map/ppermute | solution.py:99
  42.7 15.1 %collective-permute-start.20 = (bf16[4,32,2048]{2,1,0:T(8,128)(2,1)S(1)}, bf16[4,32,2048]{2,1,0:T(8,128)(2,1)S(1)}, u32[]{:S(2)}, u32[]{:S(2)}) collective-permute-start(bf16[4,32,2048]{2,1,0:T(8,128)(2,1)S(1)} %get-tuple-element.70), channel_id=1, source_target_pairs={{0,24},{8,0},{16,8},{24,16},{32,56},{40,32},{48,40},{56,48},{64,88... | collective-permute-start | bytes 1572872 | tf_op jit(solution)/shard_map/ppermute | solution.py:99
  42.7 18.0 %collective-permute-start.21 = (bf16[4,32,2048]{2,1,0:T(8,128)(2,1)S(1)}, bf16[4,32,2048]{2,1,0:T(8,128)(2,1)S(1)}, u32[]{:S(2)}, u32[]{:S(2)}) collective-permute-start(bf16[4,32,2048]{2,1,0:T(8,128)(2,1)S(1)} %get-tuple-element.72), channel_id=1, source_target_pairs={{0,32},{8,40},{16,48},{24,56},{32,64},{40,72},{48,80},{56,88},{64,... | collective-permute-start | bytes 1572872 | tf_op jit(solution)/shard_map/ppermute | solution.py:99
  44.4 26.9 %collective-permute-start.22 = (bf16[4,32,2048]{2,1,0:T(8,128)(2,1)S(1)}, bf16[4,32,2048]{2,1,0:T(8,128)(2,1)S(1)}, u32[]{:S(2)}, u32[]{:S(2)}) collective-permute-start(bf16[4,32,2048]{2,1,0:T(8,128)(2,1)S(1)} %get-tuple-element.73), channel_id=1, source_target_pairs={{0,64},{8,72},{16,80},{24,88},{32,96},{40,104},{48,112},{56,120},{... | collective-permute-start | bytes 1572872 | tf_op jit(solution)/shard_map/ppermute | solution.py:99
  47.3 24.0 %collective-permute-start.23 = (bf16[4,32,2048]{2,1,0:T(8,128)(2,1)S(1)}, bf16[4,32,2048]{2,1,0:T(8,128)(2,1)S(1)}, u32[]{:S(2)}, u32[]{:S(2)}) collective-permute-start(bf16[4,32,2048]{2,1,0:T(8,128)(2,1)S(1)} %get-tuple-element.74), channel_id=1, source_target_pairs={{0,96},{8,104},{16,112},{24,120},{32,0},{40,8},{48,16},{56,24},{64... | collective-permute-start | bytes 1572872 | tf_op jit(solution)/shard_map/ppermute | solution.py:99
  56.2 35.5 %collective-permute-start.12 = (bf16[4,32,1536]{2,1,0:T(8,128)(2,1)S(1)}, bf16[4,32,1536]{2,1,0:T(8,128)(2,1)S(1)}, u32[]{:S(2)}, u32[]{:S(2)}) collective-permute-start(bf16[4,32,1536]{2,1,0:T(8,128)(2,1)S(1)} %get-tuple-element.61), channel_id=1, source_target_pairs={{0,32},{8,40},{16,48},{24,56},{32,64},{40,72},{48,80},{56,88},{64,... | collective-permute-start | bytes 1179656 | tf_op jit(solution)/shard_map/ppermute | solution.py:99
  57.8 36.6 %collective-permute-start.13 = (bf16[4,32,1536]{2,1,0:T(8,128)(2,1)S(1)}, bf16[4,32,1536]{2,1,0:T(8,128)(2,1)S(1)}, u32[]{:S(2)}, u32[]{:S(2)}) collective-permute-start(bf16[4,32,1536]{2,1,0:T(8,128)(2,1)S(1)} %get-tuple-element.62), channel_id=1, source_target_pairs={{0,64},{8,72},{16,80},{24,88},{32,96},{40,104},{48,112},{56,120},{... | collective-permute-start | bytes 1179656 | tf_op jit(solution)/shard_map/ppermute | solution.py:99
  60.7 28.1 %collective-permute-start.6 = (bf16[4,32,512]{2,1,0:T(8,128)(2,1)S(1)}, bf16[4,32,512]{2,1,0:T(8,128)(2,1)S(1)}, u32[]{:S(2)}, u32[]{:S(2)}) collective-permute-start(bf16[4,32,512]{2,1,0:T(8,128)(2,1)S(1)} %get-tuple-element.55), channel_id=1, source_target_pairs={{0,32},{8,40},{16,48},{24,56},{32,64},{40,72},{48,80},{56,88},{64,... | collective-permute-start | bytes 393224 | tf_op jit(solution)/shard_map/ppermute | solution.py:99
  71.5 39.2 %collective-permute-start.24 = (bf16[4,32,2048]{2,1,0:T(8,128)(2,1)S(1)}, bf16[4,32,2048]{2,1,0:T(8,128)(2,1)S(1)}, u32[]{:S(2)}, u32[]{:S(2)}) collective-permute-start(bf16[4,32,2048]{2,1,0:T(8,128)(2,1)S(1)} %get-tuple-element.75), channel_id=1, source_target_pairs={{0,32},{8,40},{16,48},{24,56},{32,64},{40,72},{48,80},{56,88},{64,... | collective-permute-start | bytes 1572872 | tf_op jit(solution)/shard_map/ppermute | solution.py:99
  72.3 22.1 %collective-permute-start.14 = (bf16[4,32,1536]{2,1,0:T(8,128)(2,1)S(1)}, bf16[4,32,1536]{2,1,0:T(8,128)(2,1)S(1)}, u32[]{:S(2)}, u32[]{:S(2)}) collective-permute-start(bf16[4,32,1536]{2,1,0:T(8,128)(2,1)S(1)} %get-tuple-element.63), channel_id=1, source_target_pairs={{0,96},{8,104},{16,112},{24,120},{32,0},{40,8},{48,16},{56,24},{64... | collective-permute-start | bytes 1179656 | tf_op jit(solution)/shard_map/ppermute | solution.py:99
  88.8 13.0 %collective-permute-start.15 = (bf16[4,32,1536]{2,1,0:T(8,128)(2,1)S(1)}, bf16[4,32,1536]{2,1,0:T(8,128)(2,1)S(1)}, u32[]{:S(2)}, u32[]{:S(2)}) collective-permute-start(bf16[4,32,1536]{2,1,0:T(8,128)(2,1)S(1)} %get-tuple-element.64), channel_id=1, source_target_pairs={{0,8},{8,16},{16,24},{24,0},{32,40},{40,48},{48,56},{56,32},{64,72... | collective-permute-start | bytes 1179656 | tf_op jit(solution)/shard_map/ppermute | solution.py:99
  91.7 19.0 %collective-permute-start.16 = (bf16[4,32,1536]{2,1,0:T(8,128)(2,1)S(1)}, bf16[4,32,1536]{2,1,0:T(8,128)(2,1)S(1)}, u32[]{:S(2)}, u32[]{:S(2)}) collective-permute-start(bf16[4,32,1536]{2,1,0:T(8,128)(2,1)S(1)} %get-tuple-element.65), channel_id=1, source_target_pairs={{0,16},{8,24},{16,0},{24,8},{32,48},{40,56},{48,32},{56,40},{64,80... | collective-permute-start | bytes 1179656 | tf_op jit(solution)/shard_map/ppermute | solution.py:99
  94.4 16.3 %collective-permute-start.17 = (bf16[4,32,1536]{2,1,0:T(8,128)(2,1)S(1)}, bf16[4,32,1536]{2,1,0:T(8,128)(2,1)S(1)}, u32[]{:S(2)}, u32[]{:S(2)}) collective-permute-start(bf16[4,32,1536]{2,1,0:T(8,128)(2,1)S(1)} %get-tuple-element.66), channel_id=1, source_target_pairs={{0,24},{8,0},{16,8},{24,16},{32,56},{40,32},{48,40},{56,48},{64,88... | collective-permute-start | bytes 1179656 | tf_op jit(solution)/shard_map/ppermute | solution.py:99
  94.4 19.6 %collective-permute-start.25 = (bf16[4,32,2048]{2,1,0:T(8,128)(2,1)S(1)}, bf16[4,32,2048]{2,1,0:T(8,128)(2,1)S(1)}, u32[]{:S(2)}, u32[]{:S(2)}) collective-permute-start(bf16[4,32,2048]{2,1,0:T(8,128)(2,1)S(1)} %get-tuple-element.76), channel_id=1, source_target_pairs={{0,64},{8,72},{16,80},{24,88},{32,96},{40,104},{48,112},{56,120},{... | collective-permute-start | bytes 1572872 | tf_op jit(solution)/shard_map/ppermute | solution.py:99
  101.7 16.7 %collective-permute-start.26 = (bf16[4,32,2048]{2,1,0:T(8,128)(2,1)S(1)}, bf16[4,32,2048]{2,1,0:T(8,128)(2,1)S(1)}, u32[]{:S(2)}, u32[]{:S(2)}) collective-permute-start(bf16[4,32,2048]{2,1,0:T(8,128)(2,1)S(1)} %get-tuple-element.77), channel_id=1, source_target_pairs={{0,96},{8,104},{16,112},{24,120},{32,0},{40,8},{48,16},{56,24},{64... | collective-permute-start | bytes 1572872 | tf_op jit(solution)/shard_map/ppermute | solution.py:99
  110.7 22.4 %collective-permute-start.27 = (bf16[4,32,2048]{2,1,0:T(8,128)(2,1)S(1)}, bf16[4,32,2048]{2,1,0:T(8,128)(2,1)S(1)}, u32[]{:S(2)}, u32[]{:S(2)}) collective-permute-start(bf16[4,32,2048]{2,1,0:T(8,128)(2,1)S(1)} %get-tuple-element.78), channel_id=1, source_target_pairs={{0,8},{8,16},{16,24},{24,0},{32,40},{40,48},{48,56},{56,32},{64,72... | collective-permute-start | bytes 1572872 | tf_op jit(solution)/shard_map/ppermute | solution.py:99
  110.7 22.4 %collective-permute-start.28 = (bf16[4,32,2048]{2,1,0:T(8,128)(2,1)S(1)}, bf16[4,32,2048]{2,1,0:T(8,128)(2,1)S(1)}, u32[]{:S(2)}, u32[]{:S(2)}) collective-permute-start(bf16[4,32,2048]{2,1,0:T(8,128)(2,1)S(1)} %get-tuple-element.79), channel_id=1, source_target_pairs={{0,16},{8,24},{16,0},{24,8},{32,48},{40,56},{48,32},{56,40},{64,80... | collective-permute-start | bytes 1572872 | tf_op jit(solution)/shard_map/ppermute | solution.py:99
  110.7 23.3 %collective-permute-start.29 = (bf16[4,32,2048]{2,1,0:T(8,128)(2,1)S(1)}, bf16[4,32,2048]{2,1,0:T(8,128)(2,1)S(1)}, u32[]{:S(2)}, u32[]{:S(2)}) collective-permute-start(bf16[4,32,2048]{2,1,0:T(8,128)(2,1)S(1)} %get-tuple-element.80), channel_id=1, source_target_pairs={{0,24},{8,0},{16,8},{24,16},{32,56},{40,32},{48,40},{56,48},{64,88... | collective-permute-start | bytes 1572872 | tf_op jit(solution)/shard_map/ppermute | solution.py:99
  114.0 26.2 %collective-permute-start.7 = (bf16[4,32,512]{2,1,0:T(8,128)(2,1)S(1)}, bf16[4,32,512]{2,1,0:T(8,128)(2,1)S(1)}, u32[]{:S(2)}, u32[]{:S(2)}) collective-permute-start(bf16[4,32,512]{2,1,0:T(8,128)(2,1)S(1)} %get-tuple-element.56), channel_id=1, source_target_pairs={{0,64},{8,72},{16,80},{24,88},{32,96},{40,104},{48,112},{56,120},{... | collective-permute-start | bytes 393224 | tf_op jit(solution)/shard_map/ppermute | solution.py:99
  118.4 21.8 %collective-permute-start.8 = (bf16[4,32,512]{2,1,0:T(8,128)(2,1)S(1)}, bf16[4,32,512]{2,1,0:T(8,128)(2,1)S(1)}, u32[]{:S(2)}, u32[]{:S(2)}) collective-permute-start(bf16[4,32,512]{2,1,0:T(8,128)(2,1)S(1)} %get-tuple-element.57), channel_id=1, source_target_pairs={{0,96},{8,104},{16,112},{24,120},{32,0},{40,8},{48,16},{56,24},{64... | collective-permute-start | bytes 393224 | tf_op jit(solution)/shard_map/ppermute | solution.py:99
  133.0 7.6 %collective-permute-start.9 = (bf16[4,32,512]{2,1,0:T(8,128)(2,1)S(1)}, bf16[4,32,512]{2,1,0:T(8,128)(2,1)S(1)}, u32[]{:S(2)}, u32[]{:S(2)}) collective-permute-start(bf16[4,32,512]{2,1,0:T(8,128)(2,1)S(1)} %get-tuple-element.58), channel_id=1, source_target_pairs={{0,8},{8,16},{16,24},{24,0},{32,40},{40,48},{48,56},{56,32},{64,72... | collective-permute-start | bytes 393224 | tf_op jit(solution)/shard_map/ppermute | solution.py:99
  133.0 7.6 %collective-permute-start.10 = (bf16[4,32,512]{2,1,0:T(8,128)(2,1)S(1)}, bf16[4,32,512]{2,1,0:T(8,128)(2,1)S(1)}, u32[]{:S(2)}, u32[]{:S(2)}) collective-permute-start(bf16[4,32,512]{2,1,0:T(8,128)(2,1)S(1)} %get-tuple-element.59), channel_id=1, source_target_pairs={{0,16},{8,24},{16,0},{24,8},{32,48},{40,56},{48,32},{56,40},{64,80... | collective-permute-start | bytes 393224 | tf_op jit(solution)/shard_map/ppermute | solution.py:99
  134.1 7.5 %collective-permute-start.11 = (bf16[4,32,512]{2,1,0:T(8,128)(2,1)S(1)}, bf16[4,32,512]{2,1,0:T(8,128)(2,1)S(1)}, u32[]{:S(2)}, u32[]{:S(2)}) collective-permute-start(bf16[4,32,512]{2,1,0:T(8,128)(2,1)S(1)} %get-tuple-element.60), channel_id=1, source_target_pairs={{0,24},{8,0},{16,8},{24,16},{32,56},{40,32},{48,40},{56,48},{64,88... | collective-permute-start | bytes 393224 | tf_op jit(solution)/shard_map/ppermute | solution.py:99
  138.6 2.9 %copy-start = (f32[512,64]{0,1:T(8,128)S(1)}, f32[512,64]{0,1:T(8,128)}, u32[]{:S(2)}) copy-start(f32[512,64]{0,1:T(8,128)} %param.3) | copy-start | bytes 393220

commit v6 on v5

--- a/solution.py
+++ b/solution.py
@@ -271,19 +271,33 @@
     ft = orthonormal_t(orthonormal_t(yt, 8), 8)
     f_ref[...] = ft
     low = ft.astype(BF16)
-    i = lax.broadcasted_iota(jnp.int32, (64 * s, 64), 0)
-    j = lax.broadcasted_iota(jnp.int32, (64 * s, 64), 1)
-    wide = [jnp.dot((i == j * s + k).astype(BF16), low, preferred_element_type=F32).astype(BF16)
-            for k in range(s)]
+    n = 32 * s
+    i = lax.broadcasted_iota(jnp.int32, (n, 64), 0)
+    j = lax.broadcasted_iota(jnp.int32, (n, 64), 1)
+    wide = []
+    for k in range(s):
+        late = (i // 2 + k // 2) % 2
+        wide.append(nn(((j == i // 8 * 4 + late * 2 + i // 4 % 2) & (i % 2 == k % 2)).astype(BF16),
+                       low).astype(BF16))
     step = 512
+    tile = (n // 8, 8, step)
+    own = lax.broadcasted_iota(jnp.int32, tile, 1) % 4 < 2
     for c in range(w // step):
-        acc = None
+        pair = []
         for k in range(s):
             x_ref, at = cells_of(x_refs, k, c * step)
             x = x_ref[:, :, at:at + step].reshape(parts * m, step)
-            t = jnp.dot(wide[k], x, preferred_element_type=F32)
-            acc = t if acc is None else acc + t
-        o_ref[:, :, :, c * step:(c + 1) * step] = acc.astype(BF16).reshape(o_ref.shape[:3] + (step,))
+            t = nn(wide[k], x)
+            if k % 2:
+                pair[-1] = (pair[-1] + t).reshape(tile)
+            else:
+                pair.append(t)
+        even = jnp.where(own, pair[0], pair[1])
+        odd = jnp.where(own, pair[1], pair[0])
+        odd = jnp.where(own, pltpu.roll(odd, 6, 1), pltpu.roll(odd, 2, 1))
+        cells = slice(c * step, (c + 1) * step)
+        for h, rows in enumerate((even, odd)):
+            o_ref[:, 2 * h:2 * h + 2, :, cells] = rows.astype(BF16).reshape(parts, 2, s, step)
 
 
 def core_blocks(full, pieces, s):

time: 207 us -> 206 us (level)
  no operation moved by 1% of the time
where the time goes in v6:
time: 206 us; the launch traced here: 205 us
  waiting for transfers between devices  74.7 us (36%)
  starting transfers between devices  56 us (27%)
  blocking collectives  54.8 us (27%)
  Pallas kernels  16.6 us (8%)
  local copies, waits for them, and re-layouts  2.47 us (1%)
    ppermute x30, waiting for transfers between devices, shift(): return lax.ppermute(v, 'gx', pairs)  74.7 us
    ppermute x30, starting transfers between devices, shift(): return lax.ppermute(v, 'gx', pairs)  56 us
    all_to_all x2, blocking collectives, body(): lax.all_to_all(part.reshape(128, 2, 128), axes, split_axis=0, concat_axis...  34.8 us
    all_to_all x1, blocking collectives, body(): core = lax.all_to_all(core, 'gx', split_axis=0, concat_axis=0, tiled=True)  20.1 us
    pallas_call x1, Pallas kernels, core_blocks(): pl.pallas_call(core_kernel, in_specs=[VM] * (1 + len(pieces)), out_specs=...  6.64 us
    pallas_call x3, Pallas kernels, add_gram(): pl.pallas_call(lambda *r: gram_kernel(cut, scale, *r), in_specs=[VM] * le...  4.78 us
  transfers between devices with their start and end apart: 30, of which 12 were waited for; matrix products, arithmetic and copies ran while one was open for 0% of the time, Pallas kernels for 4%

profile of v6, /device:TPU:0, one launch (start us, length us, event | category | flops | bytes accessed | tf_op | source)
XLA Modules:
  0.0 205.4 jit_solution(11738391972043068782)
XLA Ops:
  0.6 2.5 %slice.3.x_ref = bf16[2,32,32768]{2,1,0:T(8,128)(2,1)S(1)} slice(bf16[4,32,32768]{2,1,0:T(8,128)(2,1)} %r_0_.1), slice={[0:2], [0:32], [0:32768]} | slice | bytes 8388608 | tf_op jit(solution)/shard_map/slice | solution.py:347
  3.1 0.3 split.1
  3.4 1.7 collective-permute-start.18
  5.1 3.3 %fetch_split.1 = (bf16[4,32,2048]{2,1,0:T(8,128)(2,1)S(1)}, bf16[4,32,2048]{2,1,0:T(8,128)(2,1)S(1)}, bf16[4,32,2048]{2,1,0:T(8,128)(2,1)S(1)}, bf16[4,32,2048]{...) custom-call(bf16[4,32,32768]{2,1,0:T(8,128)(2,1)} %r_0_.1), custom_call_target="tpu_custom_call" | custom-call | bytes 8388608 | tf_op jit(solution)/shard_map/fetch_split/pallas_call | solution.py:80
  8.4 1.6 collective-permute-start
  9.9 1.6 collective-permute-start.1
  11.5 2.3 %collective-permute-start.2 = (bf16[4,32,2048]{2,1,0:T(8,128)(2,1)S(1)}, bf16[4,32,2048]{2,1,0:T(8,128)(2,1)S(1)}, u32[]{:S(2)}, u32[]{:S(2)}) collective-permute-start(bf16[4,32,2048]{2,1,0:T(8,128)(2,1)S(1)} %get-tuple-element.50), channel_id=1, source_target_pairs={{0,24},{8,0},{16,8},{24,16},{32,56},{40,32},{48,40},{56,48},{64,88... | collective-permute-start | bytes 1572872 | tf_op jit(solution)/shard_map/ppermute | solution.py:99
  13.8 1.6 collective-permute-start.3
  15.4 4.1 %collective-permute-done.18.r_1_ = bf16[4,32,2048]{2,1,0:T(8,128)(2,1)S(1)} collective-permute-done((bf16[4,32,2048]{2,1,0:T(8,128)(2,1)S(1)}, bf16[4,32,2048]{2,1,0:T(8,128)(2,1)S(1)}, u32[]{:S(2)}, u32[]{:S(2)}) %collective-permute-start.18) | collective-permute-done | bytes 524320 | tf_op jit(solution)/shard_map/ppermute | solution.py:99
  19.5 3.3 %collective-permute-start.4 = (bf16[4,32,2048]{2,1,0:T(8,128)(2,1)S(1)}, bf16[4,32,2048]{2,1,0:T(8,128)(2,1)S(1)}, u32[]{:S(2)}, u32[]{:S(2)}) collective-permute-start(bf16[4,32,2048]{2,1,0:T(8,128)(2,1)S(1)} %get-tuple-element.53), channel_id=1, source_target_pairs={{0,64},{8,72},{16,80},{24,88},{32,96},{40,104},{48,112},{56,120},{... | collective-permute-start | bytes 1572872 | tf_op jit(solution)/shard_map/ppermute | solution.py:99
  22.8 6.7 %collective-permute-done.r_1_ = bf16[4,32,2048]{2,1,0:T(8,128)(2,1)S(1)} collective-permute-done((bf16[4,32,2048]{2,1,0:T(8,128)(2,1)S(1)}, bf16[4,32,2048]{2,1,0:T(8,128)(2,1)S(1)}, u32[]{:S(2)}, u32[]{:S(2)}) %collective-permute-start) | collective-permute-done | bytes 524320 | tf_op jit(solution)/shard_map/ppermute | solution.py:99
  29.5 3.3 %collective-permute-start.5 = (bf16[4,32,2048]{2,1,0:T(8,128)(2,1)}, bf16[4,32,2048]{2,1,0:T(8,128)(2,1)S(1)}, u32[]{:S(2)}, u32[]{:S(2)}) collective-permute-start(bf16[4,32,2048]{2,1,0:T(8,128)(2,1)} %get-tuple-element.54), channel_id=1, source_target_pairs={{0,96},{8,104},{16,112},{24,120},{32,0},{40,8},{48,16},{56,24},{64... | collective-permute-start | bytes 1572872 | tf_op jit(solution)/shard_map/ppermute | solution.py:99
  32.8 9.1 %collective-permute-done.1.r_2_ = bf16[4,32,2048]{2,1,0:T(8,128)(2,1)S(1)} collective-permute-done((bf16[4,32,2048]{2,1,0:T(8,128)(2,1)S(1)}, bf16[4,32,2048]{2,1,0:T(8,128)(2,1)S(1)}, u32[]{:S(2)}, u32[]{:S(2)}) %collective-permute-start.1) | collective-permute-done | bytes 524320 | tf_op jit(solution)/shard_map/ppermute | solution.py:99
  41.9 0.8 collective-permute-start.19
  42.7 1.6 collective-permute-start.21
  44.4 2.9 %collective-permute-start.22 = (bf16[4,32,2048]{2,1,0:T(8,128)(2,1)S(1)}, bf16[4,32,2048]{2,1,0:T(8,128)(2,1)S(1)}, u32[]{:S(2)}, u32[]{:S(2)}) collective-permute-start(bf16[4,32,2048]{2,1,0:T(8,128)(2,1)S(1)} %get-tuple-element.73), channel_id=1, source_target_pairs={{0,64},{8,72},{16,80},{24,88},{32,96},{40,104},{48,112},{56,120},{... | collective-permute-start | bytes 1572872 | tf_op jit(solution)/shard_map/ppermute | solution.py:99
  47.3 1.3 collective-permute-start.23
  48.9 7.4 %collective-permute-done.19.r_2_ = bf16[4,32,2048]{2,1,0:T(8,128)(2,1)S(1)} collective-permute-done((bf16[4,32,2048]{2,1,0:T(8,128)(2,1)S(1)}, bf16[4,32,2048]{2,1,0:T(8,128)(2,1)S(1)}, u32[]{:S(2)}, u32[]{:S(2)}) %collective-permute-start.19) | collective-permute-done | bytes 524320 | tf_op jit(solution)/shard_map/ppermute | solution.py:99
  56.2 1.6 collective-permute-start.12
  57.8 2.9 %collective-permute-start.13 = (bf16[4,32,1536]{2,1,0:T(8,128)(2,1)S(1)}, bf16[4,32,1536]{2,1,0:T(8,128)(2,1)S(1)}, u32[]{:S(2)}, u32[]{:S(2)}) collective-permute-start(bf16[4,32,1536]{2,1,0:T(8,128)(2,1)S(1)} %get-tuple-element.62), channel_id=1, source_target_pairs={{0,64},{8,72},{16,80},{24,88},{32,96},{40,104},{48,112},{56,120},{... | collective-permute-start | bytes 1179656 | tf_op jit(solution)/shard_map/ppermute | solution.py:99
  60.7 4.6 %collective-permute-start.6 = (bf16[4,32,512]{2,1,0:T(8,128)(2,1)S(1)}, bf16[4,32,512]{2,1,0:T(8,128)(2,1)S(1)}, u32[]{:S(2)}, u32[]{:S(2)}) collective-permute-start(bf16[4,32,512]{2,1,0:T(8,128)(2,1)S(1)} %get-tuple-element.55), channel_id=1, source_target_pairs={{0,32},{8,40},{16,48},{24,56},{32,64},{40,72},{48,80},{56,88},{64,... | collective-permute-start | bytes 393224 | tf_op jit(solution)/shard_map/ppermute | solution.py:99
  65.3 6.1 %collective-permute-done.22.r_6_.r_9_ = bf16[4,32,2048]{2,1,0:T(8,128)(2,1)S(1)} collective-permute-done((bf16[4,32,2048]{2,1,0:T(8,128)(2,1)S(1)}, bf16[4,32,2048]{2,1,0:T(8,128)(2,1)S(1)}, u32[]{:S(2)}, u32[]{:S(2)}) %collective-permute-start.22) | collective-permute-done | bytes 524320 | tf_op jit(solution)/shard_map/ppermute | solution.py:99
  71.5 0.8 collective-permute-start.24
  72.3 2.5 %collective-permute-start.14 = (bf16[4,32,1536]{2,1,0:T(8,128)(2,1)S(1)}, bf16[4,32,1536]{2,1,0:T(8,128)(2,1)S(1)}, u32[]{:S(2)}, u32[]{:S(2)}) collective-permute-start(bf16[4,32,1536]{2,1,0:T(8,128)(2,1)S(1)} %get-tuple-element.63), channel_id=1, source_target_pairs={{0,96},{8,104},{16,112},{24,120},{32,0},{40,8},{48,16},{56,24},{64... | collective-permute-start | bytes 1179656 | tf_op jit(solution)/shard_map/ppermute | solution.py:99
  74.9 13.9 %collective-permute-done.6.r_4_ = bf16[4,32,512]{2,1,0:T(8,128)(2,1)S(1)} collective-permute-done((bf16[4,32,512]{2,1,0:T(8,128)(2,1)S(1)}, bf16[4,32,512]{2,1,0:T(8,128)(2,1)S(1)}, u32[]{:S(2)}, u32[]{:S(2)}) %collective-permute-start.6) | collective-permute-done | bytes 131104 | tf_op jit(solution)/shard_map/ppermute | solution.py:99
  88.8 2.9 %collective-permute-start.15 = (bf16[4,32,1536]{2,1,0:T(8,128)(2,1)S(1)}, bf16[4,32,1536]{2,1,0:T(8,128)(2,1)S(1)}, u32[]{:S(2)}, u32[]{:S(2)}) collective-permute-start(bf16[4,32,1536]{2,1,0:T(8,128)(2,1)S(1)} %get-tuple-element.64), channel_id=1, source_target_pairs={{0,8},{8,16},{16,24},{24,0},{32,40},{40,48},{48,56},{56,32},{64,72... | collective-permute-start | bytes 1179656 | tf_op jit(solution)/shard_map/ppermute | solution.py:99
  91.7 2.7 %collective-permute-start.16 = (bf16[4,32,1536]{2,1,0:T(8,128)(2,1)S(1)}, bf16[4,32,1536]{2,1,0:T(8,128)(2,1)S(1)}, u32[]{:S(2)}, u32[]{:S(2)}) collective-permute-start(bf16[4,32,1536]{2,1,0:T(8,128)(2,1)S(1)} %get-tuple-element.65), channel_id=1, source_target_pairs={{0,16},{8,24},{16,0},{24,8},{32,48},{40,56},{48,32},{56,40},{64,80... | collective-permute-start | bytes 1179656 | tf_op jit(solution)/shard_map/ppermute | solution.py:99
  94.4 2.1 %collective-permute-start.25 = (bf16[4,32,2048]{2,1,0:T(8,128)(2,1)S(1)}, bf16[4,32,2048]{2,1,0:T(8,128)(2,1)S(1)}, u32[]{:S(2)}, u32[]{:S(2)}) collective-permute-start(bf16[4,32,2048]{2,1,0:T(8,128)(2,1)S(1)} %get-tuple-element.76), channel_id=1, source_target_pairs={{0,64},{8,72},{16,80},{24,88},{32,96},{40,104},{48,112},{56,120},{... | collective-permute-start | bytes 1572872 | tf_op jit(solution)/shard_map/ppermute | solution.py:99
  96.5 5.3 %collective-permute-done.15.r_11_ = bf16[4,32,1536]{2,1,0:T(8,128)(2,1)S(1)} collective-permute-done((bf16[4,32,1536]{2,1,0:T(8,128)(2,1)S(1)}, bf16[4,32,1536]{2,1,0:T(8,128)(2,1)S(1)}, u32[]{:S(2)}, u32[]{:S(2)}) %collective-permute-start.15) | collective-permute-done | bytes 393248 | tf_op jit(solution)/shard_map/ppermute | solution.py:99
  101.7 2.7 %collective-permute-start.26 = (bf16[4,32,2048]{2,1,0:T(8,128)(2,1)S(1)}, bf16[4,32,2048]{2,1,0:T(8,128)(2,1)S(1)}, u32[]{:S(2)}, u32[]{:S(2)}) collective-permute-start(bf16[4,32,2048]{2,1,0:T(8,128)(2,1)S(1)} %get-tuple-element.77), channel_id=1, source_target_pairs={{0,96},{8,104},{16,112},{24,120},{32,0},{40,8},{48,16},{56,24},{64... | collective-permute-start | bytes 1572872 | tf_op jit(solution)/shard_map/ppermute | solution.py:99
  104.5 6.2 %collective-permute-done.16.r_12_ = bf16[4,32,1536]{2,1,0:T(8,128)(2,1)S(1)} collective-permute-done((bf16[4,32,1536]{2,1,0:T(8,128)(2,1)S(1)}, bf16[4,32,1536]{2,1,0:T(8,128)(2,1)S(1)}, u32[]{:S(2)}, u32[]{:S(2)}) %collective-permute-start.16) | collective-permute-done | bytes 393248 | tf_op jit(solution)/shard_map/ppermute | solution.py:99
  110.7 3.3 %collective-permute-start.29 = (bf16[4,32,2048]{2,1,0:T(8,128)(2,1)S(1)}, bf16[4,32,2048]{2,1,0:T(8,128)(2,1)S(1)}, u32[]{:S(2)}, u32[]{:S(2)}) collective-permute-start(bf16[4,32,2048]{2,1,0:T(8,128)(2,1)S(1)} %get-tuple-element.80), channel_id=1, source_target_pairs={{0,24},{8,0},{16,8},{24,16},{32,56},{40,32},{48,40},{56,48},{64,88... | collective-permute-start | bytes 1572872 | tf_op jit(solution)/shard_map/ppermute | solution.py:99
  114.0 1.7 collective-permute-start.7
  115.7 2.8 %collective-permute-done.26.r_6_ = bf16[4,32,2048]{2,1,0:T(8,128)(2,1)S(1)} collective-permute-done((bf16[4,32,2048]{2,1,0:T(8,128)(2,1)S(1)}, bf16[4,32,2048]{2,1,0:T(8,128)(2,1)S(1)}, u32[]{:S(2)}, u32[]{:S(2)}) %collective-permute-start.26) | collective-permute-done | bytes 524320 | tf_op jit(solution)/shard_map/ppermute | solution.py:99
  118.4 2.7 %collective-permute-start.8 = (bf16[4,32,512]{2,1,0:T(8,128)(2,1)S(1)}, bf16[4,32,512]{2,1,0:T(8,128)(2,1)S(1)}, u32[]{:S(2)}, u32[]{:S(2)}) collective-permute-start(bf16[4,32,512]{2,1,0:T(8,128)(2,1)S(1)} %get-tuple-element.57), channel_id=1, source_target_pairs={{0,96},{8,104},{16,112},{24,120},{32,0},{40,8},{48,16},{56,24},{64... | collective-permute-start | bytes 393224 | tf_op jit(solution)/shard_map/ppermute | solution.py:99
  121.1 11.9 %collective-permute-done.27.r_11_ = bf16[4,32,2048]{2,1,0:T(8,128)(2,1)S(1)} collective-permute-done((bf16[4,32,2048]{2,1,0:T(8,128)(2,1)S(1)}, bf16[4,32,2048]{2,1,0:T(8,128)(2,1)S(1)}, u32[]{:S(2)}, u32[]{:S(2)}) %collective-permute-start.27) | collective-permute-done | bytes 524320 | tf_op jit(solution)/shard_map/ppermute | solution.py:99
  133.0 1.0 collective-permute-start.10
  134.1 2.5 %collective-permute-start.11 = (bf16[4,32,512]{2,1,0:T(8,128)(2,1)S(1)}, bf16[4,32,512]{2,1,0:T(8,128)(2,1)S(1)}, u32[]{:S(2)}, u32[]{:S(2)}) collective-permute-start(bf16[4,32,512]{2,1,0:T(8,128)(2,1)S(1)} %get-tuple-element.60), channel_id=1, source_target_pairs={{0,24},{8,0},{16,8},{24,16},{32,56},{40,32},{48,40},{56,48},{64,88... | collective-permute-start | bytes 393224 | tf_op jit(solution)/shard_map/ppermute | solution.py:99
  136.5 2.1 %gram.3 = (bf16[16,32,2048]{2,1,0:T(8,128)(2,1)S(1)}, bf16[16,32,2048]{2,1,0:T(8,128)(2,1)S(1)}, f32[3,256,256]{2,1,0:T(8,128)S(1)}) custom-call(bf16[4,32,2048]{2,1,0:T(8,128)(2,1)S(1)} %get-tuple-element.67.r_0_, bf16[4,32,2048]{2,1,0:T(8,128)(2,1)S(1)} %collective-permute-done.18.r_1_, bf16[4,32,2048]{2,1,0:T(8,128)(2,1)S(1)} %collective-permute-done.19.r_2_, ...), custom_call_target="tpu_custom_call" | custom-call | flops 1610612736 | bytes 8388608 | tf_op jit(solution)/shard_map/gram/pallas_call | solution.py:180
  138.6 1.6 gram.4
  140.3 0.4 collective-permute-done.9.r_11_
  140.6 0.9 collective-permute-done.11.r_13_
  141.5 1.1 gram.5
  142.6 20.6 %all_to_all.15 = f32[128,2,128]{2,1,0:T(2,128)S(1)} all-to-all(f32[128,2,128]{2,1,0:T(2,128)S(1)} %bitcast.10), channel_id=1, replica_groups=mesh['gx'=16,'yz'=8] {'gx','yz'}, dimensions={0} | all-to-all | bytes 262144 | tf_op jit(solution)/shard_map/all_to_all | solution.py:368
  163.3 14.2 %all_to_all.16 = f32[128,2,128]{2,1,0:T(2,128)S(1)} all-to-all(f32[128,2,128]{2,1,0:T(2,128)S(1)} %bitcast.8), channel_id=1, replica_groups=mesh['gx'=16,'yz'=8] {'gx','yz'}, dimensions={0} | all-to-all | bytes 262144 | tf_op jit(solution)/shard_map/all_to_all | solution.py:370
  177.5 6.6 %core.1 = (f32[64,512]{1,0:T(8,128)}, bf16[16,4,4,2048]{3,2,1,0:T(4,128)(2,1)S(1)}) custom-call(f32[256,128]{1,0:T(8,128)S(1)} %bitcast.6, bf16[16,32,2048]{2,1,0:T(8,128)(2,1)S(1)} %get-tuple-element.84.refs_0_, bf16[16,32,2048]{2,1,0:T(8,128)(2,1)S(1)} %get-tuple-element.85.refs_1_, bf16[16,32,1536]{2,1,0:T(8,128)(2,1)S(1)} %get-tuple-element.86.refs_2_, ...), custom_call_target="tpu_custom_call" | custom-call | tf_op jit(solution)/shard_map/core/pallas_call | solution.py:305
  184.1 20.1 %all_to_all.17.x_ref = bf16[16,4,4,2048]{3,2,1,0:T(4,128)(2,1)S(1)} all-to-all(bf16[16,4,4,2048]{3,2,1,0:T(4,128)(2,1)S(1)} %get-tuple-element.91), channel_id=1, replica_groups=mesh['gx'=16,'yz'=8] {'gx'}, dimensions={0} | all-to-all | bytes 2097152 | tf_op jit(solution)/shard_map/all_to_all | solution.py:372
  204.2 1.1 merge.1
  (28 shorter events, 0.5 us)
Async XLA Ops:
  3.4 16.1 %collective-permute-start.18 = (bf16[4,32,2048]{2,1,0:T(8,128)(2,1)S(1)}, bf16[4,32,2048]{2,1,0:T(8,128)(2,1)S(1)}, u32[]{:S(2)}, u32[]{:S(2)}) collective-permute-start(bf16[4,32,2048]{2,1,0:T(8,128)(2,1)S(1)} %get-tuple-element.68), channel_id=1, source_target_pairs={{0,8},{8,16},{16,24},{24,0},{32,40},{40,48},{48,56},{56,32},{64,72... | collective-permute-start | bytes 1572872 | tf_op jit(solution)/shard_map/ppermute | solution.py:99
  8.4 21.1 %collective-permute-start = (bf16[4,32,2048]{2,1,0:T(8,128)(2,1)S(1)}, bf16[4,32,2048]{2,1,0:T(8,128)(2,1)S(1)}, u32[]{:S(2)}, u32[]{:S(2)}) collective-permute-start(bf16[4,32,2048]{2,1,0:T(8,128)(2,1)S(1)} %get-tuple-element.48), channel_id=1, source_target_pairs={{0,8},{8,16},{16,24},{24,0},{32,40},{40,48},{48,56},{56,32},{64,72... | collective-permute-start | bytes 1572872 | tf_op jit(solution)/shard_map/ppermute | solution.py:99
  9.9 32.0 %collective-permute-start.1 = (bf16[4,32,2048]{2,1,0:T(8,128)(2,1)S(1)}, bf16[4,32,2048]{2,1,0:T(8,128)(2,1)S(1)}, u32[]{:S(2)}, u32[]{:S(2)}) collective-permute-start(bf16[4,32,2048]{2,1,0:T(8,128)(2,1)S(1)} %get-tuple-element.49), channel_id=1, source_target_pairs={{0,16},{8,24},{16,0},{24,8},{32,48},{40,56},{48,32},{56,40},{64,80... | collective-permute-start | bytes 1572872 | tf_op jit(solution)/shard_map/ppermute | solution.py:99
  11.5 31.2 %collective-permute-start.2 = (bf16[4,32,2048]{2,1,0:T(8,128)(2,1)S(1)}, bf16[4,32,2048]{2,1,0:T(8,128)(2,1)S(1)}, u32[]{:S(2)}, u32[]{:S(2)}) collective-permute-start(bf16[4,32,2048]{2,1,0:T(8,128)(2,1)S(1)} %get-tuple-element.50), channel_id=1, source_target_pairs={{0,24},{8,0},{16,8},{24,16},{32,56},{40,32},{48,40},{56,48},{64,88... | collective-permute-start | bytes 1572872 | tf_op jit(solution)/shard_map/ppermute | solution.py:99
  13.8 28.9 %collective-permute-start.3 = (bf16[4,32,2048]{2,1,0:T(8,128)(2,1)S(1)}, bf16[4,32,2048]{2,1,0:T(8,128)(2,1)S(1)}, u32[]{:S(2)}, u32[]{:S(2)}) collective-permute-start(bf16[4,32,2048]{2,1,0:T(8,128)(2,1)S(1)} %get-tuple-element.52), channel_id=1, source_target_pairs={{0,32},{8,40},{16,48},{24,56},{32,64},{40,72},{48,80},{56,88},{64,... | collective-permute-start | bytes 1572872 | tf_op jit(solution)/shard_map/ppermute | solution.py:99
  19.5 24.9 %collective-permute-start.4 = (bf16[4,32,2048]{2,1,0:T(8,128)(2,1)S(1)}, bf16[4,32,2048]{2,1,0:T(8,128)(2,1)S(1)}, u32[]{:S(2)}, u32[]{:S(2)}) collective-permute-start(bf16[4,32,2048]{2,1,0:T(8,128)(2,1)S(1)} %get-tuple-element.53), channel_id=1, source_target_pairs={{0,64},{8,72},{16,80},{24,88},{32,96},{40,104},{48,112},{56,120},{... | collective-permute-start | bytes 1572872 | tf_op jit(solution)/shard_map/ppermute | solution.py:99
  29.5 17.8 %collective-permute-start.5 = (bf16[4,32,2048]{2,1,0:T(8,128)(2,1)}, bf16[4,32,2048]{2,1,0:T(8,128)(2,1)S(1)}, u32[]{:S(2)}, u32[]{:S(2)}) collective-permute-start(bf16[4,32,2048]{2,1,0:T(8,128)(2,1)} %get-tuple-element.54), channel_id=1, source_target_pairs={{0,96},{8,104},{16,112},{24,120},{32,0},{40,8},{48,16},{56,24},{64... | collective-permute-start | bytes 1572872 | tf_op jit(solution)/shard_map/ppermute | solution.py:99
  41.9 14.3 %collective-permute-start.19 = (bf16[4,32,2048]{2,1,0:T(8,128)(2,1)S(1)}, bf16[4,32,2048]{2,1,0:T(8,128)(2,1)S(1)}, u32[]{:S(2)}, u32[]{:S(2)}) collective-permute-start(bf16[4,32,2048]{2,1,0:T(8,128)(2,1)S(1)} %get-tuple-element.69), channel_id=1, source_target_pairs={{0,16},{8,24},{16,0},{24,8},{32,48},{40,56},{48,32},{56,40},{64,80... | collective-permute-start | bytes 1572872 | tf_op jit(solution)/shard_map/ppermute | solution.py:99
  42.7 15.1 %collective-permute-start.20 = (bf16[4,32,2048]{2,1,0:T(8,128)(2,1)S(1)}, bf16[4,32,2048]{2,1,0:T(8,128)(2,1)S(1)}, u32[]{:S(2)}, u32[]{:S(2)}) collective-permute-start(bf16[4,32,2048]{2,1,0:T(8,128)(2,1)S(1)} %get-tuple-element.70), channel_id=1, source_target_pairs={{0,24},{8,0},{16,8},{24,16},{32,56},{40,32},{48,40},{56,48},{64,88... | collective-permute-start | bytes 1572872 | tf_op jit(solution)/shard_map/ppermute | solution.py:99
  42.7 18.0 %collective-permute-start.21 = (bf16[4,32,2048]{2,1,0:T(8,128)(2,1)S(1)}, bf16[4,32,2048]{2,1,0:T(8,128)(2,1)S(1)}, u32[]{:S(2)}, u32[]{:S(2)}) collective-permute-start(bf16[4,32,2048]{2,1,0:T(8,128)(2,1)S(1)} %get-tuple-element.72), channel_id=1, source_target_pairs={{0,32},{8,40},{16,48},{24,56},{32,64},{40,72},{48,80},{56,88},{64,... | collective-permute-start | bytes 1572872 | tf_op jit(solution)/shard_map/ppermute | solution.py:99
  44.4 26.9 %collective-permute-start.22 = (bf16[4,32,2048]{2,1,0:T(8,128)(2,1)S(1)}, bf16[4,32,2048]{2,1,0:T(8,128)(2,1)S(1)}, u32[]{:S(2)}, u32[]{:S(2)}) collective-permute-start(bf16[4,32,2048]{2,1,0:T(8,128)(2,1)S(1)} %get-tuple-element.73), channel_id=1, source_target_pairs={{0,64},{8,72},{16,80},{24,88},{32,96},{40,104},{48,112},{56,120},{... | collective-permute-start | bytes 1572872 | tf_op jit(solution)/shard_map/ppermute | solution.py:99
  47.3 24.0 %collective-permute-start.23 = (bf16[4,32,2048]{2,1,0:T(8,128)(2,1)S(1)}, bf16[4,32,2048]{2,1,0:T(8,128)(2,1)S(1)}, u32[]{:S(2)}, u32[]{:S(2)}) collective-permute-start(bf16[4,32,2048]{2,1,0:T(8,128)(2,1)S(1)} %get-tuple-element.74), channel_id=1, source_target_pairs={{0,96},{8,104},{16,112},{24,120},{32,0},{40,8},{48,16},{56,24},{64... | collective-permute-start | bytes 1572872 | tf_op jit(solution)/shard_map/ppermute | solution.py:99
  56.2 35.5 %collective-permute-start.12 = (bf16[4,32,1536]{2,1,0:T(8,128)(2,1)S(1)}, bf16[4,32,1536]{2,1,0:T(8,128)(2,1)S(1)}, u32[]{:S(2)}, u32[]{:S(2)}) collective-permute-start(bf16[4,32,1536]{2,1,0:T(8,128)(2,1)S(1)} %get-tuple-element.61), channel_id=1, source_target_pairs={{0,32},{8,40},{16,48},{24,56},{32,64},{40,72},{48,80},{56,88},{64,... | collective-permute-start | bytes 1179656 | tf_op jit(solution)/shard_map/ppermute | solution.py:99
  57.8 36.6 %collective-permute-start.13 = (bf16[4,32,1536]{2,1,0:T(8,128)(2,1)S(1)}, bf16[4,32,1536]{2,1,0:T(8,128)(2,1)S(1)}, u32[]{:S(2)}, u32[]{:S(2)}) collective-permute-start(bf16[4,32,1536]{2,1,0:T(8,128)(2,1)S(1)} %get-tuple-element.62), channel_id=1, source_target_pairs={{0,64},{8,72},{16,80},{24,88},{32,96},{40,104},{48,112},{56,120},{... | collective-permute-start | bytes 1179656 | tf_op jit(solution)/shard_map/ppermute | solution.py:99
  60.7 28.1 %collective-permute-start.6 = (bf16[4,32,512]{2,1,0:T(8,128)(2,1)S(1)}, bf16[4,32,512]{2,1,0:T(8,128)(2,1)S(1)}, u32[]{:S(2)}, u32[]{:S(2)}) collective-permute-start(bf16[4,32,512]{2,1,0:T(8,128)(2,1)S(1)} %get-tuple-element.55), channel_id=1, source_target_pairs={{0,32},{8,40},{16,48},{24,56},{32,64},{40,72},{48,80},{56,88},{64,... | collective-permute-start | bytes 393224 | tf_op jit(solution)/shard_map/ppermute | solution.py:99
  71.5 39.2 %collective-permute-start.24 = (bf16[4,32,2048]{2,1,0:T(8,128)(2,1)S(1)}, bf16[4,32,2048]{2,1,0:T(8,128)(2,1)S(1)}, u32[]{:S(2)}, u32[]{:S(2)}) collective-permute-start(bf16[4,32,2048]{2,1,0:T(8,128)(2,1)S(1)} %get-tuple-element.75), channel_id=1, source_target_pairs={{0,32},{8,40},{16,48},{24,56},{32,64},{40,72},{48,80},{56,88},{64,... | collective-permute-start | bytes 1572872 | tf_op jit(solution)/shard_map/ppermute | solution.py:99
  72.3 22.1 %collective-permute-start.14 = (bf16[4,32,1536]{2,1,0:T(8,128)(2,1)S(1)}, bf16[4,32,1536]{2,1,0:T(8,128)(2,1)S(1)}, u32[]{:S(2)}, u32[]{:S(2)}) collective-permute-start(bf16[4,32,1536]{2,1,0:T(8,128)(2,1)S(1)} %get-tuple-element.63), channel_id=1, source_target_pairs={{0,96},{8,104},{16,112},{24,120},{32,0},{40,8},{48,16},{56,24},{64... | collective-permute-start | bytes 1179656 | tf_op jit(solution)/shard_map/ppermute | solution.py:99
  88.8 13.0 %collective-permute-start.15 = (bf16[4,32,1536]{2,1,0:T(8,128)(2,1)S(1)}, bf16[4,32,1536]{2,1,0:T(8,128)(2,1)S(1)}, u32[]{:S(2)}, u32[]{:S(2)}) collective-permute-start(bf16[4,32,1536]{2,1,0:T(8,128)(2,1)S(1)} %get-tuple-element.64), channel_id=1, source_target_pairs={{0,8},{8,16},{16,24},{24,0},{32,40},{40,48},{48,56},{56,32},{64,72... | collective-permute-start | bytes 1179656 | tf_op jit(solution)/shard_map/ppermute | solution.py:99
  91.7 19.0 %collective-permute-start.16 = (bf16[4,32,1536]{2,1,0:T(8,128)(2,1)S(1)}, bf16[4,32,1536]{2,1,0:T(8,128)(2,1)S(1)}, u32[]{:S(2)}, u32[]{:S(2)}) collective-permute-start(bf16[4,32,1536]{2,1,0:T(8,128)(2,1)S(1)} %get-tuple-element.65), channel_id=1, source_target_pairs={{0,16},{8,24},{16,0},{24,8},{32,48},{40,56},{48,32},{56,40},{64,80... | collective-permute-start | bytes 1179656 | tf_op jit(solution)/shard_map/ppermute | solution.py:99
  94.4 16.3 %collective-permute-start.17 = (bf16[4,32,1536]{2,1,0:T(8,128)(2,1)S(1)}, bf16[4,32,1536]{2,1,0:T(8,128)(2,1)S(1)}, u32[]{:S(2)}, u32[]{:S(2)}) collective-permute-start(bf16[4,32,1536]{2,1,0:T(8,128)(2,1)S(1)} %get-tuple-element.66), channel_id=1, source_target_pairs={{0,24},{8,0},{16,8},{24,16},{32,56},{40,32},{48,40},{56,48},{64,88... | collective-permute-start | bytes 1179656 | tf_op jit(solution)/shard_map/ppermute | solution.py:99
  94.4 19.6 %collective-permute-start.25 = (bf16[4,32,2048]{2,1,0:T(8,128)(2,1)S(1)}, bf16[4,32,2048]{2,1,0:T(8,128)(2,1)S(1)}, u32[]{:S(2)}, u32[]{:S(2)}) collective-permute-start(bf16[4,32,2048]{2,1,0:T(8,128)(2,1)S(1)} %get-tuple-element.76), channel_id=1, source_target_pairs={{0,64},{8,72},{16,80},{24,88},{32,96},{40,104},{48,112},{56,120},{... | collective-permute-start | bytes 1572872 | tf_op jit(solution)/shard_map/ppermute | solution.py:99
  101.7 16.7 %collective-permute-start.26 = (bf16[4,32,2048]{2,1,0:T(8,128)(2,1)S(1)}, bf16[4,32,2048]{2,1,0:T(8,128)(2,1)S(1)}, u32[]{:S(2)}, u32[]{:S(2)}) collective-permute-start(bf16[4,32,2048]{2,1,0:T(8,128)(2,1)S(1)} %get-tuple-element.77), channel_id=1, source_target_pairs={{0,96},{8,104},{16,112},{24,120},{32,0},{40,8},{48,16},{56,24},{64... | collective-permute-start | bytes 1572872 | tf_op jit(solution)/shard_map/ppermute | solution.py:99
  110.7 22.4 %collective-permute-start.27 = (bf16[4,32,2048]{2,1,0:T(8,128)(2,1)S(1)}, bf16[4,32,2048]{2,1,0:T(8,128)(2,1)S(1)}, u32[]{:S(2)}, u32[]{:S(2)}) collective-permute-start(bf16[4,32,2048]{2,1,0:T(8,128)(2,1)S(1)} %get-tuple-element.78), channel_id=1, source_target_pairs={{0,8},{8,16},{16,24},{24,0},{32,40},{40,48},{48,56},{56,32},{64,72... | collective-permute-start | bytes 1572872 | tf_op jit(solution)/shard_map/ppermute | solution.py:99
  110.7 22.4 %collective-permute-start.28 = (bf16[4,32,2048]{2,1,0:T(8,128)(2,1)S(1)}, bf16[4,32,2048]{2,1,0:T(8,128)(2,1)S(1)}, u32[]{:S(2)}, u32[]{:S(2)}) collective-permute-start(bf16[4,32,2048]{2,1,0:T(8,128)(2,1)S(1)} %get-tuple-element.79), channel_id=1, source_target_pairs={{0,16},{8,24},{16,0},{24,8},{32,48},{40,56},{48,32},{56,40},{64,80... | collective-permute-start | bytes 1572872 | tf_op jit(solution)/shard_map/ppermute | solution.py:99
  110.7 23.3 %collective-permute-start.29 = (bf16[4,32,2048]{2,1,0:T(8,128)(2,1)S(1)}, bf16[4,32,2048]{2,1,0:T(8,128)(2,1)S(1)}, u32[]{:S(2)}, u32[]{:S(2)}) collective-permute-start(bf16[4,32,2048]{2,1,0:T(8,128)(2,1)S(1)} %get-tuple-element.80), channel_id=1, source_target_pairs={{0,24},{8,0},{16,8},{24,16},{32,56},{40,32},{48,40},{56,48},{64,88... | collective-permute-start | bytes 1572872 | tf_op jit(solution)/shard_map/ppermute | solution.py:99
  114.0 26.2 %collective-permute-start.7 = (bf16[4,32,512]{2,1,0:T(8,128)(2,1)S(1)}, bf16[4,32,512]{2,1,0:T(8,128)(2,1)S(1)}, u32[]{:S(2)}, u32[]{:S(2)}) collective-permute-start(bf16[4,32,512]{2,1,0:T(8,128)(2,1)S(1)} %get-tuple-element.56), channel_id=1, source_target_pairs={{0,64},{8,72},{16,80},{24,88},{32,96},{40,104},{48,112},{56,120},{... | collective-permute-start | bytes 393224 | tf_op jit(solution)/shard_map/ppermute | solution.py:99
  118.4 21.8 %collective-permute-start.8 = (bf16[4,32,512]{2,1,0:T(8,128)(2,1)S(1)}, bf16[4,32,512]{2,1,0:T(8,128)(2,1)S(1)}, u32[]{:S(2)}, u32[]{:S(2)}) collective-permute-start(bf16[4,32,512]{2,1,0:T(8,128)(2,1)S(1)} %get-tuple-element.57), channel_id=1, source_target_pairs={{0,96},{8,104},{16,112},{24,120},{32,0},{40,8},{48,16},{56,24},{64... | collective-permute-start | bytes 393224 | tf_op jit(solution)/shard_map/ppermute | solution.py:99
  133.0 7.6 %collective-permute-start.9 = (bf16[4,32,512]{2,1,0:T(8,128)(2,1)S(1)}, bf16[4,32,512]{2,1,0:T(8,128)(2,1)S(1)}, u32[]{:S(2)}, u32[]{:S(2)}) collective-permute-start(bf16[4,32,512]{2,1,0:T(8,128)(2,1)S(1)} %get-tuple-element.58), channel_id=1, source_target_pairs={{0,8},{8,16},{16,24},{24,0},{32,40},{40,48},{48,56},{56,32},{64,72... | collective-permute-start | bytes 393224 | tf_op jit(solution)/shard_map/ppermute | solution.py:99
  133.0 7.6 %collective-permute-start.10 = (bf16[4,32,512]{2,1,0:T(8,128)(2,1)S(1)}, bf16[4,32,512]{2,1,0:T(8,128)(2,1)S(1)}, u32[]{:S(2)}, u32[]{:S(2)}) collective-permute-start(bf16[4,32,512]{2,1,0:T(8,128)(2,1)S(1)} %get-tuple-element.59), channel_id=1, source_target_pairs={{0,16},{8,24},{16,0},{24,8},{32,48},{40,56},{48,32},{56,40},{64,80... | collective-permute-start | bytes 393224 | tf_op jit(solution)/shard_map/ppermute | solution.py:99
  134.1 7.5 %collective-permute-start.11 = (bf16[4,32,512]{2,1,0:T(8,128)(2,1)S(1)}, bf16[4,32,512]{2,1,0:T(8,128)(2,1)S(1)}, u32[]{:S(2)}, u32[]{:S(2)}) collective-permute-start(bf16[4,32,512]{2,1,0:T(8,128)(2,1)S(1)} %get-tuple-element.60), channel_id=1, source_target_pairs={{0,24},{8,0},{16,8},{24,16},{32,56},{40,32},{48,40},{56,48},{64,88... | collective-permute-start | bytes 393224 | tf_op jit(solution)/shard_map/ppermute | solution.py:99
  138.6 2.9 %copy-start = (f32[512,64]{0,1:T(8,128)S(1)}, f32[512,64]{0,1:T(8,128)}, u32[]{:S(2)}) copy-start(f32[512,64]{0,1:T(8,128)} %param.3) | copy-start | bytes 393220
